TPU v7x, 32 devices: a whole 2x2x4 slice. The times are simulated.
32 devices in a mesh: row: 8 (over z, x), col: 4 (over y, core).
Axes of the slice: x: 2, y: 2, z: 4, core: 2. Of those that a mesh axis runs over, the one named last changes fastest.
Arguments:
- layer_in: bfloat16 [8192, 768], P('row', 'col'), may hold values from -6 to 6
- cotangent: bfloat16 [8192, 768], P('row', 'col'), may hold values from -6 to 6
- token_ids: int32 [8192], P('row'), may hold values from 0 to 50303, as said below
- hash_table: int32 [50304], replicated, may hold values from 0 to 15, as said below
- prefix_len: int32 [1], replicated, may hold values from 819 to 4096
- w_query: bfloat16 [768, 768], P('row', 'col'), may hold values from -0.21875 to 0.21875
- w_key: bfloat16 [768, 768], P('row', 'col'), may hold values from -0.21875 to 0.21875
- w_value: bfloat16 [768, 768], P('row', 'col'), may hold values from -0.21875 to 0.21875
- w_output: bfloat16 [768, 768], P('row', 'col'), may hold values from -6 to 6
- bias_query: bfloat16 [64, 12], P('row', 'col'), may hold values from -0.59765625 to 0.59765625
- bias_value: bfloat16 [64, 12], P('row', 'col'), may hold values from -0.119628906 to 0.119628906
- gain_attn: bfloat16 [768], P('row'), may hold values from 0.5 to 1.5
- shift_attn: bfloat16 [768], P('row'), may hold values from -0.59765625 to 0.59765625
- gain_moe: bfloat16 [768], P('row'), may hold values from 0.5 to 1.5
- shift_moe: bfloat16 [768], P('row'), may hold values from -0.59765625 to 0.59765625
- bias_output: bfloat16 [768], P('row'), may hold values from -1.1953125 to 1.1953125
- w_up: bfloat16 [16, 768, 3072], P('row', None, 'col'), may hold values from -0.21875 to 0.21875
- bias_up: bfloat16 [16, 3072], P('row', 'col'), may hold values from -0.59765625 to 0.59765625
- w_down: bfloat16 [16, 3072, 768], P('row', 'col'), may hold values from -0.109375 to 0.109375
- bias_down: bfloat16 [16, 768], P('row'), may hold values from -0.59765625 to 0.59765625
Outputs:
- layer_out: bfloat16 [8192, 768], P('row', 'col')
- grad_in: float32 [8192, 768], P('row', 'col')
- grad_w_query: float32 [768, 768], P('row', 'col')
- grad_w_key: float32 [768, 768], P('row', 'col')
- grad_w_value: float32 [768, 768], P('row', 'col')
- grad_w_output: float32 [768, 768], P('row', 'col')
- grad_bias_query: float32 [64, 12], P('row', 'col')
- grad_bias_value: float32 [64, 12], P('row', 'col')
- grad_gain_attn: float32 [768], P('row')
- grad_shift_attn: float32 [768], P('row')
- grad_gain_moe: float32 [768], P('row')
- grad_shift_moe: float32 [768], P('row')
- grad_bias_output: float32 [768], P('row')
- grad_w_up: float32 [16, 768, 3072], P('row', None, 'col')
- grad_bias_up: float32 [16, 3072], P('row', 'col')
- grad_w_down: float32 [16, 3072, 768], P('row', 'col')
- grad_bias_down: float32 [16, 768], P('row')
Inputs may be any that keep to these rules, and one draw needn't show every extreme that they name: `hash_table`: each expert is named by the same number of vocabulary ids. `token_ids`: in each aligned block of 1024 tokens (the tokens of one index of row) no expert receives more than 128 tokens, and one expert, the same in every block, receives exactly 128.
All inputs are finite; a program needn't handle non-finite values.
Results may differ from a plain program's by a relative error of at most 0.024.
Values may be sent and summed in bfloat16 or wider, within the bound.
A program may use at most 256 MiB of HBM per device.

v0:
```python
import math

import jax
import jax.numpy as jnp
from jax import lax
from jax.sharding import PartitionSpec as P

D = 768
HD = 64
EXP_DEV = 2
LENGTH = 8192


epsilon = 1e-05
neg_big = -1e30


def norm_stats(rows):
    centred = rows - jnp.mean(rows, axis=-1, keepdims=True)
    spread = jnp.mean(centred * centred, axis=-1, keepdims=True)
    rstd = lax.rsqrt(spread + epsilon)
    return (centred * rstd, rstd)


def norm_back(incoming, normed, rstd, gain):
    scaled = incoming * gain
    first = jnp.mean(scaled, axis=-1, keepdims=True)
    second = jnp.mean(scaled * normed, axis=-1, keepdims=True)
    return rstd * (scaled - first - normed * second)


def dot_last(left, right):
    return lax.dot_general(
        left, right, (((1,), (1,)), ((), ())), preferred_element_type=jnp.float32
    )


def dot_first(left, right):
    return lax.dot_general(
        left, right, (((0,), (0,)), ((), ())), preferred_element_type=jnp.float32
    )


def exact_gelu(inputs):
    return jax.nn.gelu(inputs, approximate=False)


def per_device(
    layer_in,
    cotangent,
    token_ids,
    hash_table,
    prefix_len,
    w_query,
    w_key,
    w_value,
    w_output,
    bias_query,
    bias_value,
    gain_attn,
    shift_attn,
    gain_moe,
    shift_moe,
    bias_output,
    w_up,
    bias_up,
    w_down,
    bias_down,
):
    row_count = lax.axis_size("row")
    row_index = lax.axis_index("row")
    col_index = lax.axis_index("col")
    tok_rows = layer_in.shape[0]
    local_cols = layer_in.shape[1]
    local_heads = local_cols // HD
    all_rows = tok_rows * row_count
    seq_len = min(LENGTH, all_rows)
    qk_scale = HD ** (-0.5)
    full_in, full_grad = (
        lax.all_gather(layer_in, "col", axis=1, tiled=True),
        lax.all_gather(cotangent, "col", axis=1, tiled=True),
    )
    (
        full_wq,
        full_wk,
        full_wv,
        full_wo,
        full_bq,
        full_bv,
        gain_one,
        shift_one,
        gain_two,
        shift_two,
        out_bias,
    ) = (
        lax.all_gather(w_query, "row", axis=0, tiled=True),
        lax.all_gather(w_key, "row", axis=0, tiled=True),
        lax.all_gather(w_value, "row", axis=0, tiled=True),
        lax.all_gather(w_output, "row", axis=0, tiled=True),
        lax.all_gather(bias_query, "row", axis=0, tiled=True),
        lax.all_gather(bias_value, "row", axis=0, tiled=True),
        lax.all_gather(gain_attn, "row", axis=0, tiled=True),
        lax.all_gather(shift_attn, "row", axis=0, tiled=True),
        lax.all_gather(gain_moe, "row", axis=0, tiled=True),
        lax.all_gather(shift_moe, "row", axis=0, tiled=True),
        lax.all_gather(bias_output, "row", axis=0, tiled=True),
    )
    gain_one = gain_one.astype(jnp.float32)
    gain_two = gain_two.astype(jnp.float32)
    resid = full_in.astype(jnp.float32)
    normed_one, rstd_one = norm_stats(resid)
    h_one = (normed_one * gain_one + shift_one.astype(jnp.float32)).astype(jnp.bfloat16)
    query_bias = full_bq.astype(jnp.float32).T.reshape(local_cols)
    value_bias = full_bv.astype(jnp.float32).T.reshape(local_cols)
    queries = (jnp.dot(h_one, full_wq, preferred_element_type=jnp.float32) + query_bias).astype(
        jnp.bfloat16
    )
    keys = jnp.dot(h_one, full_wk, preferred_element_type=jnp.float32).astype(jnp.bfloat16)
    values = (jnp.dot(h_one, full_wv, preferred_element_type=jnp.float32) + value_bias).astype(
        jnp.bfloat16
    )
    key_all, value_all = (
        lax.all_gather(keys, "row", axis=0, tiled=True),
        lax.all_gather(values, "row", axis=0, tiled=True),
    )
    first_pos = row_index * tok_rows
    query_pos = first_pos + jnp.arange(tok_rows, dtype=jnp.int32)
    device_seq = first_pos // seq_len
    seq_start = device_seq * seq_len
    seq_hit = device_seq == jnp.arange(prefix_len.shape[0], dtype=jnp.int32)
    device_prefix = jnp.sum(jnp.where(seq_hit, prefix_len, 0))
    local_start = first_pos - seq_start
    key_block = math.gcd(seq_len, 1024)
    need_end = jnp.maximum(device_prefix, local_start + tok_rows)
    live_blocks = (need_end + key_block - 1) // key_block
    query_heads = queries.reshape(tok_rows, local_heads, HD)

    def block_scores(key_blk, start):
        key_pos = start + jnp.arange(key_block, dtype=jnp.int32)
        seen = (key_pos[None, :] - seq_start < device_prefix) | (
            key_pos[None, :] <= query_pos[:, None]
        )
        raw = (
            jnp.einsum("qhd,khd->hqk", query_heads, key_blk, preferred_element_type=jnp.float32)
            * qk_scale
        )
        return (raw, seen[None])

    def stats_step(index, carry):
        peak, total = carry
        start = seq_start + index * key_block
        key_blk = lax.dynamic_slice_in_dim(key_all, start, key_block, 0).reshape(
            key_block, local_heads, HD
        )
        raw, allowed = block_scores(key_blk, start)
        scores = jnp.where(allowed, raw, neg_big)
        new_peak = jnp.maximum(peak, jnp.max(scores, axis=-1))
        weights = jnp.where(allowed, jnp.exp(scores - new_peak[..., None]), 0.0)
        total = total * jnp.exp(peak - new_peak) + jnp.sum(weights, axis=-1)
        return (new_peak, total)

    peak, total = lax.fori_loop(
        0,
        live_blocks,
        stats_step,
        (
            jnp.full((local_heads, tok_rows), neg_big, jnp.float32),
            jnp.zeros((local_heads, tok_rows), jnp.float32),
        ),
    )
    log_total = peak + jnp.log(total)

    def value_step(index, summed):
        start = seq_start + index * key_block
        key_blk = lax.dynamic_slice_in_dim(key_all, start, key_block, 0).reshape(
            key_block, local_heads, HD
        )
        value_blk = lax.dynamic_slice_in_dim(value_all, start, key_block, 0).reshape(
            key_block, local_heads, HD
        )
        raw, allowed = block_scores(key_blk, start)
        probs = jnp.where(allowed, jnp.exp(raw - log_total[..., None]), 0.0)
        return summed + jnp.einsum(
            "hqk,khd->hqd",
            probs.astype(jnp.bfloat16),
            value_blk,
            preferred_element_type=jnp.float32,
        )

    attended = lax.fori_loop(
        0, live_blocks, value_step, jnp.zeros((local_heads, tok_rows, HD), jnp.float32)
    )
    attended_rows = jnp.transpose(attended, (1, 0, 2)).reshape(tok_rows, local_cols)
    attended_low = attended_rows.astype(jnp.bfloat16)
    partial_out = dot_last(attended_low, full_wo)
    branch = lax.psum(partial_out.astype(jnp.bfloat16), "col").astype(jnp.float32)
    mid = resid + branch + out_bias.astype(jnp.float32)
    normed_two, rstd_two = norm_stats(mid)
    h_two = (normed_two * gain_two + shift_two.astype(jnp.float32)).astype(jnp.bfloat16)
    expert_total = EXP_DEV * row_count
    capacity = max(2, 2 * tok_rows // expert_total)
    expert_of = hash_table[token_ids]
    hits = (expert_of[:, None] == jnp.arange(expert_total, dtype=jnp.int32)[None, :]).astype(
        jnp.int32
    )
    slot_of = jnp.sum(hits * (jnp.cumsum(hits, axis=0) - 1), axis=1)
    outgoing = (
        jnp.zeros((expert_total, capacity, D), jnp.bfloat16).at[expert_of, slot_of].set(h_two)
    )
    received = lax.all_to_all(outgoing, "row", split_axis=0, concat_axis=1, tiled=True)
    pre_act = jnp.einsum("ecd,edf->ecf", received, w_up, preferred_element_type=jnp.float32)
    pre_act = pre_act + bias_up.astype(jnp.float32)[:, None, :]
    activated, gelu_pull = jax.vjp(exact_gelu, pre_act)
    hidden = activated.astype(jnp.bfloat16)
    expert_part = jnp.einsum("ecf,efd->ecd", hidden, w_down, preferred_element_type=jnp.float32)
    expert_out = (
        lax.psum(expert_part.astype(jnp.bfloat16), "col").astype(jnp.float32)
        + bias_down.astype(jnp.float32)[:, None, :]
    )
    returned = lax.all_to_all(
        expert_out.astype(jnp.bfloat16), "row", split_axis=1, concat_axis=0, tiled=True
    )
    final = mid + returned[expert_of, slot_of].astype(jnp.float32)
    layer_out = lax.dynamic_slice_in_dim(final, col_index * local_cols, local_cols, 1).astype(
        jnp.bfloat16
    )
    grad_rows = full_grad.astype(jnp.float32)
    grad_outgoing = (
        jnp.zeros((expert_total, capacity, D), jnp.bfloat16).at[expert_of, slot_of].set(full_grad)
    )
    grad_received = lax.all_to_all(grad_outgoing, "row", split_axis=0, concat_axis=1, tiled=True)
    grad_bias_down = jnp.sum(grad_received, axis=1, dtype=jnp.float32)
    grad_w_down = jnp.einsum(
        "ecf,ecd->efd", hidden, grad_received, preferred_element_type=jnp.float32
    )
    grad_hidden = jnp.einsum(
        "ecd,efd->ecf", grad_received, w_down, preferred_element_type=jnp.float32
    )
    grad_pre = gelu_pull(grad_hidden)[0].astype(jnp.bfloat16)
    grad_bias_up = jnp.sum(grad_pre, axis=1, dtype=jnp.float32)
    grad_w_up = jnp.einsum("ecd,ecf->edf", received, grad_pre, preferred_element_type=jnp.float32)
    grad_expert_in = jnp.einsum("ecf,edf->ecd", grad_pre, w_up, preferred_element_type=jnp.float32)
    grad_expert_in = lax.psum(grad_expert_in.astype(jnp.bfloat16), "col")
    grad_back = lax.all_to_all(grad_expert_in, "row", split_axis=1, concat_axis=0, tiled=True)
    grad_h_two = grad_back[expert_of, slot_of].astype(jnp.float32)
    grad_mid = grad_rows + norm_back(grad_h_two, normed_two, rstd_two, gain_two)
    grad_gain_two = jnp.sum(grad_h_two * normed_two, axis=0)
    grad_shift_two = jnp.sum(grad_h_two, axis=0)
    grad_out_bias = jnp.sum(grad_mid, axis=0)
    grad_branch = grad_mid.astype(jnp.bfloat16)
    grad_w_output = dot_first(grad_branch, attended_low)
    grad_attended = jnp.dot(grad_branch, full_wo, preferred_element_type=jnp.float32).astype(
        jnp.bfloat16
    )
    grad_heads = grad_attended.reshape(tok_rows, local_heads, HD)
    delta = jnp.einsum("qhd,hqd->hq", grad_heads.astype(jnp.float32), attended)
    key_back, value_back = (
        lax.all_gather(keys, "row", axis=0, tiled=True),
        lax.all_gather(values, "row", axis=0, tiled=True),
    )

    def backward_step(index, carry):
        grad_query, key_buffer, value_buffer = carry
        start = seq_start + index * key_block
        key_blk = lax.dynamic_slice_in_dim(key_back, start, key_block, 0).reshape(
            key_block, local_heads, HD
        )
        value_blk = lax.dynamic_slice_in_dim(value_back, start, key_block, 0).reshape(
            key_block, local_heads, HD
        )
        raw, allowed = block_scores(key_blk, start)
        probs = jnp.where(allowed, jnp.exp(raw - log_total[..., None]), 0.0)
        grad_probs = jnp.einsum(
            "qhd,khd->hqk", grad_heads, value_blk, preferred_element_type=jnp.float32
        )
        grad_raw = (probs * (grad_probs - delta[..., None])).astype(jnp.bfloat16)
        grad_query = grad_query + jnp.einsum(
            "hqk,khd->qhd", grad_raw, key_blk, preferred_element_type=jnp.float32
        )
        grad_key = jnp.einsum(
            "hqk,qhd->khd", grad_raw, query_heads, preferred_element_type=jnp.float32
        )
        grad_value = jnp.einsum(
            "hqk,qhd->khd",
            probs.astype(jnp.bfloat16),
            grad_heads,
            preferred_element_type=jnp.float32,
        )
        key_buffer = lax.dynamic_update_slice_in_dim(
            key_buffer, grad_key.reshape(key_block, local_cols), start, 0
        )
        value_buffer = lax.dynamic_update_slice_in_dim(
            value_buffer, grad_value.reshape(key_block, local_cols), start, 0
        )
        return (grad_query, key_buffer, value_buffer)

    grad_query, key_terms, value_terms = lax.fori_loop(
        0,
        live_blocks,
        backward_step,
        (
            jnp.zeros((tok_rows, local_heads, HD), jnp.float32),
            jnp.zeros((all_rows, local_cols), jnp.float32),
            jnp.zeros((all_rows, local_cols), jnp.float32),
        ),
    )
    key_own, value_own = (
        lax.psum_scatter(
            key_terms.astype(jnp.bfloat16), "row", scatter_dimension=0, tiled=True
        ).astype(jnp.float32),
        lax.psum_scatter(
            value_terms.astype(jnp.bfloat16), "row", scatter_dimension=0, tiled=True
        ).astype(jnp.float32),
    )
    grad_q_rows = (grad_query.reshape(tok_rows, local_cols) * qk_scale).astype(jnp.bfloat16)
    grad_k_rows = (key_own * qk_scale).astype(jnp.bfloat16)
    grad_v_rows = value_own.astype(jnp.bfloat16)
    grad_wq = dot_first(h_one, grad_q_rows)
    grad_wk = dot_first(h_one, grad_k_rows)
    grad_wv = dot_first(h_one, grad_v_rows)
    grad_bq = jnp.sum(grad_q_rows, axis=0, dtype=jnp.float32).reshape(local_heads, HD).T
    grad_bv = jnp.sum(grad_v_rows, axis=0, dtype=jnp.float32).reshape(local_heads, HD).T
    grad_h_one = (
        dot_last(grad_q_rows, full_wq)
        + dot_last(grad_k_rows, full_wk)
        + dot_last(grad_v_rows, full_wv)
    )
    grad_h_one = lax.psum(grad_h_one.astype(jnp.bfloat16), "col").astype(jnp.float32)
    grad_resid = grad_mid + norm_back(grad_h_one, normed_one, rstd_one, gain_one)
    grad_gain_one = jnp.sum(grad_h_one * normed_one, axis=0)
    grad_shift_one = jnp.sum(grad_h_one, axis=0)
    grad_in = lax.dynamic_slice_in_dim(grad_resid, col_index * local_cols, local_cols, 1)
    (
        grad_wq,
        grad_wk,
        grad_wv,
        grad_w_output,
        grad_bq,
        grad_bv,
        grad_gain_one,
        grad_shift_one,
        grad_gain_two,
        grad_shift_two,
        grad_out_bias,
    ) = (
        lax.psum_scatter(
            grad_wq.astype(jnp.bfloat16), "row", scatter_dimension=0, tiled=True
        ).astype(jnp.float32),
        lax.psum_scatter(
            grad_wk.astype(jnp.bfloat16), "row", scatter_dimension=0, tiled=True
        ).astype(jnp.float32),
        lax.psum_scatter(
            grad_wv.astype(jnp.bfloat16), "row", scatter_dimension=0, tiled=True
        ).astype(jnp.float32),
        lax.psum_scatter(
            grad_w_output.astype(jnp.bfloat16), "row", scatter_dimension=0, tiled=True
        ).astype(jnp.float32),
        lax.psum_scatter(
            grad_bq.astype(jnp.bfloat16), "row", scatter_dimension=0, tiled=True
        ).astype(jnp.float32),
        lax.psum_scatter(
            grad_bv.astype(jnp.bfloat16), "row", scatter_dimension=0, tiled=True
        ).astype(jnp.float32),
        lax.psum_scatter(
            grad_gain_one.astype(jnp.bfloat16), "row", scatter_dimension=0, tiled=True
        ).astype(jnp.float32),
        lax.psum_scatter(
            grad_shift_one.astype(jnp.bfloat16), "row", scatter_dimension=0, tiled=True
        ).astype(jnp.float32),
        lax.psum_scatter(
            grad_gain_two.astype(jnp.bfloat16), "row", scatter_dimension=0, tiled=True
        ).astype(jnp.float32),
        lax.psum_scatter(
            grad_shift_two.astype(jnp.bfloat16), "row", scatter_dimension=0, tiled=True
        ).astype(jnp.float32),
        lax.psum_scatter(
            grad_out_bias.astype(jnp.bfloat16), "row", scatter_dimension=0, tiled=True
        ).astype(jnp.float32),
    )
    return (
        layer_out,
        grad_in,
        grad_wq,
        grad_wk,
        grad_wv,
        grad_w_output,
        grad_bq,
        grad_bv,
        grad_gain_one,
        grad_shift_one,
        grad_gain_two,
        grad_shift_two,
        grad_out_bias,
        grad_w_up,
        grad_bias_up,
        grad_w_down,
        grad_bias_down,
    )


def solution(mesh):
    placed = (
        P("row", "col"),
        P("row", "col"),
        P("row"),
        P(),
        P(),
        P("row", "col"),
        P("row", "col"),
        P("row", "col"),
        P("row", "col"),
        P("row", "col"),
        P("row", "col"),
        P("row"),
        P("row"),
        P("row"),
        P("row"),
        P("row"),
        P("row", None, "col"),
        P("row", "col"),
        P("row", "col", None),
        P("row", None),
    )
    return jax.shard_map(
        per_device,
        mesh=mesh,
        in_specs=placed,
        out_specs=(
            P("row", "col"),
            P("row", "col"),
            P("row", "col"),
            P("row", "col"),
            P("row", "col"),
            P("row", "col"),
            P("row", "col"),
            P("row", "col"),
            P("row"),
            P("row"),
            P("row"),
            P("row"),
            P("row"),
            P("row", None, "col"),
            P("row", "col"),
            P("row", "col", None),
            P("row", None),
        ),
        check_vma=False,
    )
```

profile of v0, /device:TPU:10, one launch (start us, length us, event | category | flops | bytes accessed | tf_op | source)
XLA Modules:
  0.0 1619.3 jit_solution(12008969213057462819)
XLA Ops:
  14.9 30.1 %all-reduce.13 = (bf16[768]{0:T(1024)(128)(2,1)S(1)}, bf16[768]{0:T(1024)(128)(2,1)S(1)}, bf16[768]{0:T(1024)(128)(2,1)S(1)}, bf16[768]{0:T(1024)(128)(2,1)S(1)}, bf16[768]{0:T(1024)(128)(2,1)}) all-reduce(bf16[768]{0:T(1024)(128)(2,1)S(1)} %dynamic-update-slice.1, ...), channel_id=1, replica_groups=mesh['row'=8,'col'=4] {'row'}, use_global_device_ids=true, to_apply=%add.1 | all-reduce | flops 3840 | bytes 15360
  45.1 31.7 %all_gather.50 = bf16[768,192]{1,0:T(8,128)(2,1)S(1)} all-gather(bf16[96,192]{1,0:T(8,128)(2,1)} %param.32), channel_id=1, replica_groups=mesh['row'=8,'col'=4] {'row'}, dimensions={0}, use_global_device_ids=true | all-gather | bytes 331776 | tf_op jit(solution)/shard_map/all_gather | solution.py:97
  87.5 21.0 %all-gather = bf16[8,8,3]{1,2,0:T(4,128)(2,1)S(1)} all-gather(bf16[1,8,3]{1,2,0:T(4,128)(2,1)S(1)} %bitcast.238), channel_id=1, replica_groups=mesh['row'=8,'col'=4] {'row'}, dimensions={0}, use_global_device_ids=true | all-gather | bytes 432 | tf_op jit(solution)/shard_map/all_gather | solution.py:100
  108.7 16.5 %all-gather.1 = bf16[8,8,3]{1,2,0:T(4,128)(2,1)S(1)} all-gather(bf16[1,8,3]{1,2,0:T(4,128)(2,1)S(1)} %bitcast.239), channel_id=1, replica_groups=mesh['row'=8,'col'=4] {'row'}, dimensions={0}, use_global_device_ids=true | all-gather | bytes 432 | tf_op jit(solution)/shard_map/all_gather | solution.py:101
  125.4 6.2 gather_fusion
  131.6 4.5 reduce-window.6
  137.4 29.1 %all_gather.52 = bf16[768,192]{1,0:T(8,128)(2,1)S(1)} all-gather(bf16[96,192]{1,0:T(8,128)(2,1)S(1)} %copy-done.35), channel_id=1, replica_groups=mesh['row'=8,'col'=4] {'row'}, dimensions={0}, use_global_device_ids=true | all-gather | bytes 331776 | tf_op jit(solution)/shard_map/all_gather | solution.py:96
  166.5 31.2 %all_gather.54 = bf16[768,192]{1,0:T(8,128)(2,1)S(1)} all-gather(bf16[96,192]{1,0:T(8,128)(2,1)S(1)} %copy-done.36), channel_id=1, replica_groups=mesh['row'=8,'col'=4] {'row'}, dimensions={0}, use_global_device_ids=true | all-gather | bytes 331776 | tf_op jit(solution)/shard_map/all_gather | solution.py:98
  197.7 48.1 %all_gather.57 = bf16[768,192]{1,0:T(8,128)(2,1)} all-gather(bf16[96,192]{1,0:T(8,128)(2,1)S(1)} %copy-done.37), channel_id=1, replica_groups=mesh['row'=8,'col'=4] {'row'}, dimensions={0}, use_global_device_ids=true | all-gather | bytes 331776 | tf_op jit(solution)/shard_map/all_gather | solution.py:99
  248.4 7.9 scatter_custom_fusion.1
  256.3 6.8 all-to-all-start.2
  268.2 32.7 %while.39 = (s32[]{:T(128)}, f32[3,1024]{1,0:T(4,128)S(1)}, f32[3,1024]{1,0:T(4,128)S(1)}, s32[]{:T(128)}, s32[]{:T(128)}, /*index=5*/s32[]{:T(128)}, bf16[8192,...) while((s32[]{:T(128)}, f32[3,1024]{1,0:T(4,128)S(1)}, ...), condition=%wide.region_5.6_spmd.clone, body=%wide.region_2.5_spmd.clone.sunk | while | flops 429927424 | bytes 30062800 | solution.py:162
  301.5 38.9 %all-gather.11.cloned.1.call-done = bf16[8192,192]{0,1:T(8,128)(2,1)} async-done(((bf16[1024,192]{0,1:T(8,128)(2,1)}), bf16[8192,192]{0,1:T(8,128)(2,1)}) %all-gather.11.cloned.1.call-update) | async-done | bytes 3145744 | tf_op jit(solution)/shard_map/all_gather | solution.py:124
  341.4 36.1 %while.40 = (s32[]{:T(128)}, f32[3,1024,64]{1,2,0:T(8,128)}, s32[]{:T(128)}, s32[]{:T(128)}, s32[]{:T(128)}, /*index=5*/bf16[8192,192]{0,1:T(8,128)(2,1)}, bf16[...) while((s32[]{:T(128)}, f32[3,1024,64]{1,2,0:T(8,128)}, ...), condition=%wide.region_7.8_spmd.clone, body=%wide.region_6.7_spmd.clone.sunk | while | flops 820188160 | bytes 6453463 | solution.py:190
  344.3 6.0 fusion.159
  353.4 6.0 fusion.159
  362.4 6.0 fusion.159
  371.4 6.0 fusion.159
  382.2 78.6 %all-reduce.19.cloned.1.call-done = bf16[1024,768]{1,0:T(8,128)(2,1)} async-done(((bf16[1024,768]{1,0:T(8,128)(2,1)}), bf16[1024,768]{1,0:T(8,128)(2,1)}) %all-reduce.19.cloned.1.call-update) | async-done | bytes 1572880 | tf_op jit(solution)/shard_map/psum | solution.py:196
  465.6 8.6 scatter_custom_fusion
  474.1 6.2 all-to-all-start
  480.3 8.3 all-reduce.21.cloned.1.call-start
  492.5 55.2 %all-to-all-done = bf16[16,128,768]{2,1,0:T(8,128)(2,1)} async-done(((bf16[16,128,768]{2,1,0:T(8,128)(2,1)}), bf16[16,128,768]{2,1,0:T(8,128)(2,1)}, u32[]{:S(2)}, u32[]{:S(2)}) %all-to-all-start) | async-done | bytes 3145760 | tf_op jit(solution)/shard_map/all_to_all | solution.py:210
  554.1 19.9 %convert_reduce_fusion.1 = (f32[2,768]{1,0:T(2,128)}, bf16[2,1024,768]{2,1,0:T(8,128)(2,1)S(1)}, f32[2,1024,768]{2,1,0:T(8,128)}) fusion(f32[2,1024,768]{2,1,0:T(8,128)S(1)} %get-tuple-element.497, f32[2,768]{1,0:T(2,128)S(1)} %convert_element_type.228, u8[1024,768]{1,0:T(8,128)(4,1)S(1)} %get-tuple-element.384, ...), kind=kOutput, calls=%fused_computation.57 | convolution fusion | flops 2541746688 | bytes 22818816 | tf_op jit(solution)/shard_map/ecd,efd->ecf/dot_general | solution.py:236
  575.7 4.0 convolution_convert_fusion
  579.7 69.6 %all-reduce.21.cloned.1.call-done = bf16[2,1024,768]{2,1,0:T(8,128)(2,1)} async-done(((bf16[2,1024,768]{2,1,0:T(8,128)(2,1)}), bf16[2,1024,768]{2,1,0:T(8,128)(2,1)}) %all-reduce.21.cloned.1.call-update) | async-done | bytes 3145744 | tf_op jit(solution)/shard_map/psum | solution.py:243
  649.3 6.8 copy.126
  656.1 6.0 all-to-all-start.3
  662.3 66.9 %all-to-all-done.3 = bf16[2,1024,768]{2,0,1:T(2,128)(2,1)} async-done(((bf16[2,1024,768]{2,0,1:T(2,128)(2,1)}), bf16[2,1024,768]{2,0,1:T(2,128)(2,1)}, u32[]{:S(2)}, u32[]{:S(2)}) %all-to-all-start.3) | async-done | bytes 3145760 | tf_op jit(solution)/shard_map/all_to_all | solution.py:244
  729.3 4.1 copy.127
  733.4 20.1 %gather_fusion.2 = bf16[1024,768]{1,0:T(8,128)(2,1)} fusion(bf16[16,128,768]{2,1,0:T(8,128)(2,1)} %bitcast.209, s32[1024]{0:T(1024)S(1)} %bitcast.205), kind=kCustom, calls=%fused_computation.2 | custom fusion | bytes 3153920 | tf_op jit(solution)/shard_map/gather | solution.py:245
  753.5 4.5 fusion.42
  767.7 109.0 %while.41 = (s32[]{:T(128)}, f32[1024,3,64]{0,2,1:T(8,128)S(1)}, bf16[8192,192]{0,1:T(8,128)(2,1)}, bf16[8192,192]{0,1:T(8,128)(2,1)}, s32[]{:T(128)}, /*index=5...) while((s32[]{:T(128)}, f32[1024,3,64]{0,2,1:T(8,128)S(1)}, ...), condition=%wide.region_21.22_spmd.clone, body=%wide.region_20.21_spmd.clone.sunk | while | flops 2047022080 | bytes 69753176 | solution.py:297
  770.8 6.4 fusion.170
  777.2 6.2 fusion.173
  783.4 7.2 fusion.171
  798.0 6.4 fusion.170
  804.4 6.2 fusion.173
  810.6 7.2 fusion.171
  825.3 6.4 fusion.170
  831.6 6.2 fusion.173
  837.8 7.2 fusion.171
  852.5 6.4 fusion.170
  858.9 6.2 fusion.173
  865.1 7.2 fusion.171
  877.9 5.5 multiply_convert_fusion
  883.4 4.0 convolution_convert_fusion.1
  890.6 170.9 %reduce-scatter.9.cloned.1.call-done = bf16[1024,192]{0,1:T(8,128)(2,1)} async-done(((bf16[8192,192]{0,1:T(8,128)(2,1)}), bf16[1024,192]{0,1:T(8,128)(2,1)}) %reduce-scatter.9.cloned.1.call-update) | async-done | bytes 393232 | tf_op jit(solution)/shard_map/reduce_scatter | solution.py:308
  1064.9 74.2 %reduce-scatter.11.cloned.1.call-done = bf16[1024,192]{0,1:T(8,128)(2,1)} async-done(((bf16[8192,192]{0,1:T(8,128)(2,1)}), bf16[1024,192]{0,1:T(8,128)(2,1)}) %reduce-scatter.11.cloned.1.call-update) | async-done | bytes 393232 | tf_op jit(solution)/shard_map/reduce_scatter | solution.py:311
  1139.1 4.8 add_convert_fusion.2
  1144.6 93.0 %all-reduce.23.cloned.1.call-done = (bf16[2,1024,768]{2,1,0:T(8,128)(2,1)}, bf16[1024,768]{1,0:T(8,128)(2,1)}) async-done(((bf16[2,1024,768]{2,1,0:T(8,128)(2,1)}, bf16[1024,768]{1,0:T(8,128)(2,1)}), (bf16[2,1024,768]{2,1,0:T(8,128)(2,1)}, bf16[1024,768]{1,0:T(8,128)(2,1)})) %all-reduce.23.cloned.1.call-update) | async-done | bytes 4718608 | tf_op jit(solution)/shard_map/psum | solution.py:217
  1240.1 4.9 copy.121
  1245.0 6.2 all-to-all-start.1
  1263.6 7.8 fusion.82
  1272.8 7.7 fusion.81
  1282.2 64.0 %reduce-scatter.19.cloned.1.call-done = bf16[96,192]{1,0:T(8,128)(2,1)} async-done(((bf16[768,192]{1,0:T(8,128)(2,1)}), bf16[96,192]{1,0:T(8,128)(2,1)}) %reduce-scatter.19.cloned.1.call-update) | async-done | bytes 36880 | tf_op jit(solution)/shard_map/reduce_scatter | solution.py:355
  1347.7 63.7 %reduce-scatter.13.cloned.1.call-done = bf16[96,192]{1,0:T(8,128)(2,1)} async-done(((bf16[768,192]{1,0:T(8,128)(2,1)}), bf16[96,192]{1,0:T(8,128)(2,1)}) %reduce-scatter.13.cloned.1.call-update) | async-done | bytes 36880 | tf_op jit(solution)/shard_map/reduce_scatter | solution.py:346
  1413.0 63.2 %reduce-scatter.15.cloned.1.call-done = bf16[96,192]{1,0:T(8,128)(2,1)} async-done(((bf16[768,192]{1,0:T(8,128)(2,1)}), bf16[96,192]{1,0:T(8,128)(2,1)}) %reduce-scatter.15.cloned.1.call-update) | async-done | bytes 36880 | tf_op jit(solution)/shard_map/reduce_scatter | solution.py:349
  1477.7 63.0 %reduce-scatter.17.cloned.1.call-done = bf16[96,192]{1,0:T(8,128)(2,1)} async-done(((bf16[768,192]{1,0:T(8,128)(2,1)}), bf16[96,192]{1,0:T(8,128)(2,1)}) %reduce-scatter.17.cloned.1.call-update) | async-done | bytes 36880 | tf_op jit(solution)/shard_map/reduce_scatter | solution.py:352
  1543.9 4.9 fusion.43
  1548.7 28.9 %all-reduce.12 = (bf16[64,3]{0,1:T(4,128)(2,1)S(1)}, bf16[64,3]{0,1:T(4,128)(2,1)S(1)}, bf16[768]{0:T(1024)(128)(2,1)S(1)}, bf16[768]{0:T(1024)(128)(2,1)S(1)}, ...) all-reduce(bf16[64,3]{0,1:T(4,128)(2,1)S(1)} %bitcast.237, ...), channel_id=8, replica_groups=mesh['row'=8,'col'=4] {'row'}, use_global_device_ids=true, to_apply=%region_32.33.clone | all-reduce | flops 4224 | bytes 16896
  1580.1 4.1 copy.122
  1584.2 19.6 %gather_fusion.1 = bf16[1024,768]{1,0:T(8,128)(2,1)} fusion(bf16[16,128,768]{2,1,0:T(8,128)(2,1)} %bitcast.210, s32[1024]{0:T(1024)S(1)} %bitcast.206), kind=kCustom, calls=%fused_computation.1 | custom fusion | bytes 3153920 | tf_op jit(solution)/shard_map/gather | solution.py:223
  1603.9 5.5 dynamic-slice_add_fusion
  (337 shorter events, 171.0 us)
Async XLA Ops:
  7.2 546.9 %copy-start = (bf16[2,768,768]{2,1,0:T(8,128)(2,1)S(1)}, bf16[2,768,768]{2,1,0:T(8,128)(2,1)}, u32[]{:S(2)}) copy-start(bf16[2,768,768]{2,1,0:T(8,128)(2,1)} %param.44) | copy-start | bytes 7077892
  7.2 69.6 %all-gather.7.cloned.1.call-start = ((), (), s32[]{:S(2)}) async-start(), calls=%async_computation.10 | async-start | bytes 1966080 | tf_op jit(solution)/shard_map/all_gather | solution.py:80
  7.9 237.9 %all-gather.13.cloned.1.call-start = ((), (), s32[]{:S(2)}) async-start(), calls=%async_computation.14 | async-start | bytes 1966080 | tf_op jit(solution)/shard_map/all_gather | solution.py:81
  8.7 259.4 %all-gather.9.cloned.1.call-start = ((), (), s32[]{:S(2)}) async-start(), calls=%async_computation.11 | async-start | bytes 3538944 | tf_op jit(solution)/shard_map/all_gather | solution.py:123
  45.1 38.4 %copy-start.38 = (f32[768]{0:T(1024)}, f32[768]{0:T(1024)S(1)}, u32[]{:S(2)}) copy-start(f32[768]{0:T(1024)S(1)} %convert_element_type.212) | copy-start | bytes 9220
  76.8 7.3 copy-start.16
  79.5 3.9 copy-start.6
  83.4 4.1 copy-start.48
  83.4 25.3 %copy-start.49 = (bf16[8,3]{0,1:T(4,128)(2,1)S(1)}, bf16[8,3]{0,1:T(4,128)(2,1)}, u32[]{:S(2)}) copy-start(bf16[8,3]{0,1:T(4,128)(2,1)} %param.36) | copy-start | bytes 148
  83.4 42.0 %copy-start.44 = (s32[1024]{0:T(1024)S(1)}, s32[1024]{0:T(1024)}, u32[]{:S(2)}) copy-start(s32[1024]{0:T(1024)} %param.28) | copy-start | bytes 12292
  83.4 42.0 %copy-start.5 = (s32[50304]{0:T(1024)S(1)}, s32[50304]{0:T(1024)}, u32[]{:S(2)}) copy-start(s32[50304]{0:T(1024)} %param.29) | copy-start | bytes 603652
  86.7 50.5 %copy-start.51 = (s32[2]{0:T(128)S(1)}, s32[2]{0:T(128)}, u32[]{:S(2)}) copy-start(s32[2]{0:T(128)} %constant.198) | copy-start | bytes 28
  86.7 50.5 %copy-start.50 = (s32[2]{0:T(128)S(1)}, s32[2]{0:T(128)}, u32[]{:S(2)}) copy-start(s32[2]{0:T(128)} %constant.201) | copy-start | bytes 28
  86.7 50.6 %copy-start.35 = (bf16[96,192]{1,0:T(8,128)(2,1)S(1)}, bf16[96,192]{1,0:T(8,128)(2,1)}, u32[]{:S(2)}) copy-start(bf16[96,192]{1,0:T(8,128)(2,1)} %param.31) | copy-start | bytes 110596
  86.7 79.8 %copy-start.36 = (bf16[96,192]{1,0:T(8,128)(2,1)S(1)}, bf16[96,192]{1,0:T(8,128)(2,1)}, u32[]{:S(2)}) copy-start(bf16[96,192]{1,0:T(8,128)(2,1)} %param.33) | copy-start | bytes 110596
  86.7 111.0 %copy-start.37 = (bf16[96,192]{1,0:T(8,128)(2,1)S(1)}, bf16[96,192]{1,0:T(8,128)(2,1)}, u32[]{:S(2)}) copy-start(bf16[96,192]{1,0:T(8,128)(2,1)} %param.34) | copy-start | bytes 110596
  166.5 99.5 %copy-start.20 = (bf16[768,192]{1,0:T(8,128)(2,1)}, bf16[768,192]{1,0:T(8,128)(2,1)S(1)}, u32[]{:S(2)}) copy-start(bf16[768,192]{1,0:T(8,128)(2,1)S(1)} %all_gather.52) | copy-start | bytes 884740
  197.7 65.4 %copy-start.14 = (bf16[768,192]{1,0:T(8,128)(2,1)}, bf16[768,192]{1,0:T(8,128)(2,1)S(1)}, u32[]{:S(2)}) copy-start(bf16[768,192]{1,0:T(8,128)(2,1)S(1)} %all_gather.54) | copy-start | bytes 884740
  256.3 217.9 %all-to-all-start.2 = ((bf16[16,128,768]{2,1,0:T(8,128)(2,1)}), bf16[16,128,768]{2,1,0:T(8,128)(2,1)}, u32[]{:S(2)}, u32[]{:S(2)}) async-start(bf16[16,128,768]{2,1,0:T(8,128)(2,1)} %bitcast.213), calls=%async_computation.2 | async-start | bytes 6291456 | tf_op jit(solution)/shard_map/all_to_all | solution.py:231
  263.1 77.3 %all-gather.11.cloned.1.call-start = ((), (), s32[]{:S(2)}) async-start(), calls=%async_computation.12 | async-start | bytes 3538944 | tf_op jit(solution)/shard_map/all_gather | solution.py:124
  266.0 194.9 %all-reduce.19.cloned.1.call-start = ((), (), s32[]{:S(2)}) async-start(), calls=%async_computation.13 | async-start | bytes 3145728 | tf_op jit(solution)/shard_map/psum | solution.py:196
  377.4 4.8 copy-start.47
  474.1 14.5 copy-start.45
  474.1 73.5 %all-to-all-start = ((bf16[16,128,768]{2,1,0:T(8,128)(2,1)}), bf16[16,128,768]{2,1,0:T(8,128)(2,1)}, u32[]{:S(2)}, u32[]{:S(2)}) async-start(bf16[16,128,768]{2,1,0:T(8,128)(2,1)} %bitcast.214), calls=%async_computation | async-start | bytes 6291456 | tf_op jit(solution)/shard_map/all_to_all | solution.py:210
  480.3 169.0 %all-reduce.21.cloned.1.call-start = ((), (), s32[]{:S(2)}) async-start(), calls=%async_computation.15 | async-start | bytes 6291456 | tf_op jit(solution)/shard_map/psum | solution.py:243
  550.0 4.1 copy-start.22
  554.1 19.9 %copy-start.13 = (f32[2,1024,768]{2,1,0:T(8,128)}, f32[2,1024,768]{2,1,0:T(8,128)S(1)}, u32[]{:S(2)}) copy-start(f32[2,1024,768]{2,1,0:T(8,128)S(1)} %get-tuple-element.497) | copy-start | bytes 18874372
  656.1 73.2 %all-to-all-start.3 = ((bf16[2,1024,768]{2,0,1:T(2,128)(2,1)}), bf16[2,1024,768]{2,0,1:T(2,128)(2,1)}, u32[]{:S(2)}, u32[]{:S(2)}) async-start(bf16[2,1024,768]{2,0,1:T(2,128)(2,1)} %copy.126), calls=%async_computation.3 | async-start | bytes 6291456 | tf_op jit(solution)/shard_map/all_to_all | solution.py:244
  662.1 399.4 %reduce-scatter.9.cloned.1.call-start = ((), (), s32[]{:S(2)}) async-start(), calls=%async_computation.16 | async-start | bytes 3538944 | tf_op jit(solution)/shard_map/reduce_scatter | solution.py:308
  729.3 4.1 copy-start.1
  753.5 4.5 copy-start.4
  753.5 4.5 copy-start.8
  770.8 6.4 copy-start.27
  770.8 6.4 copy-start.41
  777.2 6.2 copy-start.40
  798.0 6.4 copy-start.27
  798.0 6.4 copy-start.41
  804.4 6.2 copy-start.40
  825.2 6.4 copy-start.27
  825.3 6.4 copy-start.41
  831.6 6.2 copy-start.40
  852.5 6.4 copy-start.27
  852.5 6.4 copy-start.41
  858.9 6.2 copy-start.40
  876.7 262.4 %reduce-scatter.11.cloned.1.call-start = ((), (), s32[]{:S(2)}) async-start(), calls=%async_computation.17 | async-start | bytes 3538944 | tf_op jit(solution)/shard_map/reduce_scatter | solution.py:311
  877.4 360.2 %all-reduce.23.cloned.1.call-start = ((), (), s32[]{:S(2)}) async-start(), calls=%async_computation.22 | async-start | bytes 9437184 | tf_op jit(solution)/shard_map/psum | solution.py:217
  883.4 4.0 copy-start.24
  883.4 4.9 copy-start.21
  888.3 250.8 %copy-start.15 = (bf16[768,192]{1,0:T(8,128)(2,1)S(1)}, bf16[768,192]{1,0:T(8,128)(2,1)}, u32[]{:S(2)}) copy-start(bf16[768,192]{1,0:T(8,128)(2,1)} %copy-done.14) | copy-start | bytes 884740
  1245.0 6.2 copy-start.19
  1245.0 335.1 %all-to-all-start.1 = ((bf16[2,1024,768]{2,0,1:T(2,128)(2,1)}), bf16[2,1024,768]{2,0,1:T(2,128)(2,1)}, u32[]{:S(2)}, u32[]{:S(2)}) async-start(bf16[2,1024,768]{2,0,1:T(2,128)(2,1)} %copy.121), calls=%async_computation.1 | async-start | bytes 6291456 | tf_op jit(solution)/shard_map/all_to_all | solution.py:220
  1251.2 95.0 %reduce-scatter.19.cloned.1.call-start = ((), (), s32[]{:S(2)}) async-start(), calls=%async_computation.21 | async-start | bytes 442368 | tf_op jit(solution)/shard_map/reduce_scatter | solution.py:355
  1254.6 7.4 copy-start.30
  1254.6 156.8 %reduce-scatter.13.cloned.1.call-start = ((), (), s32[]{:S(2)}) async-start(), calls=%async_computation.18 | async-start | bytes 442368 | tf_op jit(solution)/shard_map/reduce_scatter | solution.py:346
  1257.5 218.8 %reduce-scatter.15.cloned.1.call-start = ((), (), s32[]{:S(2)}) async-start(), calls=%async_computation.19 | async-start | bytes 442368 | tf_op jit(solution)/shard_map/reduce_scatter | solution.py:349
  1263.3 8.1 copy-start.25
  1263.3 277.3 %reduce-scatter.17.cloned.1.call-start = ((), (), s32[]{:S(2)}) async-start(), calls=%async_computation.20 | async-start | bytes 442368 | tf_op jit(solution)/shard_map/reduce_scatter | solution.py:352
  1263.6 7.8 copy-start.11
  1280.5 263.3 %copy-start.32 = (f32[1024]{0:T(1024)S(1)}, f32[1024]{0:T(1024)}, u32[]{:S(2)}) copy-start(f32[1024]{0:T(1024)} %copy-done.31) | copy-start | bytes 12292
  1280.5 263.3 %copy-start.34 = (f32[1024]{0:T(1024)S(1)}, f32[1024]{0:T(1024)}, u32[]{:S(2)}) copy-start(f32[1024]{0:T(1024)} %copy-done.33) | copy-start | bytes 12292
  1280.5 263.3 %copy-start.39 = (f32[768]{0:T(1024)S(1)}, f32[768]{0:T(1024)}, u32[]{:S(2)}) copy-start(f32[768]{0:T(1024)} %copy-done.38) | copy-start | bytes 9220
  1543.8 4.9 copy-start.42
  1543.9 4.9 copy-start.43
  1580.1 4.1 copy-start.2
  (16 other events, 32.2 us)
Sparse Core Ops, SparseCore 0:
  9.6 20.7 all-gather.6
  31.9 19.6 all-gather.12
  86.9 66.6 all-gather.8
  266.3 74.0 all-gather.10
  382.3 78.4 all-reduce.18
  579.8 69.4 all-reduce.20
  876.8 184.6 reduce-scatter.8
  1065.1 73.9 reduce-scatter.10
  1144.0 93.5 all-reduce.22
  1255.0 91.2 reduce-scatter.18
  1350.1 61.2 reduce-scatter.12
  1415.0 61.1 reduce-scatter.14
  1479.5 61.1 reduce-scatter.16
where the time goes:
time: 1640 us; the launch traced here: 1620 us
  waiting for transfers between devices  903 us (55%)
  blocking collectives  237 us (14%)
  matrix products  203 us (12%)
  local copies, waits for them, and re-layouts  129 us (8%)
  other arithmetic  94 us (6%)
  starting transfers between devices  34.6 us (2%)
  between operations  17.4 us (1%)
    reduce_scatter x1, waiting for transfers between devices, per_device(): lax.psum_scatter(key_terms.astype(jnp.bfloat16), 'row', scatter_dimension...  171 us
    psum x1, waiting for transfers between devices, per_device(): lax.psum(expert_part.astype(jnp.bfloat16), 'col').astype(jnp.float32)  93 us
    psum x1, waiting for transfers between devices, per_device(): lax.psum(partial_out.astype(jnp.bfloat16), 'col').astype(jnp.float32)  78.6 us
    reduce_scatter x1, waiting for transfers between devices, per_device(): lax.psum_scatter(value_terms.astype(jnp.bfloat16), 'row', scatter_dimensi...  74.2 us
    psum x1, waiting for transfers between devices, per_device(): grad_expert_in = lax.psum(grad_expert_in.astype(jnp.bfloat16), 'col')  69.6 us
    all_to_all x1, waiting for transfers between devices, per_device(): lax.all_to_all(grad_expert_in, 'row', split_axis=1, concat_axis=0, tiled=...  66.9 us
    reduce_scatter x1, waiting for transfers between devices, per_device(): lax.psum_scatter(grad_w_output.astype(jnp.bfloat16), 'row', scatter_dimen...  64 us
    reduce_scatter x1, waiting for transfers between devices, per_device(): lax.psum_scatter(grad_wq.astype(jnp.bfloat16), 'row', scatter_dimension=0...  63.7 us
  transfers between devices with their start and end apart: 17, of which 12 were waited for; matrix products, arithmetic and copies ran while one was open for 12% of the time, Pallas kernels for 0%

commit v1 on v0

v1 whole, which is shorter than its diff:
```python
import functools

import jax
import jax.numpy as jnp
from jax import lax
from jax.experimental import pallas as pl
from jax.experimental.pallas import tpu as pltpu
from jax.sharding import PartitionSpec as P

D = 768
HD = 64
EXP_DEV = 2
LENGTH = 8192
PREFIX_MAX = 4096
COLS = 4

F32 = jnp.float32
BF16 = jnp.bfloat16
MESH = pl.DeviceIdType.MESH
LOG2E = 1.4426950408889634

epsilon = 1e-05
neg_big = -1e30

VSPEC = pl.BlockSpec(memory_space=pltpu.VMEM)
SSPEC = pl.BlockSpec(memory_space=pltpu.SMEM)
VMEM_BYTES = 64 * 1000 * 1000
DMA = pltpu.SemaphoreType.DMA


def params(collective=None):
    if collective is None:
        return pltpu.CompilerParams(vmem_limit_bytes=VMEM_BYTES)
    return pltpu.CompilerParams(
        vmem_limit_bytes=VMEM_BYTES, collective_id=collective, has_side_effects=True
    )


def push(src, dst, send_sem, recv_sem, peer):
    return pltpu.make_async_remote_copy(
        src_ref=src,
        dst_ref=dst,
        send_sem=send_sem,
        recv_sem=recv_sem,
        device_id=peer,
        device_id_type=MESH,
    )


def greet(peers):
    barrier = pltpu.get_barrier_semaphore()
    for peer in peers:
        pl.semaphore_signal(barrier, inc=1, device_id=peer, device_id_type=MESH)
    pl.semaphore_wait(barrier, len(peers))


def col_places():
    me = lax.axis_index("col")
    sib = me + 1 - 2 * (me % 2)
    across = (me + 2) % COLS
    diag = (sib + 2) % COLS
    return me, sib, across, diag


def start_kernel(
    rows, pieces, x_ref, w_ref, s_ref, xo_ref, wo_ref, so_ref, c_send, c_recv, r_send, r_recv
):
    me, sib, across, _ = col_places()
    row = lax.axis_index("row")
    peers = [{"row": (row + k) % rows} for k in range(1, rows)]
    greet(peers + [{"col": sib}, {"col": across}])
    step = x_ref.shape[0] // pieces
    sent = []
    for i in range(pieces):
        part = pl.ds(i * step, step)
        for way, peer in ((0, across), (1, sib)):
            copy = push(
                x_ref.at[part],
                xo_ref.at[me, part],
                c_send.at[way, i],
                c_recv.at[way, i],
                {"col": peer},
            )
            copy.start()
            sent.append(copy)
    row_copies = []
    for k, peer in enumerate(peers):
        for j, (src, dst) in enumerate(((w_ref, wo_ref), (s_ref, so_ref))):
            copy = push(src, dst.at[row], r_send.at[j, k], r_recv.at[j, k], peer)
            copy.start()
            row_copies.append(copy)
    xo_ref[me] = x_ref[...]
    wo_ref[row] = w_ref[...]
    so_ref[row] = s_ref[...]
    for i in range(pieces):
        part = pl.ds(i * step, step)
        sent[2 * i].wait_recv()
        copy = push(
            xo_ref.at[across, part],
            xo_ref.at[across, part],
            c_send.at[2, i],
            c_recv.at[2, i],
            {"col": sib},
        )
        copy.start()
        row_copies.append(copy)
    for i in range(pieces):
        sent[2 * i].wait_send()
        sent[2 * i + 1].wait()
    for copy in row_copies:
        copy.wait()


def start_gather(x, w, s, rows):
    pieces = 4
    return pl.pallas_call(
        functools.partial(start_kernel, rows, pieces),
        out_shape=(
            jax.ShapeDtypeStruct((COLS,) + x.shape, x.dtype),
            jax.ShapeDtypeStruct((rows,) + w.shape, w.dtype),
            jax.ShapeDtypeStruct((rows,) + s.shape, s.dtype),
        ),
        in_specs=[VSPEC] * 3,
        out_specs=(VSPEC,) * 3,
        scratch_shapes=[
            DMA((3, pieces)),
            DMA((3, pieces)),
            DMA((2, rows - 1)),
            DMA((2, rows - 1)),
        ],
        compiler_params=params(0),
    )(x, w, s)


def col_gather_kernel(pieces, x_ref, xo_ref, c_send, c_recv):
    me, sib, across, _ = col_places()
    greet([{"col": sib}, {"col": across}])
    step = x_ref.shape[0] // pieces
    sent, late = [], []
    for i in range(pieces):
        part = pl.ds(i * step, step)
        for way, peer in ((0, across), (1, sib)):
            copy = push(
                x_ref.at[part],
                xo_ref.at[me, part],
                c_send.at[way, i],
                c_recv.at[way, i],
                {"col": peer},
            )
            copy.start()
            sent.append(copy)
    xo_ref[me] = x_ref[...]
    for i in range(pieces):
        part = pl.ds(i * step, step)
        sent[2 * i].wait_recv()
        copy = push(
            xo_ref.at[across, part],
            xo_ref.at[across, part],
            c_send.at[2, i],
            c_recv.at[2, i],
            {"col": sib},
        )
        copy.start()
        late.append(copy)
    for i in range(pieces):
        sent[2 * i].wait_send()
        sent[2 * i + 1].wait()
        late[i].wait()


def col_gather(x, collective):
    pieces = 4
    return pl.pallas_call(
        functools.partial(col_gather_kernel, pieces),
        out_shape=jax.ShapeDtypeStruct((COLS,) + x.shape, x.dtype),
        in_specs=[VSPEC],
        out_specs=VSPEC,
        scratch_shapes=[DMA((3, pieces)), DMA((3, pieces))],
        compiler_params=params(collective),
    )(x)


def small_kernel(x_ref, xo_ref, c_send, c_recv):
    me = lax.axis_index("col")
    peers = [{"col": (me + k) % COLS} for k in range(1, COLS)]
    greet(peers)
    copies = []
    for k, peer in enumerate(peers):
        copy = push(x_ref, xo_ref.at[me], c_send.at[k], c_recv.at[k], peer)
        copy.start()
        copies.append(copy)
    xo_ref[me] = x_ref[...]
    for copy in copies:
        copy.wait()


def small_gather(x, collective):
    return pl.pallas_call(
        small_kernel,
        out_shape=jax.ShapeDtypeStruct((COLS,) + x.shape, x.dtype),
        in_specs=[VSPEC],
        out_specs=VSPEC,
        scratch_shapes=[DMA((COLS - 1,)), DMA((COLS - 1,))],
        compiler_params=params(collective),
    )(x)


def line_places(group):
    row = lax.axis_index("row")
    place = row % group
    level, side = place // 2, place % 2
    return row, place, level, side, row + 1 - 2 * side


def line_greet(levels, row, level, partner):
    barrier = pltpu.get_barrier_semaphore()
    pl.semaphore_signal(barrier, inc=1, device_id={"row": partner}, device_id_type=MESH)

    @pl.when(level > 0)
    def _():
        pl.semaphore_signal(barrier, inc=1, device_id={"row": row - 2}, device_id_type=MESH)

    @pl.when(level < levels - 1)
    def _():
        pl.semaphore_signal(barrier, inc=1, device_id={"row": row + 2}, device_id_type=MESH)

    count = 1 + (level > 0).astype(jnp.int32) + (level < levels - 1).astype(jnp.int32)
    pl.semaphore_wait(barrier, count)


def kv_kernel(
    group, low, pieces, kv_ref, out_ref, u_send, u_recv, d_send, d_recv, x_send, x_recv
):
    levels = group // 2
    row, place, level, side, partner = line_places(group)
    step = kv_ref.shape[0] // pieces
    line_greet(levels, row, level, partner)

    def make(at, i, way, src=None):
        part = pl.ds(i * step, step)
        dst = out_ref.at[2 * at + side, part]
        sems = ((u_send, u_recv), (d_send, d_recv), (x_send, x_recv))[way]
        peer = (row + 2, row - 2, partner)[way]
        return push(
            dst if src is None else src.at[part],
            dst,
            sems[0].at[at, i],
            sems[1].at[at, i],
            {"row": peer},
        )

    def other(at, i):
        part = pl.ds(i * step, step)
        dst = out_ref.at[2 * at + 1 - side, part]
        return push(dst, dst, x_send.at[at, i], x_recv.at[at, i], {"row": partner})

    def when(cond, run):
        @pl.when(cond)
        def _():
            for i in range(pieces):
                run(i)

    to_up = level < levels - 1
    own_down = (level > 0) & (level < low)
    own_side = (level < low) | (side == 0)
    for i in range(pieces):

        @pl.when(to_up)
        def _(i=i):
            make(level, i, 0, kv_ref).start()

        @pl.when(own_side)
        def _(i=i):
            make(level, i, 2, kv_ref).start()

        @pl.when(own_down)
        def _(i=i):
            make(level, i, 1, kv_ref).start()

    out_ref[place] = kv_ref[...]

    for k in range(1, levels):
        at = level - k
        for i in range(pieces):

            @pl.when(at >= 0)
            def _(at=at, i=i):
                make(at, i, 0).wait_recv()

                @pl.when(to_up)
                def _():
                    make(at, i, 0).start()

                make(at, i, 2).start()

    for k in range(1, low):
        at = level + k
        for i in range(pieces):

            @pl.when(at < low)
            def _(at=at, i=i):
                make(at, i, 1).wait_recv()

                @pl.when(level > 0)
                def _():
                    make(at, i, 1).start()

                make(at, i, 2).start()

    for at in range(levels):
        comes = (at < level) | ((at == level) & (side == 1)) if at >= low else None
        if comes is None:
            for i in range(pieces):
                other(at, i).wait_recv()
        else:
            when(comes, lambda i, at=at: other(at, i).wait_recv())

    when(to_up, lambda i: make(level, i, 0, kv_ref).wait_send())
    when(own_side, lambda i: make(level, i, 2, kv_ref).wait_send())
    when(own_down, lambda i: make(level, i, 1, kv_ref).wait_send())
    for k in range(1, levels):
        at = level - k
        when((at >= 0) & to_up, lambda i, at=at: make(at, i, 0).wait_send())
        when(at >= 0, lambda i, at=at: make(at, i, 2).wait_send())
    for k in range(1, low):
        at = level + k
        when((at < low) & (level > 0), lambda i, at=at: make(at, i, 1).wait_send())
        when(at < low, lambda i, at=at: make(at, i, 2).wait_send())


def kv_gather(kv, group, low, collective):
    pieces = 4
    levels = group // 2
    return pl.pallas_call(
        functools.partial(kv_kernel, group, low, pieces),
        out_shape=jax.ShapeDtypeStruct((group,) + kv.shape, kv.dtype),
        in_specs=[VSPEC],
        out_specs=VSPEC,
        scratch_shapes=[DMA((levels, pieces))] * 6,
        compiler_params=params(collective),
    )(kv)


def dkv_kernel(
    group,
    low,
    pieces,
    part_ref,
    out_ref,
    rx_ref,
    above_ref,
    below_ref,
    snd_ref,
    acc_ref,
    u_send,
    u_recv,
    d_send,
    d_recv,
    x_send,
    x_recv,
):
    levels = group // 2
    row, place, level, side, partner = line_places(group)
    step = out_ref.shape[0] // pieces
    line_greet(levels, row, level, partner)

    def cross(at, i):
        part = pl.ds(i * step, step)
        return push(
            part_ref.at[2 * at + 1 - side, part],
            rx_ref.at[at, part],
            x_send.at[at, i],
            x_recv.at[at, i],
            {"row": partner},
        )

    def line(at, i, up):
        part = pl.ds(i * step, step)
        sems = (u_send, u_recv) if up else (d_send, d_recv)
        return push(
            snd_ref.at[at, part],
            (below_ref if up else above_ref).at[at, part],
            sems[0].at[at, i],
            sems[1].at[at, i],
            {"row": row + 2 if up else row - 2},
        )

    def gone(at):
        return (at < low) | (at < level) | ((at == level) & (side == 1))

    def comes(at):
        return (at < low) | (at < level) | ((at == level) & (side == 0))

    for at in range(levels):
        for i in range(pieces):

            @pl.when(gone(at))
            def _(at=at, i=i):
                cross(at, i).start()

    def total(at, i, from_above, from_below):
        part = pl.ds(i * step, step)
        acc_ref[...] = part_ref[2 * at + side, part].astype(F32)

        @pl.when(comes(at))
        def _():
            cross(at, i).wait_recv()
            acc_ref[...] += rx_ref[at, part].astype(F32)

        @pl.when(from_above)
        def _():
            line(at, i, False).wait_recv()
            acc_ref[...] += above_ref[at, part].astype(F32)

        @pl.when(from_below)
        def _():
            line(at, i, True).wait_recv()
            acc_ref[...] += below_ref[at, part].astype(F32)

    not_top = level < levels - 1
    for at in range(levels - 1):
        for i in range(pieces):

            @pl.when(at < level)
            def _(at=at, i=i):
                total(at, i, not_top, jnp.bool_(False) if at >= low else jnp.bool_(False))
                snd_ref[at, pl.ds(i * step, step)] = acc_ref[...].astype(BF16)
                line(at, i, False).start()

    for at in range(low - 1, 0, -1):
        for i in range(pieces):

            @pl.when(at > level)
            def _(at=at, i=i):
                total(at, i, jnp.bool_(False), level > 0)
                snd_ref[at, pl.ds(i * step, step)] = acc_ref[...].astype(BF16)
                line(at, i, True).start()

    for i in range(pieces):
        total(level, i, not_top, (level > 0) & (level < low))
        out_ref[pl.ds(i * step, step)] = acc_ref[...].astype(BF16)

    for at in range(levels):
        for i in range(pieces):

            @pl.when(gone(at))
            def _(at=at, i=i):
                cross(at, i).wait_send()

            @pl.when(at < level)
            def _(at=at, i=i):
                line(at, i, False).wait_send()

            if at < low:

                @pl.when(at > level)
                def _(at=at, i=i):
                    line(at, i, True).wait_send()


def dkv_scatter(parts, group, low, collective):
    pieces = 4
    levels = group // 2
    _, tokens, width = parts.shape
    block = pltpu.VMEM((levels, tokens, width), BF16)
    return pl.pallas_call(
        functools.partial(dkv_kernel, group, low, pieces),
        out_shape=jax.ShapeDtypeStruct((tokens, width), BF16),
        in_specs=[VSPEC],
        out_specs=VSPEC,
        scratch_shapes=[
            block,
            block,
            pltpu.VMEM((low, tokens, width), BF16),
            block,
            pltpu.VMEM((tokens // pieces, width), F32),
        ]
        + [DMA((levels, pieces))] * 6,
        compiler_params=params(collective),
    )(parts)


def product_kernel(pieces, a_ref, b_ref, out_ref, snd_ref, rx_ref, far_ref, tot_ref, send, recv):
    me, sib, across, diag = col_places()
    greet([{"col": sib}, {"col": across}])
    step = a_ref.shape[0] // pieces

    def term(i, who):
        return lax.dot_general(
            a_ref[pl.ds(i * step, step)],
            b_ref[who],
            (((1,), (1,)), ((), ())),
            preferred_element_type=F32,
        )

    def near(i, j):
        part = pl.ds(i * step, step)
        return push(
            snd_ref.at[j, part], rx_ref.at[j, part], send.at[j, i], recv.at[j, i], {"col": sib}
        )

    def over(i):
        part = pl.ds(i * step, step)
        return push(tot_ref.at[part], far_ref.at[part], send.at[2, i], recv.at[2, i], {"col": across})

    for i in range(pieces):
        snd_ref[0, pl.ds(i * step, step)] = term(i, diag).astype(BF16)
        near(i, 0).start()
    for i in range(pieces):
        part = pl.ds(i * step, step)
        mine = term(i, across)
        near(i, 0).wait_recv()
        tot_ref[part] = (mine + rx_ref[0, part].astype(F32)).astype(BF16)
        over(i).start()
    for i in range(pieces):
        snd_ref[1, pl.ds(i * step, step)] = term(i, sib).astype(BF16)
        near(i, 1).start()
    for i in range(pieces):
        part = pl.ds(i * step, step)
        mine = term(i, me)
        near(i, 1).wait_recv()
        mine = mine + rx_ref[1, part].astype(F32)
        over(i).wait_recv()
        out_ref[part] = mine + far_ref[part].astype(F32)
    for i in range(pieces):
        near(i, 0).wait_send()
        near(i, 1).wait_send()
        over(i).wait_send()


def product_scatter(a, b, collective):
    pieces = 4
    tokens, width = a.shape[0], b.shape[1]
    block = pltpu.VMEM((tokens, width), BF16)
    pair = pltpu.VMEM((2, tokens, width), BF16)
    return pl.pallas_call(
        functools.partial(product_kernel, pieces),
        out_shape=jax.ShapeDtypeStruct((tokens, width), F32),
        in_specs=[VSPEC] * 2,
        out_specs=VSPEC,
        scratch_shapes=[pair, pair, block, block, DMA((3, pieces)), DMA((3, pieces))],
        compiler_params=params(collective),
    )(a, b)


def dispatch_kernel(rows, in_ref, out_ref, r_send, r_recv, c_send, c_recv):
    me, sib, across, _ = col_places()
    row = lax.axis_index("row")
    peers = [(row + k) % rows for k in range(1, rows)]
    greet([{"row": p} for p in peers] + [{"col": sib}, {"col": across}])
    copies = []
    for k, peer in enumerate(peers):
        copy = push(
            in_ref.at[peer], out_ref.at[me, row], r_send.at[k], r_recv.at[k], {"row": peer}
        )
        copy.start()
        copies.append(copy)

    def col(src, dst, k, way):
        return push(
            src, dst, c_send.at[way, k], c_recv.at[way, k], {"col": across if way == 0 else sib}
        )

    done, first = [], []
    for way in range(2):
        copy = col(in_ref.at[row], out_ref.at[me, row], 0, way)
        copy.start()
        (first if way == 0 else done).append(copy)
    out_ref[me, row] = in_ref[row]
    sources = [row] + [(row + rows - k) % rows for k in range(1, rows)]

    def forward(k):
        first[k].wait_recv()
        src = sources[k]
        copy = col(out_ref.at[across, src], out_ref.at[across, src], k, 2)
        copy.start()
        done.append(copy)

    for k in range(1, rows):
        copies[k - 1].wait_recv()
        block = out_ref.at[me, sources[k]]
        for way in range(2):
            copy = col(block, block, k, way)
            copy.start()
            (first if way == 0 else done).append(copy)
        forward(k - 1)
    forward(rows - 1)
    for copy in copies:
        copy.wait_send()
    for copy in first:
        copy.wait_send()
    for copy in done:
        copy.wait()


def dispatch(x, rows, collective):
    return pl.pallas_call(
        functools.partial(dispatch_kernel, rows),
        out_shape=jax.ShapeDtypeStruct((COLS,) + x.shape, x.dtype),
        in_specs=[VSPEC],
        out_specs=VSPEC,
        scratch_shapes=[DMA((rows - 1,)), DMA((rows - 1,)), DMA((3, rows)), DMA((3, rows))],
        compiler_params=params(collective),
    )(x)


def giveback_kernel(
    rows, in_ref, bias_ref, out_ref, rx_ref, far_ref, tot_ref, fin_ref, send, recv, r_send, r_recv
):
    me, sib, across, diag = col_places()
    row = lax.axis_index("row")
    order = [(row + k) % rows for k in range(1, rows)] + [row]
    greet([{"row": p} for p in order[:-1]] + [{"col": sib}, {"col": across}])

    def near(k, j):
        who = diag if j == 0 else sib
        return push(
            in_ref.at[who, order[k]], rx_ref.at[j, k], send.at[j, k], recv.at[j, k], {"col": sib}
        )

    def over(k):
        return push(tot_ref.at[k], far_ref.at[k], send.at[2, k], recv.at[2, k], {"col": across})

    def home(k):
        return push(
            fin_ref.at[k], out_ref.at[row], r_send.at[k], r_recv.at[k], {"row": order[k]}
        )

    for k in range(rows):
        near(k, 0).start()
        near(k, 1).start()

    def finish(k):
        near(k, 1).wait_recv()
        over(k).wait_recv()
        total = in_ref[me, order[k]].astype(F32) + rx_ref[1, k].astype(F32)
        total = total + far_ref[k].astype(F32) + bias_ref[...]
        if k == rows - 1:
            out_ref[row] = total.astype(BF16)
        else:
            fin_ref[k] = total.astype(BF16)
            home(k).start()

    for k in range(rows):
        near(k, 0).wait_recv()
        tot_ref[k] = (in_ref[across, order[k]].astype(F32) + rx_ref[0, k].astype(F32)).astype(BF16)
        over(k).start()
        if k >= 1:
            finish(k - 1)
    finish(rows - 1)
    for k in range(rows):
        near(k, 0).wait_send()
        near(k, 1).wait_send()
        over(k).wait_send()
        if k < rows - 1:
            home(k).wait()


def giveback(parts, bias, rows, collective):
    block = parts.shape[2:]
    one = pltpu.VMEM((rows,) + block, BF16)
    return pl.pallas_call(
        functools.partial(giveback_kernel, rows),
        out_shape=jax.ShapeDtypeStruct((rows,) + block, BF16),
        in_specs=[VSPEC] * 2,
        out_specs=VSPEC,
        scratch_shapes=[
            pltpu.VMEM((2, rows) + block, BF16),
            one,
            one,
            one,
            DMA((3, rows)),
            DMA((3, rows)),
            DMA((rows - 1,)),
            DMA((rows - 1,)),
        ],
        compiler_params=params(collective),
    )(parts, bias)


def end_kernel(rows, w_ref, s_ref, wo_ref, so_ref, wr_ref, sr_ref, send, recv):
    row = lax.axis_index("row")
    peers = [(row + k) % rows for k in range(1, rows)]
    greet([{"row": p} for p in peers])
    copies = []
    for k, peer in enumerate(peers):
        for j, (src, dst) in enumerate(((w_ref, wr_ref), (s_ref, sr_ref))):
            copy = push(src.at[peer], dst.at[k], send.at[j, k], recv.at[j, k], {"row": peer})
            copy.start()
            copies.append(copy)
    wo_ref[...] = w_ref[row].astype(F32)
    so_ref[...] = s_ref[row]
    for k in range(rows - 1):
        copies[2 * k].wait_recv()
        copies[2 * k + 1].wait_recv()
        wo_ref[...] += wr_ref[k].astype(F32)
        so_ref[...] += sr_ref[k]
    for copy in copies:
        copy.wait_send()


def end_scatter(w, s, rows, collective):
    return pl.pallas_call(
        functools.partial(end_kernel, rows),
        out_shape=(
            jax.ShapeDtypeStruct(w.shape[1:], F32),
            jax.ShapeDtypeStruct(s.shape[1:], F32),
        ),
        in_specs=[VSPEC] * 2,
        out_specs=(VSPEC,) * 2,
        scratch_shapes=[
            pltpu.VMEM((rows - 1,) + w.shape[1:], w.dtype),
            pltpu.VMEM((rows - 1,) + s.shape[1:], s.dtype),
            DMA((2, rows - 1)),
            DMA((2, rows - 1)),
        ],
        compiler_params=params(collective),
    )(w, s)


def nt(left, right):
    return lax.dot_general(left, right, (((1,), (1,)), ((), ())), preferred_element_type=F32)


def nn(left, right):
    return lax.dot_general(left, right, (((1,), (0,)), ((), ())), preferred_element_type=F32)


def tn(left, right):
    return lax.dot_general(left, right, (((0,), (0,)), ((), ())), preferred_element_type=F32)


def seen(key_start, query_start, shape, prefix):
    key = key_start + lax.broadcasted_iota(jnp.int32, shape, 0)
    query = query_start + lax.broadcasted_iota(jnp.int32, shape, 1)
    return (key < prefix) | (key <= query)


def forward_kernel(
    low_blocks, kb, qb, info_ref, q_ref, kv_ref, o_ref, ob_ref, lse_ref, m_ref, acc_ref
):
    place, prefix = info_ref[0], info_ref[1]
    tokens, width = q_ref.shape
    heads = width // HD
    per = tokens // kb
    ext = HD + 16
    m_ref[...] = jnp.full(m_ref.shape, neg_big, F32)
    acc_ref[...] = jnp.zeros(acc_ref.shape, F32)

    def block(j, masked):
        blk = j // per
        start = pl.multiple_of((j % per) * kb, kb)
        rows = kv_ref[blk, pl.ds(start, kb), :]
        for h in range(heads):
            k = rows[:, h * HD : (h + 1) * HD]
            v = rows[:, width + h * HD : width + (h + 1) * HD]
            v_ext = jnp.concatenate([v.T, jnp.ones((16, kb), BF16)], axis=0)
            for i in range(tokens // qb):
                cols = slice(i * qb, (i + 1) * qb)
                raw = nt(k, q_ref[cols, h * HD : (h + 1) * HD]) * LOG2E
                if masked:
                    allowed = seen(j * kb, place * tokens + i * qb, raw.shape, prefix)
                    raw = jnp.where(allowed, raw, neg_big)
                old = m_ref[h : h + 1, cols]
                new = jnp.maximum(old, jnp.max(raw, axis=0, keepdims=True))
                m_ref[h : h + 1, cols] = new
                weights = jnp.exp2(raw - new).astype(BF16)
                acc_ref[h, :, cols] = acc_ref[h, :, cols] * jnp.exp2(old - new) + nn(
                    v_ext, weights
                )

    def run(masked):
        def body(j, carry):
            block(j, masked)
            return carry

        return body

    lax.fori_loop(0, place * per, run(False), 0)
    lax.fori_loop(place * per, jnp.maximum(place + 1, low_blocks) * per, run(True), 0)
    for h in range(heads):
        total = acc_ref[h, HD : HD + 1, :]
        out = (acc_ref[h, :HD, :] / total).T
        o_ref[:, h * HD : (h + 1) * HD] = out
        ob_ref[:, h * HD : (h + 1) * HD] = out.astype(BF16)
        lse_ref[h : h + 1, :] = m_ref[h : h + 1, :] + jnp.log2(total)


def attention_forward(info, q, kv_all, low_blocks):
    tokens, width = q.shape
    heads = width // HD
    return pl.pallas_call(
        functools.partial(forward_kernel, low_blocks, 512, 512),
        out_shape=(
            jax.ShapeDtypeStruct((tokens, width), F32),
            jax.ShapeDtypeStruct((tokens, width), BF16),
            jax.ShapeDtypeStruct((8, tokens), F32),
        ),
        in_specs=[SSPEC, VSPEC, VSPEC],
        out_specs=(VSPEC,) * 3,
        scratch_shapes=[
            pltpu.VMEM((8, tokens), F32),
            pltpu.VMEM((heads, HD + 16, tokens), F32),
        ],
        compiler_params=params(),
    )(info, q, kv_all)


def backward_kernel(
    low_blocks, kb, info_ref, q_ref, kv_ref, do_ref, lse_ref, delta_ref, dq_ref, dkv_ref, dqt_ref
):
    place, prefix = info_ref[0], info_ref[1]
    tokens, width = q_ref.shape
    heads = width // HD
    per = tokens // kb
    dqt_ref[...] = jnp.zeros(dqt_ref.shape, F32)

    def block(j, masked):
        blk = j // per
        start = pl.multiple_of((j % per) * kb, kb)
        rows = kv_ref[blk, pl.ds(start, kb), :]
        for h in range(heads):
            feats = slice(h * HD, (h + 1) * HD)
            k = rows[:, feats]
            v = rows[:, width + h * HD : width + (h + 1) * HD]
            q, do = q_ref[:, feats], do_ref[:, feats]
            probs = jnp.exp2(nt(k, q) * LOG2E - lse_ref[h : h + 1, :])
            if masked:
                allowed = seen(j * kb, place * tokens, probs.shape, prefix)
                probs = jnp.where(allowed, probs, 0.0)
            grad = (probs * (nt(v, do) - delta_ref[h : h + 1, :])).astype(BF16)
            dkv_ref[blk, pl.ds(start, kb), feats] = nn(grad, q).astype(BF16)
            dkv_ref[blk, pl.ds(start, kb), width + h * HD : width + (h + 1) * HD] = nn(
                probs.astype(BF16), do
            ).astype(BF16)
            dqt_ref[feats, :] += nn(k.T, grad)

    def run(masked):
        def body(j, carry):
            block(j, masked)
            return carry

        return body

    lax.fori_loop(0, place * per, run(False), 0)
    lax.fori_loop(place * per, jnp.maximum(place + 1, low_blocks) * per, run(True), 0)
    dq_ref[...] = (dqt_ref[...] * HD**-0.5).T.astype(BF16)


def attention_backward(info, q, kv_all, do, lse, delta, low_blocks):
    tokens, width = q.shape
    return pl.pallas_call(
        functools.partial(backward_kernel, low_blocks, 256),
        out_shape=(
            jax.ShapeDtypeStruct((tokens, width), BF16),
            jax.ShapeDtypeStruct(kv_all.shape, BF16),
        ),
        in_specs=[SSPEC] + [VSPEC] * 5,
        out_specs=(VSPEC,) * 2,
        scratch_shapes=[pltpu.VMEM((width, tokens), F32)],
        compiler_params=params(),
    )(info, q, kv_all, do, lse, delta)


def expert_kernel(
    x_ref, up_ref, bias_ref, down_ref, part_ref, gup_ref, gbu_ref, gdown_ref, gbd_ref
):
    cols, rows, _, cap, both = x_ref.shape
    width = both // 2
    slots = rows * cap
    blocks = [x_ref[b, :, 0].reshape(slots, both) for b in range(cols)]
    x = jnp.concatenate([b[:, :width] for b in blocks], axis=1)
    g = jnp.concatenate([b[:, width:] for b in blocks], axis=1)
    gbd_ref[...] = jnp.sum(g.astype(F32), axis=0).reshape(gbd_ref.shape)
    hidden_units = up_ref.shape[2]
    chunk = 256
    part = jnp.zeros((slots, cols * width), F32)
    gx = jnp.zeros((slots, cols * width), F32)
    for f in range(hidden_units // chunk):
        cut = slice(f * chunk, (f + 1) * chunk)
        up, down = up_ref[0, :, cut], down_ref[0, cut, :]
        pre = nn(x, up) + bias_ref[0, :, cut].astype(F32)
        cdf = 0.5 * (1.0 + lax.erf(pre * (0.5**0.5)))
        slope = cdf + pre * (jnp.exp(-0.5 * pre * pre) * 0.3989422804014327)
        hidden = (pre * cdf).astype(BF16)
        grad = nt(g, down) * slope
        grad = grad.astype(BF16)
        part = part + nn(hidden, down)
        gx = gx + nt(grad, up)
        gdown_ref[0, cut, :] = tn(hidden, g)
        gup_ref[0, :, cut] = tn(x, grad)
        gbu_ref[0, :, cut] = jnp.sum(grad.astype(F32), axis=0, keepdims=True)
    for b in range(cols):
        cut = slice(b * width, (b + 1) * width)
        both_parts = jnp.concatenate([part[:, cut].astype(BF16), gx[:, cut].astype(BF16)], axis=1)
        part_ref[b, :, 0] = both_parts.reshape(rows, cap, both)


def experts(x, w_up, bias_up, w_down):
    cols, rows, count, cap, both = x.shape
    _, features, hidden = w_up.shape
    return pl.pallas_call(
        expert_kernel,
        grid=(count,),
        out_shape=(
            jax.ShapeDtypeStruct(x.shape, BF16),
            jax.ShapeDtypeStruct(w_up.shape, F32),
            jax.ShapeDtypeStruct((count, 1, hidden), F32),
            jax.ShapeDtypeStruct(w_down.shape, F32),
            jax.ShapeDtypeStruct((count, 1, features), F32),
        ),
        in_specs=[
            pl.BlockSpec((cols, rows, 1, cap, both), lambda e: (0, 0, e, 0, 0)),
            pl.BlockSpec((1, features, hidden), lambda e: (e, 0, 0)),
            pl.BlockSpec((1, 1, hidden), lambda e: (e, 0, 0)),
            pl.BlockSpec((1, hidden, features), lambda e: (e, 0, 0)),
        ],
        out_specs=(
            pl.BlockSpec((cols, rows, 1, cap, both), lambda e: (0, 0, e, 0, 0)),
            pl.BlockSpec((1, features, hidden), lambda e: (e, 0, 0)),
            pl.BlockSpec((1, 1, hidden), lambda e: (e, 0, 0)),
            pl.BlockSpec((1, hidden, features), lambda e: (e, 0, 0)),
            pl.BlockSpec((1, 1, features), lambda e: (e, 0, 0)),
        ),
        compiler_params=params(),
    )(x, w_up, bias_up.reshape(count, 1, hidden), w_down)


def per_device(
    layer_in,
    cotangent,
    token_ids,
    hash_table,
    prefix_len,
    w_query,
    w_key,
    w_value,
    w_output,
    bias_query,
    bias_value,
    gain_attn,
    shift_attn,
    gain_moe,
    shift_moe,
    bias_output,
    w_up,
    bias_up,
    w_down,
    bias_down,
):
    rows = lax.axis_size("row")
    row = lax.axis_index("row")
    col = lax.axis_index("col")
    tokens, width = layer_in.shape
    heads = width // HD
    seq_len = min(LENGTH, tokens * rows)
    group = seq_len // tokens
    low = -(-PREFIX_MAX // (2 * tokens))
    share = w_query.shape[0]
    bias_share = bias_query.shape[0]

    def line(v):
        return jnp.pad(v.astype(F32), (0, 128 - v.shape[0]))

    small = jnp.stack(
        [
            line(gain_attn),
            line(shift_attn),
            line(gain_moe),
            line(shift_moe),
            line(bias_output),
            line(bias_query.T.reshape(-1)),
            line(bias_value.T.reshape(-1)),
            jnp.zeros((128,), F32),
        ]
    )
    weights = jnp.concatenate([w_query, w_key, w_value, w_output], axis=1)
    x_all, w_all, s_all = start_gather(layer_in, weights, small, rows)
    w_all = w_all.reshape(D, 4 * width)
    w_qkv = w_all[:, : 3 * width]
    w_out = w_all[:, 3 * width :].reshape(COLS, width, width)
    gain_one, shift_one, gain_two, shift_two, out_bias = (
        s_all[:, i, :share].reshape(D) for i in range(5)
    )

    def own(v):
        return lax.dynamic_slice_in_dim(v, col * width, width, 0)

    query_bias, value_bias = (
        s_all[:, i, : heads * bias_share]
        .reshape(rows, heads, bias_share)
        .transpose(1, 0, 2)
        .reshape(width)
        for i in (5, 6)
    )

    expert_total = EXP_DEV * rows
    capacity = max(2, 2 * tokens // expert_total)
    expert_of = hash_table[token_ids]
    hits = expert_of[:, None] == jnp.arange(expert_total, dtype=jnp.int32)[None, :]
    earlier = (
        jnp.arange(tokens, dtype=jnp.int32)[None, :] < jnp.arange(tokens, dtype=jnp.int32)[:, None]
    )
    before = jnp.dot(earlier.astype(BF16), hits.astype(BF16), preferred_element_type=F32)
    slot_of = jnp.sum(jnp.where(hits, before, 0.0), axis=1).astype(jnp.int32)
    target = expert_of * capacity + slot_of
    chosen = (
        jnp.arange(expert_total * capacity, dtype=jnp.int32)[:, None] == target[None, :]
    ).astype(BF16)

    resid = x_all.transpose(1, 0, 2).reshape(tokens, D).astype(F32)
    mean_one = jnp.mean(resid, axis=-1, keepdims=True)
    centred = resid - mean_one
    rstd_one = lax.rsqrt(jnp.mean(centred * centred, axis=-1, keepdims=True) + epsilon)
    h_one = (centred * rstd_one * gain_one + shift_one).astype(BF16)
    qkv_bias = jnp.concatenate([query_bias, jnp.zeros_like(query_bias), value_bias])
    qkv = (jnp.dot(h_one, w_qkv, preferred_element_type=F32) + qkv_bias).astype(BF16)
    queries = qkv[:, :width] * jnp.asarray(HD**-0.5, BF16)
    kv_all = kv_gather(qkv[:, width:], group, low, 1)
    place = row % group
    seq_hit = row // group == jnp.arange(prefix_len.shape[0], dtype=jnp.int32)
    prefix = jnp.sum(jnp.where(seq_hit, prefix_len, 0))
    info = jnp.stack([place.astype(jnp.int32), prefix.astype(jnp.int32)])
    attended, attended_low, lse = attention_forward(info, queries, kv_all, 2 * low)
    branch = product_scatter(attended_low, w_out, 2)
    x_own = layer_in.astype(F32)
    mid = x_own + branch + own(out_bias)

    part_mean = jnp.mean(mid, axis=-1)
    part_spread = jnp.sum((mid - part_mean[:, None]) ** 2, axis=-1)
    stats = jnp.stack([part_mean, part_spread]).reshape(-1, 128)
    stats = small_gather(stats, 3).reshape(COLS, 2, tokens)
    mean_two = jnp.mean(stats[:, 0], axis=0)
    spread = jnp.sum(stats[:, 1] + width * (stats[:, 0] - mean_two) ** 2, axis=0) / D
    rstd_two = lax.rsqrt(spread + epsilon)[:, None]
    normed_two = (mid - mean_two[:, None]) * rstd_two
    gain_two_own = own(gain_two)
    h_two = (normed_two * gain_two_own + own(shift_two)).astype(BF16)

    outgoing = jnp.dot(
        chosen, jnp.concatenate([h_two, cotangent], axis=1), preferred_element_type=F32
    ).astype(BF16)
    block = (rows, EXP_DEV, capacity, 2 * width)
    received = dispatch(outgoing.reshape(block), rows, 4)
    parts, grad_w_up, grad_bias_up, grad_w_down, grad_bias_down = experts(
        received, w_up, bias_up, w_down
    )
    down_own = lax.dynamic_slice_in_dim(bias_down, col * width, width, 1).astype(F32)
    down_own = jnp.concatenate([down_own, jnp.zeros_like(down_own)], axis=1)[:, None, :]
    returned = giveback(parts, down_own, rows, 5).reshape(-1, 2 * width)
    combined = lax.dot_general(
        chosen, returned, (((0,), (0,)), ((), ())), preferred_element_type=F32
    )
    layer_out = (mid + combined[:, :width]).astype(BF16)
    grad_h_two = combined[:, width:]

    scaled = grad_h_two * gain_two_own
    sums = jnp.stack([jnp.sum(scaled, axis=-1), jnp.sum(scaled * normed_two, axis=-1)])
    sums = small_gather(sums.reshape(-1, 128), 6).reshape(COLS, 2, tokens)
    sums = jnp.sum(sums, axis=0) / D
    grad_mid = cotangent.astype(F32) + rstd_two * (
        scaled - sums[0][:, None] - normed_two * sums[1][:, None]
    )
    grad_all = col_gather(grad_mid.astype(BF16), 7)
    grad_wide = grad_all.transpose(1, 0, 2).reshape(tokens, D)
    grad_w_out = lax.dot_general(
        grad_wide, attended_low, (((0,), (0,)), ((), ())), preferred_element_type=F32
    )
    grad_attended = jnp.dot(
        grad_wide, w_out.reshape(D, width), preferred_element_type=F32
    ).astype(BF16)
    delta = jnp.sum(
        (grad_attended.astype(F32) * attended).reshape(tokens, heads, HD), axis=-1
    ).T
    delta = jnp.pad(delta, ((0, 8 - heads), (0, 0)))
    grad_q, kv_terms = attention_backward(
        info, queries, kv_all, grad_attended, lse, delta, 2 * low
    )
    grad_kv = dkv_scatter(kv_terms, group, low, 8)
    grad_qkv = jnp.concatenate([grad_q, grad_kv], axis=1)
    grad_w_qkv = lax.dot_general(
        h_one, grad_qkv, (((0,), (0,)), ((), ())), preferred_element_type=F32
    )
    grad_bias = jnp.sum(grad_qkv, axis=0, dtype=F32)
    grad_h_one = product_scatter(grad_qkv, w_qkv.reshape(COLS, width, 3 * width), 9)
    normed_one = (x_own - mean_one) * rstd_one
    scaled = grad_h_one * own(gain_one)
    sums = jnp.stack([jnp.sum(scaled, axis=-1), jnp.sum(scaled * normed_one, axis=-1)])
    vectors = jnp.stack(
        [
            jnp.sum(grad_h_one * normed_one, axis=0),
            jnp.sum(grad_h_one, axis=0),
            jnp.sum(grad_h_two * normed_two, axis=0),
            jnp.sum(grad_h_two, axis=0),
            jnp.sum(grad_mid, axis=0),
        ]
    )
    vectors = jnp.pad(vectors, ((0, 3), (0, 256 - width))).reshape(-1, 128)
    shared = small_gather(jnp.concatenate([sums.reshape(-1, 128), vectors]), 10)
    used = 2 * tokens // 128
    sums = jnp.sum(shared[:, :used].reshape(COLS, 2, tokens), axis=0) / D
    grad_in = grad_mid + rstd_one * (scaled - sums[0][:, None] - normed_one * sums[1][:, None])
    vectors = shared[:, used:].reshape(COLS, 8, 256)[:, :5, :width]
    vectors = vectors.transpose(1, 0, 2).reshape(5, rows, share).transpose(1, 0, 2)

    def by_row(v):
        v = v.reshape(heads, rows, bias_share).transpose(1, 0, 2).reshape(rows, 1, -1)
        return jnp.pad(v, ((0, 0), (0, 0), (0, 128 - v.shape[2])))

    small_terms = jnp.concatenate(
        [
            jnp.pad(vectors, ((0, 0), (0, 0), (0, 128 - share))),
            by_row(grad_bias[:width]),
            by_row(grad_bias[2 * width :]),
            jnp.zeros((rows, 1, 128), F32),
        ],
        axis=1,
    )
    weight_terms = jnp.concatenate([grad_w_qkv, grad_w_out], axis=1).astype(BF16)
    weight_sums, small_sums = end_scatter(
        weight_terms.reshape(rows, share, 4 * width), small_terms, rows, 11
    )

    def bias_back(v):
        return v[: heads * bias_share].reshape(heads, bias_share).T

    return (
        layer_out,
        grad_in,
        weight_sums[:, :width],
        weight_sums[:, width : 2 * width],
        weight_sums[:, 2 * width : 3 * width],
        weight_sums[:, 3 * width :],
        bias_back(small_sums[5]),
        bias_back(small_sums[6]),
        small_sums[0, :share],
        small_sums[1, :share],
        small_sums[2, :share],
        small_sums[3, :share],
        small_sums[4, :share],
        grad_w_up,
        grad_bias_up[:, 0],
        grad_w_down,
        grad_bias_down[:, 0],
    )


def solution(mesh):
    placed = (
        P("row", "col"),
        P("row", "col"),
        P("row"),
        P(),
        P(),
        P("row", "col"),
        P("row", "col"),
        P("row", "col"),
        P("row", "col"),
        P("row", "col"),
        P("row", "col"),
        P("row"),
        P("row"),
        P("row"),
        P("row"),
        P("row"),
        P("row", None, "col"),
        P("row", "col"),
        P("row", "col", None),
        P("row", None),
    )
    return jax.shard_map(
        per_device,
        mesh=mesh,
        in_specs=placed,
        out_specs=(
            P("row", "col"),
            P("row", "col"),
            P("row", "col"),
            P("row", "col"),
            P("row", "col"),
            P("row", "col"),
            P("row", "col"),
            P("row", "col"),
            P("row"),
            P("row"),
            P("row"),
            P("row"),
            P("row"),
            P("row", None, "col"),
            P("row", "col"),
            P("row", "col", None),
            P("row", None),
        ),
        check_vma=False,
    )
```

time: 1640 us -> 665 us (0.41)
  waiting for transfers between devices: 903 us -> 0 us
  Pallas kernels: 0 us -> 565 us
  blocking collectives: 237 us -> 0 us
  matrix products: 203 us -> 19.2 us
  local copies, waits for them, and re-layouts: 129 us -> 40 us
  other arithmetic: 94 us -> 34.2 us
  starting transfers between devices: 34.6 us -> 0 us
    pallas_call x0 -> x15, Pallas kernels: none -> 565 us  [the longest x1 111 us: dispatch(): pl.pallas_call(functools.partial(dispatch_kernel, rows), out_shape=jax.Sh...]
    reduce_scatter x6 -> x0, waiting for transfers between devices: 499 us -> none  [the longest x1 171 us: per_device(): lax.psum_scatter(key_terms.astype(jnp.bfloat16), 'row', scatter_dimension...]
    psum x3 -> x0, waiting for transfers between devices: 241 us -> none  [the longest x1 93 us: per_device(): lax.psum(expert_part.astype(jnp.bfloat16), 'col').astype(jnp.float32)]
    dot_general x46 -> x7, matrix products: 203 us -> 19.2 us  [the longest x1 4.93 us: per_device(): lax.dot_general(chosen, returned, (((0,), (0,)), ((), ())), preferred_ele...]
    all_gather x6 -> x0, blocking collectives: 178 us -> none  [the longest x1 48.1 us: per_device(): lax.all_gather(w_output, 'row', axis=0, tiled=True)]
    all_to_all x4 -> x0, waiting for transfers between devices: 122 us -> none  [the longest x1 66.9 us: per_device(): lax.all_to_all(grad_expert_in, 'row', split_axis=1, concat_axis=0, tiled=...]
    unnamed x2 -> x0, blocking collectives: 59.1 us -> none
    gather x2 -> x0, local copies, waits for them, and re-layouts: 39.8 us -> none  [the longest x1 20.1 us: per_device(): grad_h_two = grad_back[expert_of, slot_of].astype(jnp.float32)]
  transfers between devices with their start and end apart: 17 -> 0, of which waited for: 12 -> 0; matrix products, arithmetic and copies ran while one was open for 12% -> 0% of each run, Pallas kernels for 0% -> 0%
where the time goes in v1:
time: 665 us; the launch traced here: 660 us
  Pallas kernels  565 us (85%)
  local copies, waits for them, and re-layouts  40 us (6%)
  other arithmetic  34.2 us (5%)
  matrix products  19.2 us (3%)
    pallas_call x1, Pallas kernels, dispatch(): pl.pallas_call(functools.partial(dispatch_kernel, rows), out_shape=jax.Sh...  111 us
    pallas_call x1, Pallas kernels, dkv_scatter(): pl.pallas_call(functools.partial(dkv_kernel, group, low, pieces), out_sha...  86.2 us
    pallas_call x1, Pallas kernels, giveback(): pl.pallas_call(functools.partial(giveback_kernel, rows), out_shape=jax.Sh...  62.9 us
    pallas_call x1, Pallas kernels, end_scatter(): pl.pallas_call(functools.partial(end_kernel, rows), out_shape=(jax.ShapeD...  54.1 us
    pallas_call x1, Pallas kernels, attention_forward(): pl.pallas_call(functools.partial(forward_kernel, low_blocks, 512, 512), o...  41.2 us
    pallas_call x1, Pallas kernels, attention_backward(): pl.pallas_call(functools.partial(backward_kernel, low_blocks, 256), out_s...  41.1 us
    pallas_call x1, Pallas kernels, kv_gather(): pl.pallas_call(functools.partial(kv_kernel, group, low, pieces), out_shap...  41 us
    pallas_call x2, Pallas kernels, product_scatter(): pl.pallas_call(functools.partial(product_kernel, pieces), out_shape=jax.S...  37.5 us

profile of v1, /device:TPU:10, one launch (start us, length us, event | category | flops | bytes accessed | tf_op | source)
XLA Modules:
  0.0 660.2 jit_solution(9265316033348681435)
XLA Ops:
  2.0 0.8 convert_element_type.101
  2.7 0.8 convert_element_type.99
  3.5 0.7 bitcast_convert_fusion.2
  4.2 0.7 bitcast_convert_fusion.4
  4.8 0.7 bitcast_convert_fusion.6
  5.5 0.6 stack.111.s_ref
  6.1 2.0 copy.48.x_ref
  8.1 1.6 pad_maximum_fusion.2.w_ref
  9.8 33.8 %shard_map.323 = (bf16[4,1024,192]{2,1,0:T(8,128)(2,1)}, bf16[8,96,768]{2,1,0:T(8,128)(2,1)}, f32[8,8,128]{2,1,0:T(8,128)}) custom-call(bf16[1024,192]{1,0:T(8,128)(2,1)} %copy.48.x_ref, bf16[96,768]{1,0:T(8,128)(2,1)} %pad_maximum_fusion.2.w_ref, f32[8,128]{1,0:T(8,128)} %stack.111.s_ref), custom_call_target="tpu_custom_call" | custom-call | tf_op jit(solution)/shard_map/pallas_call | solution.py:116
  43.6 2.1 convert_reduce_fusion
  45.8 0.8 fusion.3
  46.8 2.4 convert_bitcast_fusion
  49.2 3.8 copy.50
  53.0 1.7 fusion.10
  55.1 3.1 add_convert_fusion
  58.3 1.2 slice.171.kv_ref
  59.5 41.0 %shard_map.324.kv_ref = bf16[8,1024,384]{2,1,0:T(8,128)(2,1)} custom-call(bf16[1024,384]{1,0:T(8,128)(2,1)} %slice.171.kv_ref), custom_call_target="tpu_custom_call" | custom-call | tf_op jit(solution)/shard_map/pallas_call | solution.py:334
  100.5 0.9 slice_multiply_fusion.1.q_ref
  101.4 41.2 %shard_map.325 = (f32[1024,192]{1,0:T(8,128)}, bf16[1024,192]{1,0:T(8,128)(2,1)}, f32[8,1024]{1,0:T(8,128)}) custom-call(s32[2]{0:T(128)} %pad_add_fusion.info_ref, bf16[1024,192]{1,0:T(8,128)(2,1)} %slice_multiply_fusion.1.q_ref, bf16[8,1024,384]{2,1,0:T(8,128)(2,1)} %shard_map.324.kv_ref), custom_call_target="tpu_custom_call" | custom-call | tf_op jit(solution)/shard_map/pallas_call | solution.py:792
  142.6 2.0 slice.172
  144.6 18.3 %shard_map.326 = f32[1024,192]{1,0:T(8,128)} custom-call(bf16[1024,192]{1,0:T(8,128)(2,1)} %get-tuple-element.35.a_ref, bf16[4,192,192]{2,1,0:T(8,128)(2,1)} %bitcast.141), custom_call_target="tpu_custom_call" | custom-call | tf_op jit(solution)/shard_map/pallas_call | solution.py:536
  163.1 1.5 fusion.45
  165.5 5.0 shard_map.327
  170.5 0.8 reshape.221
  172.1 6.2 gather_fusion
  179.0 3.6 fusion.11
  182.6 111.2 %shard_map.328.x_ref = bf16[4,8,2,128,384]{4,3,2,1,0:T(8,128)(2,1)} custom-call(bf16[8,2,128,384]{3,2,1,0:T(8,128)(2,1)} %bitcast.142), custom_call_target="tpu_custom_call" | custom-call | tf_op jit(solution)/shard_map/pallas_call | solution.py:597
  294.4 23.0 %shard_map.329 = (bf16[4,8,2,128,384]{4,3,2,1,0:T(8,128)(2,1)}, f32[2,768,768]{2,1,0:T(8,128)}, f32[2,1,768]{2,1,0:T(1,128)}, f32[2,768,768]{2,1,0:T(8,128)}, f32[2,1,768]{2,1,0:T(1,128)}) custom-call(bf16[4,8,2,128,384]{4,3,2,1,0:T(8,128)(2,1)} %shard_map.328.x_ref, bf16[2,768,768]{2,1,0:T(8,128)(2,1)} %up_ref.1, bf16[2,1,768]{2,1,0:T(2,128)(2,1)} %copy.56.bias_ref, ...), custom_call_target="tpu_custom_call" | custom-call | tf_op jit(solution)/shard_map/pallas_call | solution.py:902
  317.5 0.8 constant_dynamic-slice_fusion
  318.8 62.9 %shard_map.330 = bf16[8,2,128,384]{3,2,1,0:T(8,128)(2,1)} custom-call(bf16[4,8,2,128,384]{4,3,2,1,0:T(8,128)(2,1)} %get-tuple-element.36.in_ref, f32[2,1,384]{2,1,0:T(1,128)} %reshape.247.bias_ref), custom_call_target="tpu_custom_call" | custom-call | tf_op jit(solution)/shard_map/pallas_call | solution.py:662
  381.7 4.9 fusion
  386.6 2.2 multiply_reduce_fusion
  388.8 0.6 reshape.225.x_ref
  389.4 5.0 shard_map.331
  394.4 0.8 reduce_sum.193
  395.2 3.0 fusion.44
  398.2 0.8 convert_element_type.113.x_ref
  399.1 17.5 %shard_map.332 = bf16[4,1024,192]{2,1,0:T(8,128)(2,1)} custom-call(bf16[1024,192]{1,0:T(8,128)(2,1)} %convert_element_type.113.x_ref), custom_call_target="tpu_custom_call" | custom-call | tf_op jit(solution)/shard_map/pallas_call | solution.py:173
  416.6 3.9 copy.60
  420.5 3.4 convert_multiply_fusion
  423.9 1.2 copy.62
  425.1 1.2 reduce_sum.194
  426.3 0.6 pad.58.delta_ref
  427.0 41.1 %shard_map.333 = (bf16[1024,192]{1,0:T(8,128)(2,1)}, bf16[8,1024,384]{2,1,0:T(8,128)(2,1)}) custom-call(s32[2]{0:T(128)} %pad_add_fusion.info_ref, bf16[1024,192]{1,0:T(8,128)(2,1)} %slice_multiply_fusion.1.q_ref, bf16[8,1024,384]{2,1,0:T(8,128)(2,1)} %shard_map.324.kv_ref, bf16[1024,192]{1,0:T(8,128)(2,1)} %get-tuple-element.124.do_ref, ...), custom_call_target="tpu_custom_call" | custom-call | tf_op jit(solution)/shard_map/pallas_call | solution.py:852
  468.1 86.2 %shard_map.334 = bf16[1024,384]{1,0:T(8,128)(2,1)} custom-call(bf16[8,1024,384]{2,1,0:T(8,128)(2,1)} %get-tuple-element.40.part_ref), custom_call_target="tpu_custom_call" | custom-call | tf_op jit(solution)/shard_map/pallas_call | solution.py:466
  554.2 1.9 convert_reduce_fusion.1
  556.5 2.9 pad_maximum_fusion.a_ref
  559.4 1.0 slice.169
  560.5 19.1 %shard_map.335 = f32[1024,192]{1,0:T(8,128)} custom-call(bf16[1024,576]{1,0:T(8,128)(2,1)} %pad_maximum_fusion.a_ref, bf16[4,192,576]{2,1,0:T(8,128)(2,1)} %bitcast.133), custom_call_target="tpu_custom_call" | custom-call | tf_op jit(solution)/shard_map/pallas_call | solution.py:536
  579.7 2.0 fusion.20
  582.3 5.1 shard_map.336
  587.5 0.8 fusion.48
  588.5 0.7 fusion.31.s_ref
  589.2 3.1 convolution_convert_fusion
  592.9 1.2 pad_maximum_fusion.1.w_ref
  594.2 54.1 %shard_map.337 = (f32[96,768]{1,0:T(8,128)}, f32[8,128]{1,0:T(8,128)}) custom-call(bf16[8,96,768]{2,1,0:T(8,128)(2,1)} %pad_maximum_fusion.1.w_ref, f32[8,8,128]{2,1,0:T(8,128)} %fusion.31.s_ref), custom_call_target="tpu_custom_call" | custom-call | tf_op jit(solution)/shard_map/pallas_call | solution.py:703
  648.3 1.9 fusion.47
  650.2 0.8 slice_reduce_fusion.9
  650.9 0.7 reshape.237
  651.6 0.7 reshape.238
  652.3 1.4 slice_bitcast_fusion.4
  653.7 1.7 fusion.24
  655.4 2.5 copy.70
  657.9 0.9 copy.69
  (100 shorter events, 8.2 us)
Async XLA Ops:
  0.7 171.4 %copy-start = (s32[50304]{0:T(1024)S(1)}, s32[50304]{0:T(1024)}, u32[]{:S(2)}) copy-start(s32[50304]{0:T(1024)} %param.23) | copy-start | bytes 603652
  43.6 2.2 copy-start.2
  43.6 3.0 copy-start.12
  142.6 20.5 %copy-start.3 = (bf16[1024,192]{1,0:T(8,128)(2,1)S(1)}, bf16[1024,192]{1,0:T(8,128)(2,1)}, u32[]{:S(2)}) copy-start(bf16[1024,192]{1,0:T(8,128)(2,1)} %copy.48.x_ref) | copy-start | bytes 1179652
  164.5 7.6 %copy-start.15 = (s32[1024]{0:T(1024)S(1)}, s32[1024]{0:T(1024)}, u32[]{:S(2)}) copy-start(s32[1024]{0:T(1024)} %param.22) | copy-start | bytes 12292
  172.1 6.7 %copy-start.11 = (bf16[1024,192]{0,1:T(8,128)(2,1)S(1)}, bf16[1024,192]{0,1:T(8,128)(2,1)}, u32[]{:S(2)}) copy-start(bf16[1024,192]{0,1:T(8,128)(2,1)} %param.21) | copy-start | bytes 1179652
  179.0 3.6 copy-start.9
  182.6 111.2 %copy-start.16 = (bf16[2,768]{1,0:T(2,128)(2,1)S(1)}, bf16[2,768]{1,0:T(2,128)(2,1)}, u32[]{:S(2)}) copy-start(bf16[2,768]{1,0:T(2,128)(2,1)} %param.37) | copy-start | bytes 9220
  554.2 5.2 copy-start.7
  560.5 28.7 %copy-start.5 = (bf16[1024,384]{1,0:T(8,128)(2,1)S(1)}, bf16[1024,384]{1,0:T(8,128)(2,1)}, u32[]{:S(2)}) copy-start(bf16[1024,384]{1,0:T(8,128)(2,1)} %shard_map.334) | copy-start | bytes 2359300
  589.2 3.1 copy-start.6
  589.2 3.2 copy-start.10
  592.9 60.7 %copy-start.4 = (f32[1024,192]{1,0:T(8,128)S(1)}, f32[1024,192]{1,0:T(8,128)}, u32[]{:S(2)}) copy-start(f32[1024,192]{1,0:T(8,128)} %shard_map.335) | copy-start | bytes 2359300
  653.7 6.3 copy-start.1
  655.4 2.5 copy-start.8
  655.4 3.4 copy-start.14
  655.4 4.0 copy-start.13

commit v2 on v1

--- a/solution.py
+++ b/solution.py
@@ -228,12 +228,51 @@
     pl.semaphore_wait(barrier, count)
 
 
-def kv_kernel(
-    group, low, pieces, kv_ref, out_ref, u_send, u_recv, d_send, d_recv, x_send, x_recv
+def nt(left, right):
+    return lax.dot_general(left, right, (((1,), (1,)), ((), ())), preferred_element_type=F32)
+
+
+def nn(left, right):
+    return lax.dot_general(left, right, (((1,), (0,)), ((), ())), preferred_element_type=F32)
+
+
+def tn(left, right):
+    return lax.dot_general(left, right, (((0,), (0,)), ((), ())), preferred_element_type=F32)
+
+
+def seen(key_start, query_start, shape, prefix):
+    key = key_start + lax.broadcasted_iota(jnp.int32, shape, 0)
+    query = query_start + lax.broadcasted_iota(jnp.int32, shape, 1)
+    return (key < prefix) | (key <= query)
+
+
+def forward_kernel(
+    group,
+    low,
+    pieces,
+    qb,
+    info_ref,
+    q_ref,
+    kv_ref,
+    out_ref,
+    o_ref,
+    ob_ref,
+    lse_ref,
+    m_ref,
+    acc_ref,
+    u_send,
+    u_recv,
+    d_send,
+    d_recv,
+    x_send,
+    x_recv,
 ):
     levels = group // 2
     row, place, level, side, partner = line_places(group)
-    step = kv_ref.shape[0] // pieces
+    prefix = info_ref[0]
+    tokens, width = q_ref.shape
+    heads = width // HD
+    step = tokens // pieces
     line_greet(levels, row, level, partner)
 
     def make(at, i, way, src=None):
@@ -278,42 +317,95 @@
             make(level, i, 1, kv_ref).start()
 
     out_ref[place] = kv_ref[...]
-
-    for k in range(1, levels):
-        at = level - k
-        for i in range(pieces):
-
-            @pl.when(at >= 0)
-            def _(at=at, i=i):
+    m_ref[...] = jnp.full(m_ref.shape, neg_big, F32)
+    acc_ref[...] = jnp.zeros(acc_ref.shape, F32)
+    units = [(h, i) for h in range(heads) for i in range(tokens // qb)]
+
+    def block(blk, masked):
+        def raw_of(h, i):
+            feats = slice(h * HD, (h + 1) * HD)
+            raw = nt(out_ref[blk, :, feats], q_ref[i * qb : (i + 1) * qb, feats])
+            if masked:
+                allowed = seen(blk * tokens, place * tokens + i * qb, raw.shape, prefix)
+                raw = jnp.where(allowed, raw, neg_big)
+            return raw
+
+        def soften(h, i, raw):
+            cols = slice(i * qb, (i + 1) * qb)
+            old = m_ref[h : h + 1, cols]
+            new = jnp.maximum(old, jnp.max(raw, axis=0, keepdims=True))
+            m_ref[h : h + 1, cols] = new
+            weights = jnp.exp2((raw - new) * LOG2E).astype(BF16)
+            return weights, jnp.exp2((old - new) * LOG2E)
+
+        def gather(h, i, weights, scale):
+            cols = slice(i * qb, (i + 1) * qb)
+            v = out_ref[blk, :, width + h * HD : width + (h + 1) * HD]
+            v_ext = jnp.concatenate([v.T, jnp.ones((16, tokens), BF16)], axis=0)
+            acc_ref[h, :, cols] = acc_ref[h, :, cols] * scale + nn(v_ext, weights)
+
+        coming, waiting = raw_of(*units[0]), None
+        for n, unit in enumerate(units):
+            raw = coming
+            if n + 1 < len(units):
+                coming = raw_of(*units[n + 1])
+            soft = soften(*unit, raw)
+            if waiting is not None:
+                gather(*waiting)
+            waiting = unit + soft
+        gather(*waiting)
+
+    def event(e, carry):
+        t, cross = e // 2, e % 2
+        at = jnp.where(t <= level, level - t, t)
+        live = (t <= level) | (t < low)
+        line_in = live & (cross == 0)
+
+        @pl.when(line_in & (at < level))
+        def _():
+            for i in range(pieces):
                 make(at, i, 0).wait_recv()
 
                 @pl.when(to_up)
-                def _():
+                def _(i=i):
                     make(at, i, 0).start()
 
                 make(at, i, 2).start()
 
-    for k in range(1, low):
-        at = level + k
-        for i in range(pieces):
-
-            @pl.when(at < low)
-            def _(at=at, i=i):
+        @pl.when(line_in & (at > level))
+        def _():
+            for i in range(pieces):
                 make(at, i, 1).wait_recv()
 
                 @pl.when(level > 0)
-                def _():
+                def _(i=i):
                     make(at, i, 1).start()
 
                 make(at, i, 2).start()
 
-    for at in range(levels):
-        comes = (at < level) | ((at == level) & (side == 1)) if at >= low else None
-        if comes is None:
-            for i in range(pieces):
-                other(at, i).wait_recv()
-        else:
-            when(comes, lambda i, at=at: other(at, i).wait_recv())
+        comes = live & (cross == 1) & ((at < low) | (at < level) | (side == 1))
+        when(comes, lambda i: other(at, i).wait_recv())
+        blk = 2 * at + jnp.where(cross == 0, side, 1 - side)
+        needed = line_in | comes
+
+        @pl.when(needed & (blk < place))
+        def _():
+            block(blk, False)
+
+        @pl.when(needed & (blk >= place))
+        def _():
+            block(blk, True)
+
+        return carry
+
+    lax.fori_loop(0, 2 * levels, event, 0)
+
+    for h in range(heads):
+        total = acc_ref[h, HD : HD + 1, :]
+        out = (acc_ref[h, :HD, :] / total).T
+        o_ref[:, h * HD : (h + 1) * HD] = out
+        ob_ref[:, h * HD : (h + 1) * HD] = out.astype(BF16)
+        lse_ref[h : h + 1, :] = m_ref[h : h + 1, :] * LOG2E + jnp.log2(total)
 
     when(to_up, lambda i: make(level, i, 0, kv_ref).wait_send())
     when(own_side, lambda i: make(level, i, 2, kv_ref).wait_send())
@@ -328,30 +420,50 @@
         when(at < low, lambda i, at=at: make(at, i, 2).wait_send())
 
 
-def kv_gather(kv, group, low, collective):
+def attention_forward(info, q, kv, group, low, collective):
     pieces = 4
     levels = group // 2
+    tokens, width = q.shape
+    heads = width // HD
     return pl.pallas_call(
-        functools.partial(kv_kernel, group, low, pieces),
-        out_shape=jax.ShapeDtypeStruct((group,) + kv.shape, kv.dtype),
-        in_specs=[VSPEC],
-        out_specs=VSPEC,
-        scratch_shapes=[DMA((levels, pieces))] * 6,
+        functools.partial(forward_kernel, group, low, pieces, tokens // 2),
+        out_shape=(
+            jax.ShapeDtypeStruct((group,) + kv.shape, kv.dtype),
+            jax.ShapeDtypeStruct((tokens, width), F32),
+            jax.ShapeDtypeStruct((tokens, width), BF16),
+            jax.ShapeDtypeStruct((8, tokens), F32),
+        ),
+        in_specs=[SSPEC, VSPEC, VSPEC],
+        out_specs=(VSPEC,) * 4,
+        scratch_shapes=[
+            pltpu.VMEM((8, tokens), F32),
+            pltpu.VMEM((heads, HD + 16, tokens), F32),
+        ]
+        + [DMA((levels, pieces))] * 6,
         compiler_params=params(collective),
-    )(kv)
-
-
-def dkv_kernel(
+    )(info, q, kv)
+
+
+def backward_kernel(
     group,
     low,
     pieces,
+    kb,
+    info_ref,
+    q_ref,
+    kv_ref,
+    do_ref,
+    lse_ref,
+    delta_ref,
+    dq_ref,
+    out_ref,
     part_ref,
-    out_ref,
     rx_ref,
     above_ref,
     below_ref,
     snd_ref,
     acc_ref,
+    dqt_ref,
     u_send,
     u_recv,
     d_send,
@@ -361,8 +473,33 @@
 ):
     levels = group // 2
     row, place, level, side, partner = line_places(group)
-    step = out_ref.shape[0] // pieces
+    prefix = info_ref[0]
+    tokens, width = q_ref.shape
+    heads = width // HD
+    step = tokens // pieces
     line_greet(levels, row, level, partner)
+    dqt_ref[...] = jnp.zeros(dqt_ref.shape, F32)
+
+    def block(blk, masked):
+        def body(j, carry):
+            start = pl.multiple_of(j * kb, kb)
+            keys = pl.ds(start, kb)
+            for h in range(heads):
+                feats = slice(h * HD, (h + 1) * HD)
+                vals = slice(width + h * HD, width + (h + 1) * HD)
+                k, v = kv_ref[blk, keys, feats], kv_ref[blk, keys, vals]
+                q, do = q_ref[:, feats], do_ref[:, feats]
+                probs = jnp.exp2(nt(k, q) * LOG2E - lse_ref[h : h + 1, :])
+                if masked:
+                    allowed = seen(blk * tokens + start, place * tokens, probs.shape, prefix)
+                    probs = jnp.where(allowed, probs, 0.0)
+                grad = (probs * (nt(v, do) - delta_ref[h : h + 1, :])).astype(BF16)
+                part_ref[blk, keys, feats] = nn(grad, q).astype(BF16)
+                part_ref[blk, keys, vals] = nn(probs.astype(BF16), do).astype(BF16)
+                dqt_ref[feats, :] += nn(k.T, grad)
+            return carry
+
+        lax.fori_loop(0, tokens // kb, body, 0)
 
     def cross(at, i):
         part = pl.ds(i * step, step)
@@ -391,13 +528,6 @@
     def comes(at):
         return (at < low) | (at < level) | ((at == level) & (side == 0))
 
-    for at in range(levels):
-        for i in range(pieces):
-
-            @pl.when(gone(at))
-            def _(at=at, i=i):
-                cross(at, i).start()
-
     def total(at, i, from_above, from_below):
         part = pl.ds(i * step, step)
         acc_ref[...] = part_ref[2 * at + side, part].astype(F32)
@@ -407,34 +537,69 @@
             cross(at, i).wait_recv()
             acc_ref[...] += rx_ref[at, part].astype(F32)
 
-        @pl.when(from_above)
+        if from_above is not None:
+
+            @pl.when(from_above)
+            def _():
+                line(at, i, False).wait_recv()
+                acc_ref[...] += above_ref[at, part].astype(F32)
+
+        if from_below is not None:
+
+            @pl.when(from_below)
+            def _():
+                line(at, i, True).wait_recv()
+                acc_ref[...] += below_ref[at, part].astype(F32)
+
+    not_top = level < levels - 1
+    above = jnp.maximum(low - 1 - level, 0)
+
+    def level_of(t):
+        return jnp.where(t < above, low - 1 - t, t - above)
+
+    def event(e, carry):
+        t, own = e // 2, e % 2
+        at = level_of(t)
+        live = (t < above) | (at <= level)
+
+        down = t - (levels - level)
+
+        @pl.when((own == 1) & (down >= 0) & (down < level))
         def _():
-            line(at, i, False).wait_recv()
-            acc_ref[...] += above_ref[at, part].astype(F32)
-
-        @pl.when(from_below)
+            for i in range(pieces):
+                total(down, i, not_top, None)
+                snd_ref[down, pl.ds(i * step, step)] = acc_ref[...].astype(BF16)
+                line(down, i, False).start()
+
+        @pl.when((own == 1) & (t >= 1) & (t - 1 < above))
         def _():
-            line(at, i, True).wait_recv()
-            acc_ref[...] += below_ref[at, part].astype(F32)
-
-    not_top = level < levels - 1
-    for at in range(levels - 1):
-        for i in range(pieces):
-
-            @pl.when(at < level)
-            def _(at=at, i=i):
-                total(at, i, not_top, jnp.bool_(False) if at >= low else jnp.bool_(False))
-                snd_ref[at, pl.ds(i * step, step)] = acc_ref[...].astype(BF16)
-                line(at, i, False).start()
-
-    for at in range(low - 1, 0, -1):
-        for i in range(pieces):
-
-            @pl.when(at > level)
-            def _(at=at, i=i):
-                total(at, i, jnp.bool_(False), level > 0)
-                snd_ref[at, pl.ds(i * step, step)] = acc_ref[...].astype(BF16)
-                line(at, i, True).start()
+            up = level_of(t - 1)
+            for i in range(pieces):
+                total(up, i, None, level > 0)
+                snd_ref[up, pl.ds(i * step, step)] = acc_ref[...].astype(BF16)
+                line(up, i, True).start()
+
+        goes = live & (own == 0) & gone(at)
+        blk = 2 * at + jnp.where(own == 1, side, 1 - side)
+        needed = goes | (live & (own == 1))
+
+        @pl.when(needed & (blk < place))
+        def _():
+            block(blk, False)
+
+        @pl.when(needed & (blk >= place))
+        def _():
+            block(blk, True)
+
+        @pl.when(goes)
+        def _():
+            for i in range(pieces):
+                cross(at, i).start()
+
+        return carry
+
+    lax.fori_loop(0, 2 * levels, event, 0)
+    dq_ref[...] = (dqt_ref[...] * HD**-0.5).T.astype(BF16)
 
     for i in range(pieces):
         total(level, i, not_top, (level > 0) & (level < low))
@@ -458,26 +623,32 @@
                     line(at, i, True).wait_send()
 
 
-def dkv_scatter(parts, group, low, collective):
+def attention_backward(info, q, kv_all, do, lse, delta, group, low, collective):
     pieces = 4
     levels = group // 2
-    _, tokens, width = parts.shape
-    block = pltpu.VMEM((levels, tokens, width), BF16)
+    tokens, width = q.shape
+    both = 2 * width
+    block = pltpu.VMEM((levels, tokens, both), BF16)
     return pl.pallas_call(
-        functools.partial(dkv_kernel, group, low, pieces),
-        out_shape=jax.ShapeDtypeStruct((tokens, width), BF16),
-        in_specs=[VSPEC],
-        out_specs=VSPEC,
+        functools.partial(backward_kernel, group, low, pieces, tokens // 2),
+        out_shape=(
+            jax.ShapeDtypeStruct((tokens, width), BF16),
+            jax.ShapeDtypeStruct((tokens, both), BF16),
+        ),
+        in_specs=[SSPEC] + [VSPEC] * 5,
+        out_specs=(VSPEC,) * 2,
         scratch_shapes=[
+            pltpu.VMEM(kv_all.shape, BF16),
             block,
             block,
-            pltpu.VMEM((low, tokens, width), BF16),
+            pltpu.VMEM((low, tokens, both), BF16),
             block,
-            pltpu.VMEM((tokens // pieces, width), F32),
+            pltpu.VMEM((tokens // pieces, both), F32),
+            pltpu.VMEM((width, tokens), F32),
         ]
         + [DMA((levels, pieces))] * 6,
         compiler_params=params(collective),
-    )(parts)
+    )(info, q, kv_all, do, lse, delta)
 
 
 def product_kernel(pieces, a_ref, b_ref, out_ref, snd_ref, rx_ref, far_ref, tot_ref, send, recv):
@@ -716,150 +887,6 @@
         ],
         compiler_params=params(collective),
     )(w, s)
-
-
-def nt(left, right):
-    return lax.dot_general(left, right, (((1,), (1,)), ((), ())), preferred_element_type=F32)
-
-
-def nn(left, right):
-    return lax.dot_general(left, right, (((1,), (0,)), ((), ())), preferred_element_type=F32)
-
-
-def tn(left, right):
-    return lax.dot_general(left, right, (((0,), (0,)), ((), ())), preferred_element_type=F32)
-
-
-def seen(key_start, query_start, shape, prefix):
-    key = key_start + lax.broadcasted_iota(jnp.int32, shape, 0)
-    query = query_start + lax.broadcasted_iota(jnp.int32, shape, 1)
-    return (key < prefix) | (key <= query)
-
-
-def forward_kernel(
-    low_blocks, kb, qb, info_ref, q_ref, kv_ref, o_ref, ob_ref, lse_ref, m_ref, acc_ref
-):
-    place, prefix = info_ref[0], info_ref[1]
-    tokens, width = q_ref.shape
-    heads = width // HD
-    per = tokens // kb
-    ext = HD + 16
-    m_ref[...] = jnp.full(m_ref.shape, neg_big, F32)
-    acc_ref[...] = jnp.zeros(acc_ref.shape, F32)
-
-    def block(j, masked):
-        blk = j // per
-        start = pl.multiple_of((j % per) * kb, kb)
-        rows = kv_ref[blk, pl.ds(start, kb), :]
-        for h in range(heads):
-            k = rows[:, h * HD : (h + 1) * HD]
-            v = rows[:, width + h * HD : width + (h + 1) * HD]
-            v_ext = jnp.concatenate([v.T, jnp.ones((16, kb), BF16)], axis=0)
-            for i in range(tokens // qb):
-                cols = slice(i * qb, (i + 1) * qb)
-                raw = nt(k, q_ref[cols, h * HD : (h + 1) * HD]) * LOG2E
-                if masked:
-                    allowed = seen(j * kb, place * tokens + i * qb, raw.shape, prefix)
-                    raw = jnp.where(allowed, raw, neg_big)
-                old = m_ref[h : h + 1, cols]
-                new = jnp.maximum(old, jnp.max(raw, axis=0, keepdims=True))
-                m_ref[h : h + 1, cols] = new
-                weights = jnp.exp2(raw - new).astype(BF16)
-                acc_ref[h, :, cols] = acc_ref[h, :, cols] * jnp.exp2(old - new) + nn(
-                    v_ext, weights
-                )
-
-    def run(masked):
-        def body(j, carry):
-            block(j, masked)
-            return carry
-
-        return body
-
-    lax.fori_loop(0, place * per, run(False), 0)
-    lax.fori_loop(place * per, jnp.maximum(place + 1, low_blocks) * per, run(True), 0)
-    for h in range(heads):
-        total = acc_ref[h, HD : HD + 1, :]
-        out = (acc_ref[h, :HD, :] / total).T
-        o_ref[:, h * HD : (h + 1) * HD] = out
-        ob_ref[:, h * HD : (h + 1) * HD] = out.astype(BF16)
-        lse_ref[h : h + 1, :] = m_ref[h : h + 1, :] + jnp.log2(total)
-
-
-def attention_forward(info, q, kv_all, low_blocks):
-    tokens, width = q.shape
-    heads = width // HD
-    return pl.pallas_call(
-        functools.partial(forward_kernel, low_blocks, 512, 512),
-        out_shape=(
-            jax.ShapeDtypeStruct((tokens, width), F32),
-            jax.ShapeDtypeStruct((tokens, width), BF16),
-            jax.ShapeDtypeStruct((8, tokens), F32),
-        ),
-        in_specs=[SSPEC, VSPEC, VSPEC],
-        out_specs=(VSPEC,) * 3,
-        scratch_shapes=[
-            pltpu.VMEM((8, tokens), F32),
-            pltpu.VMEM((heads, HD + 16, tokens), F32),
-        ],
-        compiler_params=params(),
-    )(info, q, kv_all)
-
-
-def backward_kernel(
-    low_blocks, kb, info_ref, q_ref, kv_ref, do_ref, lse_ref, delta_ref, dq_ref, dkv_ref, dqt_ref
-):
-    place, prefix = info_ref[0], info_ref[1]
-    tokens, width = q_ref.shape
-    heads = width // HD
-    per = tokens // kb
-    dqt_ref[...] = jnp.zeros(dqt_ref.shape, F32)
-
-    def block(j, masked):
-        blk = j // per
-        start = pl.multiple_of((j % per) * kb, kb)
-        rows = kv_ref[blk, pl.ds(start, kb), :]
-        for h in range(heads):
-            feats = slice(h * HD, (h + 1) * HD)
-            k = rows[:, feats]
-            v = rows[:, width + h * HD : width + (h + 1) * HD]
-            q, do = q_ref[:, feats], do_ref[:, feats]
-            probs = jnp.exp2(nt(k, q) * LOG2E - lse_ref[h : h + 1, :])
-            if masked:
-                allowed = seen(j * kb, place * tokens, probs.shape, prefix)
-                probs = jnp.where(allowed, probs, 0.0)
-            grad = (probs * (nt(v, do) - delta_ref[h : h + 1, :])).astype(BF16)
-            dkv_ref[blk, pl.ds(start, kb), feats] = nn(grad, q).astype(BF16)
-            dkv_ref[blk, pl.ds(start, kb), width + h * HD : width + (h + 1) * HD] = nn(
-                probs.astype(BF16), do
-            ).astype(BF16)
-            dqt_ref[feats, :] += nn(k.T, grad)
-
-    def run(masked):
-        def body(j, carry):
-            block(j, masked)
-            return carry
-
-        return body
-
-    lax.fori_loop(0, place * per, run(False), 0)
-    lax.fori_loop(place * per, jnp.maximum(place + 1, low_blocks) * per, run(True), 0)
-    dq_ref[...] = (dqt_ref[...] * HD**-0.5).T.astype(BF16)
-
-
-def attention_backward(info, q, kv_all, do, lse, delta, low_blocks):
-    tokens, width = q.shape
-    return pl.pallas_call(
-        functools.partial(backward_kernel, low_blocks, 256),
-        out_shape=(
-            jax.ShapeDtypeStruct((tokens, width), BF16),
-            jax.ShapeDtypeStruct(kv_all.shape, BF16),
-        ),
-        in_specs=[SSPEC] + [VSPEC] * 5,
-        out_specs=(VSPEC,) * 2,
-        scratch_shapes=[pltpu.VMEM((width, tokens), F32)],
-        compiler_params=params(),
-    )(info, q, kv_all, do, lse, delta)
 
 
 def expert_kernel(
@@ -1016,12 +1043,12 @@
     qkv_bias = jnp.concatenate([query_bias, jnp.zeros_like(query_bias), value_bias])
     qkv = (jnp.dot(h_one, w_qkv, preferred_element_type=F32) + qkv_bias).astype(BF16)
     queries = qkv[:, :width] * jnp.asarray(HD**-0.5, BF16)
-    kv_all = kv_gather(qkv[:, width:], group, low, 1)
-    place = row % group
     seq_hit = row // group == jnp.arange(prefix_len.shape[0], dtype=jnp.int32)
     prefix = jnp.sum(jnp.where(seq_hit, prefix_len, 0))
-    info = jnp.stack([place.astype(jnp.int32), prefix.astype(jnp.int32)])
-    attended, attended_low, lse = attention_forward(info, queries, kv_all, 2 * low)
+    info = prefix.astype(jnp.int32).reshape(1)
+    kv_all, attended, attended_low, lse = attention_forward(
+        info, queries, qkv[:, width:], group, low, 1
+    )
     branch = product_scatter(attended_low, w_out, 2)
     x_own = layer_in.astype(F32)
     mid = x_own + branch + own(out_bias)
@@ -1073,10 +1100,9 @@
         (grad_attended.astype(F32) * attended).reshape(tokens, heads, HD), axis=-1
     ).T
     delta = jnp.pad(delta, ((0, 8 - heads), (0, 0)))
-    grad_q, kv_terms = attention_backward(
-        info, queries, kv_all, grad_attended, lse, delta, 2 * low
-    )
-    grad_kv = dkv_scatter(kv_terms, group, low, 8)
+    grad_q, grad_kv = attention_backward(
+        info, queries, kv_all, grad_attended, lse, delta, group, low, 8
+    )
     grad_qkv = jnp.concatenate([grad_q, grad_kv], axis=1)
     grad_w_qkv = lax.dot_general(
         h_one, grad_qkv, (((0,), (0,)), ((), ())), preferred_element_type=F32

time: 665 us -> 548 us (0.82)
  Pallas kernels: 565 us -> 447 us
    pallas_call x4 -> x2, Pallas kernels: 209 us -> 136 us  [the longest x1 82.9 us: attention_backward(): pl.pallas_call(functools.partial(backward_kernel, group, low, pieces, tok...]
    pallas_call x1, Pallas kernels: 111 us -> 87.3 us  [dispatch(): pl.pallas_call(functools.partial(dispatch_kernel, rows), out_shape=jax.Sh...]
    pallas_call x1, Pallas kernels: 54.1 us -> 33.5 us  [end_scatter(): pl.pallas_call(functools.partial(end_kernel, rows), out_shape=(jax.ShapeD...]
where the time goes in v2:
time: 548 us; the launch traced here: 542 us
  Pallas kernels  447 us (82%)
  local copies, waits for them, and re-layouts  40 us (7%)
  other arithmetic  33.7 us (6%)
  matrix products  19.2 us (4%)
    pallas_call x1, Pallas kernels, dispatch(): pl.pallas_call(functools.partial(dispatch_kernel, rows), out_shape=jax.Sh...  87.3 us
    pallas_call x1, Pallas kernels, attention_backward(): pl.pallas_call(functools.partial(backward_kernel, group, low, pieces, tok...  82.9 us
    pallas_call x1, Pallas kernels, giveback(): pl.pallas_call(functools.partial(giveback_kernel, rows), out_shape=jax.Sh...  62.9 us
    pallas_call x1, Pallas kernels, attention_forward(): pl.pallas_call(functools.partial(forward_kernel, group, low, pieces, toke...  53.5 us
    pallas_call x2, Pallas kernels, product_scatter(): pl.pallas_call(functools.partial(product_kernel, pieces), out_shape=jax.S...  37.4 us
    pallas_call x1, Pallas kernels, start_gather(): pl.pallas_call(functools.partial(start_kernel, rows, pieces), out_shape=(...  33.8 us
    pallas_call x1, Pallas kernels, end_scatter(): pl.pallas_call(functools.partial(end_kernel, rows), out_shape=(jax.ShapeD...  33.5 us
    pallas_call x1, Pallas kernels, experts(): pl.pallas_call(expert_kernel, grid=(count,), out_shape=(jax.ShapeDtypeStr...  23.1 us

profile of v2, /device:TPU:10, one launch (start us, length us, event | category | flops | bytes accessed | tf_op | source)
XLA Modules:
  0.0 542.0 jit_solution(10471719584366243960)
XLA Ops:
  0.7 0.8 convert_element_type.101
  1.5 0.8 convert_element_type.99
  2.2 0.7 bitcast_convert_fusion.2
  2.9 0.7 bitcast_convert_fusion.4
  3.6 0.7 bitcast_convert_fusion.6
  4.3 0.6 stack.102.s_ref
  4.9 2.0 copy.48.x_ref
  6.9 1.6 pad_maximum_fusion.2.w_ref
  8.5 33.8 %shard_map.323 = (bf16[4,1024,192]{2,1,0:T(8,128)(2,1)}, bf16[8,96,768]{2,1,0:T(8,128)(2,1)}, f32[8,8,128]{2,1,0:T(8,128)}) custom-call(bf16[1024,192]{1,0:T(8,128)(2,1)} %copy.48.x_ref, bf16[96,768]{1,0:T(8,128)(2,1)} %pad_maximum_fusion.2.w_ref, f32[8,128]{1,0:T(8,128)} %stack.102.s_ref), custom_call_target="tpu_custom_call" | custom-call | tf_op jit(solution)/shard_map/pallas_call | solution.py:116
  42.3 2.1 convert_reduce_fusion
  44.5 0.8 fusion.3
  45.5 2.4 convert_bitcast_fusion
  47.9 3.8 copy.50
  51.8 1.7 fusion.10
  53.9 3.1 add_convert_fusion
  57.0 0.9 slice_multiply_fusion.1.q_ref
  57.9 1.2 slice.171.kv_ref
  59.8 53.5 %shard_map.324 = (bf16[8,1024,384]{2,1,0:T(8,128)(2,1)}, f32[1024,192]{1,0:T(8,128)}, bf16[1024,192]{1,0:T(8,128)(2,1)}, f32[8,1024]{1,0:T(8,128)}) custom-call(s32[1]{0:T(128)S(6)} %select_n.24.info_ref, bf16[1024,192]{1,0:T(8,128)(2,1)} %slice_multiply_fusion.1.q_ref, bf16[1024,384]{1,0:T(8,128)(2,1)} %slice.171.kv_ref), custom_call_target="tpu_custom_call" | custom-call | tf_op jit(solution)/shard_map/pallas_call | solution.py:428
  113.3 1.9 slice.172
  115.2 18.3 %shard_map.325 = f32[1024,192]{1,0:T(8,128)} custom-call(bf16[1024,192]{1,0:T(8,128)(2,1)} %get-tuple-element.36.a_ref, bf16[4,192,192]{2,1,0:T(8,128)(2,1)} %bitcast.140), custom_call_target="tpu_custom_call" | custom-call | tf_op jit(solution)/shard_map/pallas_call | solution.py:707
  133.7 1.5 fusion.45
  135.6 0.6 reshape.221.x_ref
  136.2 5.0 shard_map.326
  141.2 0.8 reshape.222
  142.8 6.2 %gather_fusion = s32[1024]{0:T(1024)S(1)} fusion(s32[50304]{0:T(1024)S(1)} %copy-done, s32[1024]{0:T(1024)S(1)} %fusion.40), kind=kCustom, calls=%fused_computation | custom fusion | bytes 12288 | tf_op jit(solution)/shard_map/gather | solution.py:1026
  149.7 3.6 fusion.11
  153.2 87.3 %shard_map.327.x_ref = bf16[4,8,2,128,384]{4,3,2,1,0:T(8,128)(2,1)} custom-call(bf16[8,2,128,384]{3,2,1,0:T(8,128)(2,1)} %bitcast.141), custom_call_target="tpu_custom_call" | custom-call | tf_op jit(solution)/shard_map/pallas_call | solution.py:768
  241.2 23.1 %shard_map.328 = (bf16[4,8,2,128,384]{4,3,2,1,0:T(8,128)(2,1)}, f32[2,768,768]{2,1,0:T(8,128)}, f32[2,1,768]{2,1,0:T(1,128)}, f32[2,768,768]{2,1,0:T(8,128)}, f32[2,1,768]{2,1,0:T(1,128)}) custom-call(bf16[4,8,2,128,384]{4,3,2,1,0:T(8,128)(2,1)} %shard_map.327.x_ref, bf16[2,768,768]{2,1,0:T(8,128)(2,1)} %up_ref.1, bf16[2,1,768]{2,1,0:T(2,128)(2,1)} %copy.56.bias_ref, ...), custom_call_target="tpu_custom_call" | custom-call | tf_op jit(solution)/shard_map/pallas_call | solution.py:929
  264.3 0.8 constant_dynamic-slice_fusion
  265.6 62.9 %shard_map.329 = bf16[8,2,128,384]{3,2,1,0:T(8,128)(2,1)} custom-call(bf16[4,8,2,128,384]{4,3,2,1,0:T(8,128)(2,1)} %get-tuple-element.37.in_ref, f32[2,1,384]{2,1,0:T(1,128)} %reshape.248.bias_ref), custom_call_target="tpu_custom_call" | custom-call | tf_op jit(solution)/shard_map/pallas_call | solution.py:833
  328.5 4.9 fusion
  333.4 2.2 multiply_reduce_fusion
  335.6 0.6 reshape.226.x_ref
  336.2 5.0 shard_map.330
  341.3 0.8 reduce_sum.193
  342.0 3.0 fusion.44
  345.0 0.8 convert_element_type.113.x_ref
  345.9 17.5 %shard_map.331 = bf16[4,1024,192]{2,1,0:T(8,128)(2,1)} custom-call(bf16[1024,192]{1,0:T(8,128)(2,1)} %convert_element_type.113.x_ref), custom_call_target="tpu_custom_call" | custom-call | tf_op jit(solution)/shard_map/pallas_call | solution.py:173
  363.4 3.9 copy.60
  367.3 3.4 convert_multiply_fusion
  370.8 1.2 copy.62
  372.0 1.2 reduce_sum.194
  373.2 0.6 pad.58.delta_ref
  373.8 82.9 %shard_map.332 = (bf16[1024,192]{1,0:T(8,128)(2,1)}, bf16[1024,384]{1,0:T(8,128)(2,1)}) custom-call(s32[1]{0:T(128)S(6)} %select_n.24.info_ref, bf16[1024,192]{1,0:T(8,128)(2,1)} %slice_multiply_fusion.1.q_ref, bf16[8,1024,384]{2,1,0:T(8,128)(2,1)} %get-tuple-element.38.kv_ref, bf16[1024,192]{1,0:T(8,128)(2,1)} %get-tuple-element.126.do_ref, ...), custom_call_target="tpu_custom_call" | custom-call | tf_op jit(solution)/shard_map/pallas_call | solution.py:632
  456.7 1.9 convert_reduce_fusion.1
  458.9 2.9 pad_maximum_fusion.a_ref
  461.9 1.0 slice.169
  462.9 19.1 %shard_map.333 = f32[1024,192]{1,0:T(8,128)} custom-call(bf16[1024,576]{1,0:T(8,128)(2,1)} %pad_maximum_fusion.a_ref, bf16[4,192,576]{2,1,0:T(8,128)(2,1)} %bitcast.132), custom_call_target="tpu_custom_call" | custom-call | tf_op jit(solution)/shard_map/pallas_call | solution.py:707
  482.1 2.0 fusion.20
  484.1 0.6 pad_maximum_fusion.3.x_ref
  484.7 5.1 shard_map.334
  489.9 0.8 fusion.48
  490.9 0.7 fusion.31.s_ref
  491.6 3.1 convolution_convert_fusion
  495.3 1.2 pad_maximum_fusion.1.w_ref
  496.6 33.5 %shard_map.335 = (f32[96,768]{1,0:T(8,128)}, f32[8,128]{1,0:T(8,128)}) custom-call(bf16[8,96,768]{2,1,0:T(8,128)(2,1)} %pad_maximum_fusion.1.w_ref, f32[8,8,128]{2,1,0:T(8,128)} %fusion.31.s_ref), custom_call_target="tpu_custom_call" | custom-call | tf_op jit(solution)/shard_map/pallas_call | solution.py:874
  530.1 1.9 fusion.47
  532.0 0.8 slice_reduce_fusion.9
  532.7 0.7 reshape.238
  533.4 0.7 reshape.239
  534.1 1.4 slice_bitcast_fusion.4
  535.5 1.7 fusion.24
  537.2 2.5 copy.70
  539.6 0.9 copy.69
  (97 shorter events, 6.4 us)
Async XLA Ops:
  0.7 142.1 %copy-start = (s32[50304]{0:T(1024)S(1)}, s32[50304]{0:T(1024)}, u32[]{:S(2)}) copy-start(s32[50304]{0:T(1024)} %param.23) | copy-start | bytes 603652
  42.3 2.2 copy-start.2
  42.3 3.0 copy-start.12
  59.1 74.6 %copy-start.3 = (bf16[1024,192]{1,0:T(8,128)(2,1)S(1)}, bf16[1024,192]{1,0:T(8,128)(2,1)}, u32[]{:S(2)}) copy-start(bf16[1024,192]{1,0:T(8,128)(2,1)} %copy.48.x_ref) | copy-start | bytes 1179652
  135.2 7.6 %copy-start.15 = (s32[1024]{0:T(1024)S(1)}, s32[1024]{0:T(1024)}, u32[]{:S(2)}) copy-start(s32[1024]{0:T(1024)} %param.22) | copy-start | bytes 12292
  142.7 6.7 %copy-start.11 = (bf16[1024,192]{0,1:T(8,128)(2,1)S(1)}, bf16[1024,192]{0,1:T(8,128)(2,1)}, u32[]{:S(2)}) copy-start(bf16[1024,192]{0,1:T(8,128)(2,1)} %param.21) | copy-start | bytes 1179652
  149.6 3.6 copy-start.9
  153.2 87.3 %copy-start.16 = (bf16[2,768]{1,0:T(2,128)(2,1)S(1)}, bf16[2,768]{1,0:T(2,128)(2,1)}, u32[]{:S(2)}) copy-start(bf16[2,768]{1,0:T(2,128)(2,1)} %param.37) | copy-start | bytes 9220
  456.6 5.2 copy-start.7
  462.9 28.7 %copy-start.6 = (bf16[1024,384]{1,0:T(8,128)(2,1)S(1)}, bf16[1024,384]{1,0:T(8,128)(2,1)}, u32[]{:S(2)}) copy-start(bf16[1024,384]{1,0:T(8,128)(2,1)} %get-tuple-element.42) | copy-start | bytes 2359300
  491.6 3.1 copy-start.5
  491.6 3.2 copy-start.10
  495.3 40.2 %copy-start.4 = (f32[1024,192]{1,0:T(8,128)S(1)}, f32[1024,192]{1,0:T(8,128)}, u32[]{:S(2)}) copy-start(f32[1024,192]{1,0:T(8,128)} %shard_map.333) | copy-start | bytes 2359300
  535.5 6.3 %copy-start.1 = (s32[50304]{0:T(1024)S(1)}, s32[50304]{0:T(1024)}, u32[]{:S(2)}) copy-start(s32[50304]{0:T(1024)} %param.23) | copy-start | bytes 603652
  537.2 2.5 copy-start.8
  537.2 3.4 copy-start.14
  537.2 4.0 copy-start.13

commit v3 on v2

--- a/solution.py
+++ b/solution.py
@@ -62,14 +62,68 @@
     return me, sib, across, diag
 
 
+def line_places(group):
+    row = lax.axis_index("row")
+    place = row % group
+    level, side = place // 2, place % 2
+    return row, place, level, side, row + 1 - 2 * side
+
+
+def far_first(rows):
+    return sorted(range(1, rows), key=lambda k: -min(k, rows - k))
+
+
 def start_kernel(
-    rows, pieces, x_ref, w_ref, s_ref, xo_ref, wo_ref, so_ref, c_send, c_recv, r_send, r_recv
+    rows,
+    pieces,
+    x_ref,
+    g_ref,
+    w_ref,
+    s_ref,
+    xo_ref,
+    go_ref,
+    wo_ref,
+    so_ref,
+    c_send,
+    c_recv,
+    r_send,
+    r_recv,
+    l_send,
+    l_recv,
 ):
     me, sib, across, _ = col_places()
-    row = lax.axis_index("row")
-    peers = [{"row": (row + k) % rows} for k in range(1, rows)]
+    row, _, level, side, partner = line_places(rows)
+    levels = rows // 2
+    order = far_first(rows)
+    peers = [{"row": (row + k) % rows} for k in order]
     greet(peers + [{"col": sib}, {"col": across}])
     step = x_ref.shape[0] // pieces
+    to_up, to_down = level < levels - 1, level > 0
+
+    def weight(at, way, src=None):
+        dst = wo_ref.at[2 * at + side]
+        peer = (row + 2, row - 2, partner)[way]
+        return push(
+            dst if src is None else src,
+            dst,
+            l_send.at[way, at],
+            l_recv.at[way, at],
+            {"row": peer},
+        )
+
+    def weight_other(at):
+        dst = wo_ref.at[2 * at + 1 - side]
+        return push(dst, dst, l_send.at[2, at], l_recv.at[2, at], {"row": partner})
+
+    @pl.when(to_up)
+    def _():
+        weight(level, 0, w_ref).start()
+
+    @pl.when(to_down)
+    def _():
+        weight(level, 1, w_ref).start()
+
+    weight(level, 2, w_ref).start()
     sent = []
     for i in range(pieces):
         part = pl.ds(i * step, step)
@@ -85,51 +139,99 @@
             sent.append(copy)
     row_copies = []
     for k, peer in enumerate(peers):
-        for j, (src, dst) in enumerate(((w_ref, wo_ref), (s_ref, so_ref))):
+        target = (row + order[k]) % rows
+        for j, (src, dst) in enumerate(((s_ref, so_ref), (g_ref.at[target], go_ref))):
             copy = push(src, dst.at[row], r_send.at[j, k], r_recv.at[j, k], peer)
             copy.start()
             row_copies.append(copy)
     xo_ref[me] = x_ref[...]
     wo_ref[row] = w_ref[...]
     so_ref[row] = s_ref[...]
-    for i in range(pieces):
-        part = pl.ds(i * step, step)
-        sent[2 * i].wait_recv()
-        copy = push(
-            xo_ref.at[across, part],
-            xo_ref.at[across, part],
-            c_send.at[2, i],
-            c_recv.at[2, i],
-            {"col": sib},
-        )
-        copy.start()
-        row_copies.append(copy)
+    go_ref[row] = g_ref[row]
+
+    def pass_on(k):
+        at = level - k
+
+        @pl.when(at >= 0)
+        def _():
+            weight(at, 0).wait_recv()
+
+            @pl.when(to_up)
+            def _():
+                weight(at, 0).start()
+
+            weight(at, 2).start()
+
+        up = level + k
+
+        @pl.when(up < levels)
+        def _():
+            weight(up, 1).wait_recv()
+
+            @pl.when(to_down)
+            def _():
+                weight(up, 1).start()
+
+            weight(up, 2).start()
+
+    late = []
+    for k in range(1, max(levels, pieces + 1)):
+        if k < levels:
+            pass_on(k)
+        if k <= pieces:
+            part = pl.ds((k - 1) * step, step)
+            sent[2 * k - 2].wait_recv()
+            copy = push(
+                xo_ref.at[across, part],
+                xo_ref.at[across, part],
+                c_send.at[2, k - 1],
+                c_recv.at[2, k - 1],
+                {"col": sib},
+            )
+            copy.start()
+            late.append(copy)
     for i in range(pieces):
         sent[2 * i].wait_send()
         sent[2 * i + 1].wait()
+        late[i].wait()
+    for at in range(levels):
+        weight_other(at).wait_recv()
+        weight(at, 2).wait_send()
+
+        @pl.when((at <= level) & to_up)
+        def _(at=at):
+            weight(at, 0).wait_send()
+
+        @pl.when((at >= level) & to_down)
+        def _(at=at):
+            weight(at, 1).wait_send()
+
     for copy in row_copies:
         copy.wait()
 
 
-def start_gather(x, w, s, rows):
+def start_gather(x, g, w, s, rows):
     pieces = 4
     return pl.pallas_call(
         functools.partial(start_kernel, rows, pieces),
         out_shape=(
             jax.ShapeDtypeStruct((COLS,) + x.shape, x.dtype),
+            jax.ShapeDtypeStruct(g.shape, g.dtype),
             jax.ShapeDtypeStruct((rows,) + w.shape, w.dtype),
             jax.ShapeDtypeStruct((rows,) + s.shape, s.dtype),
         ),
-        in_specs=[VSPEC] * 3,
-        out_specs=(VSPEC,) * 3,
+        in_specs=[VSPEC] * 4,
+        out_specs=(VSPEC,) * 4,
         scratch_shapes=[
             DMA((3, pieces)),
             DMA((3, pieces)),
             DMA((2, rows - 1)),
             DMA((2, rows - 1)),
+            DMA((3, rows // 2)),
+            DMA((3, rows // 2)),
         ],
         compiler_params=params(0),
-    )(x, w, s)
+    )(x, g, w, s)
 
 
 def col_gather_kernel(pieces, x_ref, xo_ref, c_send, c_recv):
@@ -205,15 +307,12 @@
     )(x)
 
 
-def line_places(group):
-    row = lax.axis_index("row")
-    place = row % group
-    level, side = place // 2, place % 2
-    return row, place, level, side, row + 1 - 2 * side
-
-
 def line_greet(levels, row, level, partner):
     barrier = pltpu.get_barrier_semaphore()
+    me = lax.axis_index("col")
+    for k in range(1, COLS):
+        peer = {"col": (me + k) % COLS}
+        pl.semaphore_signal(barrier, inc=1, device_id=peer, device_id_type=MESH)
     pl.semaphore_signal(barrier, inc=1, device_id={"row": partner}, device_id_type=MESH)
 
     @pl.when(level > 0)
@@ -224,7 +323,7 @@
     def _():
         pl.semaphore_signal(barrier, inc=1, device_id={"row": row + 2}, device_id_type=MESH)
 
-    count = 1 + (level > 0).astype(jnp.int32) + (level < levels - 1).astype(jnp.int32)
+    count = COLS + (level > 0).astype(jnp.int32) + (level < levels - 1).astype(jnp.int32)
     pl.semaphore_wait(barrier, count)
 
 
@@ -254,10 +353,12 @@
     info_ref,
     q_ref,
     kv_ref,
+    g_ref,
     out_ref,
     o_ref,
     ob_ref,
     lse_ref,
+    ga_ref,
     m_ref,
     acc_ref,
     u_send,
@@ -266,6 +367,8 @@
     d_recv,
     x_send,
     x_recv,
+    g_send,
+    g_recv,
 ):
     levels = group // 2
     row, place, level, side, partner = line_places(group)
@@ -316,6 +419,14 @@
         def _(i=i):
             make(level, i, 1, kv_ref).start()
 
+    me = lax.axis_index("col")
+    wide = []
+    for k in range(1, COLS):
+        peer = {"col": (me + k) % COLS}
+        copy = push(g_ref, ga_ref.at[me], g_send.at[k - 1], g_recv.at[k - 1], peer)
+        copy.start()
+        wide.append(copy)
+    ga_ref[me] = g_ref[...]
     out_ref[place] = kv_ref[...]
     m_ref[...] = jnp.full(m_ref.shape, neg_big, F32)
     acc_ref[...] = jnp.zeros(acc_ref.shape, F32)
@@ -418,9 +529,11 @@
         at = level + k
         when((at < low) & (level > 0), lambda i, at=at: make(at, i, 1).wait_send())
         when(at < low, lambda i, at=at: make(at, i, 2).wait_send())
-
-
-def attention_forward(info, q, kv, group, low, collective):
+    for copy in wide:
+        copy.wait()
+
+
+def attention_forward(info, q, kv, g, group, low, collective):
     pieces = 4
     levels = group // 2
     tokens, width = q.shape
@@ -432,16 +545,18 @@
             jax.ShapeDtypeStruct((tokens, width), F32),
             jax.ShapeDtypeStruct((tokens, width), BF16),
             jax.ShapeDtypeStruct((8, tokens), F32),
+            jax.ShapeDtypeStruct((COLS,) + g.shape, g.dtype),
         ),
-        in_specs=[SSPEC, VSPEC, VSPEC],
-        out_specs=(VSPEC,) * 4,
+        in_specs=[SSPEC, VSPEC, VSPEC, VSPEC],
+        out_specs=(VSPEC,) * 5,
         scratch_shapes=[
             pltpu.VMEM((8, tokens), F32),
             pltpu.VMEM((heads, HD + 16, tokens), F32),
         ]
-        + [DMA((levels, pieces))] * 6,
+        + [DMA((levels, pieces))] * 6
+        + [DMA((COLS - 1,))] * 2,
         compiler_params=params(collective),
-    )(info, q, kv)
+    )(info, q, kv, g)
 
 
 def backward_kernel(
@@ -455,8 +570,11 @@
     do_ref,
     lse_ref,
     delta_ref,
+    e_ref,
+    bias_ref,
     dq_ref,
     out_ref,
+    eo_ref,
     part_ref,
     rx_ref,
     above_ref,
@@ -464,12 +582,15 @@
     snd_ref,
     acc_ref,
     dqt_ref,
+    er_ref,
     u_send,
     u_recv,
     d_send,
     d_recv,
     x_send,
     x_recv,
+    e_send,
+    e_recv,
 ):
     levels = group // 2
     row, place, level, side, partner = line_places(group)
@@ -478,6 +599,15 @@
     heads = width // HD
     step = tokens // pieces
     line_greet(levels, row, level, partner)
+    me = lax.axis_index("col")
+    terms = []
+    for k in range(1, COLS):
+        peer = (me + k) % COLS
+        copy = push(
+            e_ref.at[peer], er_ref.at[k - 1], e_send.at[k - 1], e_recv.at[k - 1], {"col": peer}
+        )
+        copy.start()
+        terms.append(copy)
     dqt_ref[...] = jnp.zeros(dqt_ref.shape, F32)
 
     def block(blk, masked):
@@ -599,6 +729,17 @@
         return carry
 
     lax.fori_loop(0, 2 * levels, event, 0)
+    for copy in terms:
+        copy.wait()
+
+    def finish(r, carry):
+        total = e_ref[me, r].astype(F32) + bias_ref[...]
+        for k in range(COLS - 1):
+            total = total + er_ref[k, r].astype(F32)
+        eo_ref[r] = total.astype(BF16)
+        return carry
+
+    lax.fori_loop(0, e_ref.shape[1], finish, 0)
     dq_ref[...] = (dqt_ref[...] * HD**-0.5).T.astype(BF16)
 
     for i in range(pieces):
@@ -623,7 +764,7 @@
                     line(at, i, True).wait_send()
 
 
-def attention_backward(info, q, kv_all, do, lse, delta, group, low, collective):
+def attention_backward(info, q, kv_all, do, lse, delta, e, bias, group, low, collective):
     pieces = 4
     levels = group // 2
     tokens, width = q.shape
@@ -634,9 +775,10 @@
         out_shape=(
             jax.ShapeDtypeStruct((tokens, width), BF16),
             jax.ShapeDtypeStruct((tokens, both), BF16),
+            jax.ShapeDtypeStruct(e.shape[1:], BF16),
         ),
-        in_specs=[SSPEC] + [VSPEC] * 5,
-        out_specs=(VSPEC,) * 2,
+        in_specs=[SSPEC] + [VSPEC] * 7,
+        out_specs=(VSPEC,) * 3,
         scratch_shapes=[
             pltpu.VMEM(kv_all.shape, BF16),
             block,
@@ -645,15 +787,32 @@
             block,
             pltpu.VMEM((tokens // pieces, both), F32),
             pltpu.VMEM((width, tokens), F32),
+            pltpu.VMEM((COLS - 1,) + e.shape[1:], BF16),
         ]
-        + [DMA((levels, pieces))] * 6,
+        + [DMA((levels, pieces))] * 6
+        + [DMA((COLS - 1,))] * 2,
         compiler_params=params(collective),
-    )(info, q, kv_all, do, lse, delta)
-
-
-def product_kernel(pieces, a_ref, b_ref, out_ref, snd_ref, rx_ref, far_ref, tot_ref, send, recv):
+    )(info, q, kv_all, do, lse, delta, e, bias)
+
+
+def product_kernel(pieces, rows, *refs):
+    if rows:
+        a_ref, b_ref, e_ref, out_ref, eo_ref = refs[:5]
+        snd_ref, rx_ref, far_ref, tot_ref, send, recv, e_send, e_recv = refs[5:]
+    else:
+        a_ref, b_ref, out_ref, snd_ref, rx_ref, far_ref, tot_ref, send, recv = refs
     me, sib, across, diag = col_places()
-    greet([{"col": sib}, {"col": across}])
+    row = lax.axis_index("row")
+    order = far_first(rows)
+    greet([{"row": (row + k) % rows} for k in order] + [{"col": sib}, {"col": across}])
+    home = []
+    for n, k in enumerate(order):
+        peer = (row + k) % rows
+        copy = push(e_ref.at[peer], eo_ref.at[row], e_send.at[n], e_recv.at[n], {"row": peer})
+        copy.start()
+        home.append(copy)
+    if rows:
+        eo_ref[row] = e_ref[row]
     step = a_ref.shape[0] // pieces
 
     def term(i, who):
@@ -697,27 +856,37 @@
         near(i, 0).wait_send()
         near(i, 1).wait_send()
         over(i).wait_send()
-
-
-def product_scatter(a, b, collective):
+    for copy in home:
+        copy.wait()
+
+
+def product_scatter(a, b, collective, back=None):
     pieces = 4
     tokens, width = a.shape[0], b.shape[1]
     block = pltpu.VMEM((tokens, width), BF16)
     pair = pltpu.VMEM((2, tokens, width), BF16)
+    out = jax.ShapeDtypeStruct((tokens, width), F32)
+    scratch = [pair, pair, block, block, DMA((3, pieces)), DMA((3, pieces))]
+    rows = 0
+    if back is not None:
+        rows = back.shape[0]
+        out = (out, jax.ShapeDtypeStruct(back.shape, back.dtype))
+        scratch = scratch + [DMA((rows - 1,))] * 2
     return pl.pallas_call(
-        functools.partial(product_kernel, pieces),
-        out_shape=jax.ShapeDtypeStruct((tokens, width), F32),
-        in_specs=[VSPEC] * 2,
-        out_specs=VSPEC,
-        scratch_shapes=[pair, pair, block, block, DMA((3, pieces)), DMA((3, pieces))],
+        functools.partial(product_kernel, pieces, rows),
+        out_shape=out,
+        in_specs=[VSPEC] * (3 if rows else 2),
+        out_specs=(VSPEC, VSPEC) if rows else VSPEC,
+        scratch_shapes=scratch,
         compiler_params=params(collective),
-    )(a, b)
+    )(*((a, b, back) if rows else (a, b)))
 
 
 def dispatch_kernel(rows, in_ref, out_ref, r_send, r_recv, c_send, c_recv):
     me, sib, across, _ = col_places()
     row = lax.axis_index("row")
-    peers = [(row + k) % rows for k in range(1, rows)]
+    order = far_first(rows)
+    peers = [(row + k) % rows for k in order]
     greet([{"row": p} for p in peers] + [{"col": sib}, {"col": across}])
     copies = []
     for k, peer in enumerate(peers):
@@ -738,7 +907,7 @@
         copy.start()
         (first if way == 0 else done).append(copy)
     out_ref[me, row] = in_ref[row]
-    sources = [row] + [(row + rows - k) % rows for k in range(1, rows)]
+    sources = [row] + [(row + rows - k) % rows for k in order]
 
     def forward(k):
         first[k].wait_recv()
@@ -776,11 +945,11 @@
 
 
 def giveback_kernel(
-    rows, in_ref, bias_ref, out_ref, rx_ref, far_ref, tot_ref, fin_ref, send, recv, r_send, r_recv
+    rows, in_ref, out_ref, rx_ref, far_ref, tot_ref, fin_ref, send, recv, r_send, r_recv
 ):
     me, sib, across, diag = col_places()
     row = lax.axis_index("row")
-    order = [(row + k) % rows for k in range(1, rows)] + [row]
+    order = [(row + k) % rows for k in far_first(rows)] + [row]
     greet([{"row": p} for p in order[:-1]] + [{"col": sib}, {"col": across}])
 
     def near(k, j):
@@ -805,7 +974,7 @@
         near(k, 1).wait_recv()
         over(k).wait_recv()
         total = in_ref[me, order[k]].astype(F32) + rx_ref[1, k].astype(F32)
-        total = total + far_ref[k].astype(F32) + bias_ref[...]
+        total = total + far_ref[k].astype(F32)
         if k == rows - 1:
             out_ref[row] = total.astype(BF16)
         else:
@@ -827,13 +996,13 @@
             home(k).wait()
 
 
-def giveback(parts, bias, rows, collective):
+def giveback(parts, rows, collective):
     block = parts.shape[2:]
     one = pltpu.VMEM((rows,) + block, BF16)
     return pl.pallas_call(
         functools.partial(giveback_kernel, rows),
         out_shape=jax.ShapeDtypeStruct((rows,) + block, BF16),
-        in_specs=[VSPEC] * 2,
+        in_specs=[VSPEC],
         out_specs=VSPEC,
         scratch_shapes=[
             pltpu.VMEM((2, rows) + block, BF16),
@@ -846,7 +1015,7 @@
             DMA((rows - 1,)),
         ],
         compiler_params=params(collective),
-    )(parts, bias)
+    )(parts)
 
 
 def end_kernel(rows, w_ref, s_ref, wo_ref, so_ref, wr_ref, sr_ref, send, recv):
@@ -890,14 +1059,22 @@
 
 
 def expert_kernel(
-    x_ref, up_ref, bias_ref, down_ref, part_ref, gup_ref, gbu_ref, gdown_ref, gbd_ref
+    x_ref,
+    g_ref,
+    up_ref,
+    bias_ref,
+    down_ref,
+    part_ref,
+    gx_ref,
+    gup_ref,
+    gbu_ref,
+    gdown_ref,
+    gbd_ref,
 ):
-    cols, rows, _, cap, both = x_ref.shape
-    width = both // 2
+    cols, rows, _, cap, width = x_ref.shape
     slots = rows * cap
-    blocks = [x_ref[b, :, 0].reshape(slots, both) for b in range(cols)]
-    x = jnp.concatenate([b[:, :width] for b in blocks], axis=1)
-    g = jnp.concatenate([b[:, width:] for b in blocks], axis=1)
+    x = jnp.concatenate([x_ref[b, :, 0].reshape(slots, width) for b in range(cols)], axis=1)
+    g = jnp.concatenate([g_ref[b, :, 0].reshape(slots, width) for b in range(cols)], axis=1)
     gbd_ref[...] = jnp.sum(g.astype(F32), axis=0).reshape(gbd_ref.shape)
     hidden_units = up_ref.shape[2]
     chunk = 256
@@ -919,17 +1096,19 @@
         gbu_ref[0, :, cut] = jnp.sum(grad.astype(F32), axis=0, keepdims=True)
     for b in range(cols):
         cut = slice(b * width, (b + 1) * width)
-        both_parts = jnp.concatenate([part[:, cut].astype(BF16), gx[:, cut].astype(BF16)], axis=1)
-        part_ref[b, :, 0] = both_parts.reshape(rows, cap, both)
-
-
-def experts(x, w_up, bias_up, w_down):
-    cols, rows, count, cap, both = x.shape
+        part_ref[b, :, 0] = part[:, cut].astype(BF16).reshape(rows, cap, width)
+        gx_ref[b, :, 0] = gx[:, cut].astype(BF16).reshape(rows, cap, width)
+
+
+def experts(x, g, w_up, bias_up, w_down):
+    cols, rows, count, cap, width = x.shape
+    slots = pl.BlockSpec((cols, rows, 1, cap, width), lambda e: (0, 0, e, 0, 0))
     _, features, hidden = w_up.shape
     return pl.pallas_call(
         expert_kernel,
         grid=(count,),
         out_shape=(
+            jax.ShapeDtypeStruct(x.shape, BF16),
             jax.ShapeDtypeStruct(x.shape, BF16),
             jax.ShapeDtypeStruct(w_up.shape, F32),
             jax.ShapeDtypeStruct((count, 1, hidden), F32),
@@ -937,20 +1116,22 @@
             jax.ShapeDtypeStruct((count, 1, features), F32),
         ),
         in_specs=[
-            pl.BlockSpec((cols, rows, 1, cap, both), lambda e: (0, 0, e, 0, 0)),
+            slots,
+            slots,
             pl.BlockSpec((1, features, hidden), lambda e: (e, 0, 0)),
             pl.BlockSpec((1, 1, hidden), lambda e: (e, 0, 0)),
             pl.BlockSpec((1, hidden, features), lambda e: (e, 0, 0)),
         ],
         out_specs=(
-            pl.BlockSpec((cols, rows, 1, cap, both), lambda e: (0, 0, e, 0, 0)),
+            slots,
+            slots,
             pl.BlockSpec((1, features, hidden), lambda e: (e, 0, 0)),
             pl.BlockSpec((1, 1, hidden), lambda e: (e, 0, 0)),
             pl.BlockSpec((1, hidden, features), lambda e: (e, 0, 0)),
             pl.BlockSpec((1, 1, features), lambda e: (e, 0, 0)),
         ),
         compiler_params=params(),
-    )(x, w_up, bias_up.reshape(count, 1, hidden), w_down)
+    )(x, g, w_up, bias_up.reshape(count, 1, hidden), w_down)
 
 
 def per_device(
@@ -1001,8 +1182,28 @@
             jnp.zeros((128,), F32),
         ]
     )
+    expert_total = EXP_DEV * rows
+    capacity = max(2, 2 * tokens // expert_total)
+    expert_of = hash_table[token_ids]
+    hits = expert_of[:, None] == jnp.arange(expert_total, dtype=jnp.int32)[None, :]
+    earlier = (
+        jnp.arange(tokens, dtype=jnp.int32)[None, :] < jnp.arange(tokens, dtype=jnp.int32)[:, None]
+    )
+    before = jnp.dot(earlier.astype(BF16), hits.astype(BF16), preferred_element_type=F32)
+    slot_of = jnp.sum(jnp.where(hits, before, 0.0), axis=1).astype(jnp.int32)
+    target = expert_of * capacity + slot_of
+    chosen = (
+        jnp.arange(expert_total * capacity, dtype=jnp.int32)[:, None] == target[None, :]
+    ).astype(BF16)
+
+    def place_rows(v):
+        v = jnp.dot(chosen, v, preferred_element_type=F32).astype(BF16)
+        return v.reshape(rows, EXP_DEV, capacity, width)
+
     weights = jnp.concatenate([w_query, w_key, w_value, w_output], axis=1)
-    x_all, w_all, s_all = start_gather(layer_in, weights, small, rows)
+    x_all, g_own, w_all, s_all = start_gather(
+        layer_in, place_rows(cotangent), weights, small, rows
+    )
     w_all = w_all.reshape(D, 4 * width)
     w_qkv = w_all[:, : 3 * width]
     w_out = w_all[:, 3 * width :].reshape(COLS, width, width)
@@ -1020,20 +1221,6 @@
         .reshape(width)
         for i in (5, 6)
     )
-
-    expert_total = EXP_DEV * rows
-    capacity = max(2, 2 * tokens // expert_total)
-    expert_of = hash_table[token_ids]
-    hits = expert_of[:, None] == jnp.arange(expert_total, dtype=jnp.int32)[None, :]
-    earlier = (
-        jnp.arange(tokens, dtype=jnp.int32)[None, :] < jnp.arange(tokens, dtype=jnp.int32)[:, None]
-    )
-    before = jnp.dot(earlier.astype(BF16), hits.astype(BF16), preferred_element_type=F32)
-    slot_of = jnp.sum(jnp.where(hits, before, 0.0), axis=1).astype(jnp.int32)
-    target = expert_of * capacity + slot_of
-    chosen = (
-        jnp.arange(expert_total * capacity, dtype=jnp.int32)[:, None] == target[None, :]
-    ).astype(BF16)
 
     resid = x_all.transpose(1, 0, 2).reshape(tokens, D).astype(F32)
     mean_one = jnp.mean(resid, axis=-1, keepdims=True)
@@ -1046,8 +1233,8 @@
     seq_hit = row // group == jnp.arange(prefix_len.shape[0], dtype=jnp.int32)
     prefix = jnp.sum(jnp.where(seq_hit, prefix_len, 0))
     info = prefix.astype(jnp.int32).reshape(1)
-    kv_all, attended, attended_low, lse = attention_forward(
-        info, queries, qkv[:, width:], group, low, 1
+    kv_all, attended, attended_low, lse, g_all = attention_forward(
+        info, queries, qkv[:, width:], g_own, group, low, 1
     )
     branch = product_scatter(attended_low, w_out, 2)
     x_own = layer_in.astype(F32)
@@ -1064,22 +1251,11 @@
     gain_two_own = own(gain_two)
     h_two = (normed_two * gain_two_own + own(shift_two)).astype(BF16)
 
-    outgoing = jnp.dot(
-        chosen, jnp.concatenate([h_two, cotangent], axis=1), preferred_element_type=F32
-    ).astype(BF16)
-    block = (rows, EXP_DEV, capacity, 2 * width)
-    received = dispatch(outgoing.reshape(block), rows, 4)
-    parts, grad_w_up, grad_bias_up, grad_w_down, grad_bias_down = experts(
-        received, w_up, bias_up, w_down
-    )
-    down_own = lax.dynamic_slice_in_dim(bias_down, col * width, width, 1).astype(F32)
-    down_own = jnp.concatenate([down_own, jnp.zeros_like(down_own)], axis=1)[:, None, :]
-    returned = giveback(parts, down_own, rows, 5).reshape(-1, 2 * width)
-    combined = lax.dot_general(
-        chosen, returned, (((0,), (0,)), ((), ())), preferred_element_type=F32
-    )
-    layer_out = (mid + combined[:, :width]).astype(BF16)
-    grad_h_two = combined[:, width:]
+    received = dispatch(place_rows(h_two), rows, 4)
+    parts, grad_parts, grad_w_up, grad_bias_up, grad_w_down, grad_bias_down = experts(
+        received, g_all, w_up, bias_up, w_down
+    )
+    grad_h_two = tn(chosen, giveback(grad_parts, rows, 5).reshape(-1, width))
 
     scaled = grad_h_two * gain_two_own
     sums = jnp.stack([jnp.sum(scaled, axis=-1), jnp.sum(scaled * normed_two, axis=-1)])
@@ -1100,15 +1276,27 @@
         (grad_attended.astype(F32) * attended).reshape(tokens, heads, HD), axis=-1
     ).T
     delta = jnp.pad(delta, ((0, 8 - heads), (0, 0)))
-    grad_q, grad_kv = attention_backward(
-        info, queries, kv_all, grad_attended, lse, delta, group, low, 8
+    down_own = lax.dynamic_slice_in_dim(bias_down, col * width, width, 1).astype(F32)
+    grad_q, grad_kv, outs = attention_backward(
+        info,
+        queries,
+        kv_all,
+        grad_attended,
+        lse,
+        delta,
+        parts,
+        down_own[:, None, :],
+        group,
+        low,
+        8,
     )
     grad_qkv = jnp.concatenate([grad_q, grad_kv], axis=1)
     grad_w_qkv = lax.dot_general(
         h_one, grad_qkv, (((0,), (0,)), ((), ())), preferred_element_type=F32
     )
     grad_bias = jnp.sum(grad_qkv, axis=0, dtype=F32)
-    grad_h_one = product_scatter(grad_qkv, w_qkv.reshape(COLS, width, 3 * width), 9)
+    grad_h_one, outs = product_scatter(grad_qkv, w_qkv.reshape(COLS, width, 3 * width), 9, outs)
+    layer_out = (mid + tn(chosen, outs.reshape(-1, width))).astype(BF16)
     normed_one = (x_own - mean_one) * rstd_one
     scaled = grad_h_one * own(gain_one)
     sums = jnp.stack([jnp.sum(scaled, axis=-1), jnp.sum(scaled * normed_one, axis=-1)])

time: 548 us -> 555 us (1.013)
    pallas_call x1, Pallas kernels: 62.9 us -> 39.8 us  [giveback(): pl.pallas_call(functools.partial(giveback_kernel, rows), out_shape=jax.Sh...]
    pallas_call x2, Pallas kernels: 37.4 us -> 50.8 us  [product_scatter(): pl.pallas_call(functools.partial(product_kernel, pieces, rows), out_shape...]
    pallas_call x1, Pallas kernels: 33.8 us -> 41.9 us  [start_gather(): pl.pallas_call(functools.partial(start_kernel, rows, pieces), out_shape=(...]
    dot_general x2 -> x4, matrix products: 8.49 us -> 11.6 us  [the longest x2 7.51 us: tn(): lax.dot_general(left, right, (((0,), (0,)), ((), ())), preferred_element_...]
where the time goes in v3:
time: 555 us; the launch traced here: 547 us
  Pallas kernels  445 us (80%)
  local copies, waits for them, and re-layouts  45 us (8%)
  other arithmetic  32.3 us (6%)
  matrix products  22.3 us (4%)
    pallas_call x1, Pallas kernels, dispatch(): pl.pallas_call(functools.partial(dispatch_kernel, rows), out_shape=jax.Sh...  85.5 us
    pallas_call x1, Pallas kernels, attention_backward(): pl.pallas_call(functools.partial(backward_kernel, group, low, pieces, tok...  84.1 us
    pallas_call x1, Pallas kernels, attention_forward(): pl.pallas_call(functools.partial(forward_kernel, group, low, pieces, toke...  54.5 us
    pallas_call x2, Pallas kernels, product_scatter(): pl.pallas_call(functools.partial(product_kernel, pieces, rows), out_shape...  50.8 us
    pallas_call x1, Pallas kernels, start_gather(): pl.pallas_call(functools.partial(start_kernel, rows, pieces), out_shape=(...  41.9 us
    pallas_call x1, Pallas kernels, giveback(): pl.pallas_call(functools.partial(giveback_kernel, rows), out_shape=jax.Sh...  39.8 us
    pallas_call x1, Pallas kernels, end_scatter(): pl.pallas_call(functools.partial(end_kernel, rows), out_shape=(jax.ShapeD...  31.9 us
    pallas_call x1, Pallas kernels, experts(): pl.pallas_call(expert_kernel, grid=(count,), out_shape=(jax.ShapeDtypeStr...  23.2 us

profile of v3, /device:TPU:10, one launch (start us, length us, event | category | flops | bytes accessed | tf_op | source)
XLA Modules:
  0.0 546.9 jit_solution(8996129088798250227)
XLA Ops:
  0.7 0.8 convert_element_type.104
  1.5 0.8 convert_element_type.106
  2.2 0.7 bitcast_convert_fusion.2
  2.9 0.7 bitcast_convert_fusion.4
  4.9 0.7 fusion.45
  5.6 6.2 %gather_fusion = s32[1024]{0:T(1024)S(1)} fusion(s32[50304]{0:T(1024)S(1)} %copy-done, s32[1024]{0:T(1024)S(1)} %fusion.45), kind=kCustom, calls=%fused_computation | custom fusion | bytes 12288 | tf_op jit(solution)/shard_map/gather | solution.py:1187
  12.3 1.9 fusion.15
  14.2 1.3 copy.51
  15.5 1.0 copy.50.x_ref
  16.6 0.8 pad_maximum_fusion.2.w_ref
  17.3 41.9 %shard_map.323 = (bf16[4,1024,192]{2,1,0:T(8,128)(2,1)}, bf16[8,2,128,192]{3,2,1,0:T(8,128)(2,1)}, bf16[8,96,768]{2,1,0:T(8,128)(2,1)}, f32[8,8,128]{2,1,0:T(8,128)}) custom-call(bf16[1024,192]{1,0:T(8,128)(2,1)} %copy.50.x_ref, bf16[8,2,128,192]{3,2,1,0:T(8,128)(2,1)} %bitcast.137, bf16[96,768]{1,0:T(8,128)(2,1)} %pad_maximum_fusion.2.w_ref, ...), custom_call_target="tpu_custom_call" | custom-call | tf_op jit(solution)/shard_map/pallas_call | solution.py:215
  59.2 2.1 convert_reduce_fusion
  61.4 0.8 fusion.5
  62.4 2.4 convert_bitcast_fusion
  64.8 3.8 copy.53
  68.7 1.6 fusion.14
  70.8 3.1 add_convert_fusion
  73.9 0.9 slice_multiply_fusion.q_ref
  74.8 1.2 slice.163.kv_ref
  76.7 54.5 %shard_map.324 = (bf16[8,1024,384]{2,1,0:T(8,128)(2,1)}, f32[1024,192]{1,0:T(8,128)}, bf16[1024,192]{1,0:T(8,128)(2,1)}, f32[8,1024]{1,0:T(8,128)}, bf16[4,8,2,128,192]{4,3,2,1,0:T(8,128)(2,1)}) custom-call(s32[1]{0:T(128)S(6)} %select_n.24.info_ref, bf16[1024,192]{1,0:T(8,128)(2,1)} %slice_multiply_fusion.q_ref, bf16[1024,384]{1,0:T(8,128)(2,1)} %slice.163.kv_ref, ...), custom_call_target="tpu_custom_call" | custom-call | tf_op jit(solution)/shard_map/pallas_call | solution.py:541
  131.2 1.9 slice.164
  133.1 19.2 %shard_map.325 = f32[1024,192]{1,0:T(8,128)} custom-call(bf16[1024,192]{1,0:T(8,128)(2,1)} %get-tuple-element.43.refs_0_, bf16[4,192,192]{2,1,0:T(8,128)(2,1)} %bitcast.145), custom_call_target="tpu_custom_call" | custom-call | tf_op jit(solution)/shard_map/pallas_call | solution.py:875
  152.5 1.5 fusion.49
  154.9 5.0 shard_map.326
  159.9 0.8 reshape.229
  161.1 2.1 fusion.16
  163.3 1.3 copy.59
  164.6 85.5 %shard_map.327.x_ref = bf16[4,8,2,128,192]{4,3,2,1,0:T(8,128)(2,1)} custom-call(bf16[8,2,128,192]{3,2,1,0:T(8,128)(2,1)} %bitcast.136), custom_call_target="tpu_custom_call" | custom-call | tf_op jit(solution)/shard_map/pallas_call | solution.py:937
  250.7 23.2 %shard_map.328 = (bf16[4,8,2,128,192]{4,3,2,1,0:T(8,128)(2,1)}, bf16[4,8,2,128,192]{4,3,2,1,0:T(8,128)(2,1)}, f32[2,768,768]{2,1,0:T(8,128)}, f32[2,1,768]{2,1,0...) custom-call(bf16[4,8,2,128,192]{4,3,2,1,0:T(8,128)(2,1)} %shard_map.327.x_ref, ...), custom_call_target="tpu_custom_call" | custom-call | tf_op jit(solution)/shard_map/pallas_call | solution.py:1107
  274.0 39.8 %shard_map.329 = bf16[8,2,128,192]{3,2,1,0:T(8,128)(2,1)} custom-call(bf16[4,8,2,128,192]{4,3,2,1,0:T(8,128)(2,1)} %get-tuple-element.46.in_ref), custom_call_target="tpu_custom_call" | custom-call | tf_op jit(solution)/shard_map/pallas_call | solution.py:1002
  313.7 3.9 fusion.55
  317.6 1.5 copy.61
  320.4 5.2 shard_map.330
  325.6 0.8 reduce_sum.193
  326.4 2.0 copy.57
  328.4 1.9 fusion.48
  330.3 1.0 copy-done.4
  331.3 0.8 convert_element_type.116.x_ref
  332.2 18.1 %shard_map.331 = bf16[4,1024,192]{2,1,0:T(8,128)(2,1)} custom-call(bf16[1024,192]{1,0:T(8,128)(2,1)} %convert_element_type.116.x_ref), custom_call_target="tpu_custom_call" | custom-call | tf_op jit(solution)/shard_map/pallas_call | solution.py:275
  350.3 3.9 copy.62
  354.2 3.4 convert_multiply_fusion
  357.7 1.2 copy.64
  358.9 1.2 reduce_sum.194
  360.7 0.8 dynamic-slice_convert_fusion
  362.0 84.1 %shard_map.332 = (bf16[1024,192]{1,0:T(8,128)(2,1)}, bf16[1024,384]{1,0:T(8,128)(2,1)}, bf16[8,2,128,192]{3,2,1,0:T(8,128)(2,1)}) custom-call(s32[1]{0:T(128)S(6)} %select_n.24.info_ref, bf16[1024,192]{1,0:T(8,128)(2,1)} %slice_multiply_fusion.q_ref, bf16[8,1024,384]{2,1,0:T(8,128)(2,1)} %get-tuple-element.44.kv_ref, ...), custom_call_target="tpu_custom_call" | custom-call | tf_op jit(solution)/shard_map/pallas_call | solution.py:773
  446.1 1.9 convert_reduce_fusion.1
  448.4 2.9 pad_maximum_fusion.refs_0_
  451.3 1.0 slice.161
  452.4 31.6 %shard_map.333 = (f32[1024,192]{1,0:T(8,128)}, bf16[8,2,128,192]{3,2,1,0:T(8,128)(2,1)}) custom-call(bf16[1024,576]{1,0:T(8,128)(2,1)} %pad_maximum_fusion.refs_0_, bf16[4,192,576]{2,1,0:T(8,128)(2,1)} %bitcast.138, bf16[8,2,128,192]{3,2,1,0:T(8,128)(2,1)} %get-tuple-element.52.refs_2_), custom_call_target="tpu_custom_call" | custom-call | tf_op jit(solution)/shard_map/pallas_call | solution.py:875
  484.0 2.0 fusion.27
  486.7 5.1 shard_map.334
  491.8 0.8 fusion.52
  492.8 0.7 fusion.37.s_ref
  493.5 3.1 convolution_convert_fusion
  497.2 1.2 pad_maximum_fusion.1.w_ref
  498.5 31.9 %shard_map.335 = (f32[96,768]{1,0:T(8,128)}, f32[8,128]{1,0:T(8,128)}) custom-call(bf16[8,96,768]{2,1,0:T(8,128)(2,1)} %pad_maximum_fusion.1.w_ref, f32[8,8,128]{2,1,0:T(8,128)} %fusion.37.s_ref), custom_call_target="tpu_custom_call" | custom-call | tf_op jit(solution)/shard_map/pallas_call | solution.py:1043
  530.4 1.9 fusion.51
  532.3 0.8 slice_reduce_fusion.8
  533.0 0.7 reshape.246
  534.4 1.4 slice_bitcast_fusion.4
  535.8 2.7 fusion.31
  538.5 2.4 copy.74
  540.9 3.6 fusion.19
  544.5 0.9 copy.73
  (106 shorter events, 10.9 us)
Async XLA Ops:
  0.7 4.9 copy-start
  5.6 6.7 %copy-start.11 = (bf16[1024,192]{0,1:T(8,128)(2,1)S(1)}, bf16[1024,192]{0,1:T(8,128)(2,1)}, u32[]{:S(2)}) copy-start(bf16[1024,192]{0,1:T(8,128)(2,1)} %param.21) | copy-start | bytes 1179652
  14.2 1.4 copy-start.10
  14.2 2.3 copy-start.12
  14.2 2.3 copy-start.13
  14.2 2.3 copy-start.14
  14.2 2.3 copy-start.15
  59.2 2.2 copy-start.2
  59.2 3.0 copy-start.16
  76.7 75.8 %copy-start.3 = (bf16[1024,192]{1,0:T(8,128)(2,1)S(1)}, bf16[1024,192]{1,0:T(8,128)(2,1)}, u32[]{:S(2)}) copy-start(bf16[1024,192]{1,0:T(8,128)(2,1)} %copy.50.x_ref) | copy-start | bytes 1179652
  164.6 85.6 %copy-start.19 = (bf16[2,768]{1,0:T(2,128)(2,1)S(1)}, bf16[2,768]{1,0:T(2,128)(2,1)}, u32[]{:S(2)}) copy-start(bf16[2,768]{1,0:T(2,128)(2,1)} %param.37) | copy-start | bytes 9220
  330.3 1.0 copy-start.4
  446.1 5.2 copy-start.8
  452.4 41.1 %copy-start.7 = (bf16[1024,384]{1,0:T(8,128)(2,1)S(1)}, bf16[1024,384]{1,0:T(8,128)(2,1)}, u32[]{:S(2)}) copy-start(bf16[1024,384]{1,0:T(8,128)(2,1)} %get-tuple-element.51) | copy-start | bytes 2359300
  493.5 3.1 copy-start.6
  493.5 3.2 copy-start.9
  497.2 38.5 %copy-start.5 = (f32[1024,192]{1,0:T(8,128)S(1)}, f32[1024,192]{1,0:T(8,128)}, u32[]{:S(2)}) copy-start(f32[1024,192]{1,0:T(8,128)} %copy-done.4) | copy-start | bytes 2359300
  540.9 4.6 copy-start.18
  540.9 5.2 copy-start.17
  540.9 5.8 %copy-start.1 = (s32[50304]{0:T(1024)S(1)}, s32[50304]{0:T(1024)}, u32[]{:S(2)}) copy-start(s32[50304]{0:T(1024)} %param.23) | copy-start | bytes 603652

commit v4 on v3

--- a/solution.py
+++ b/solution.py
@@ -73,17 +73,53 @@
     return sorted(range(1, rows), key=lambda k: -min(k, rows - k))
 
 
+def nt(left, right):
+    return lax.dot_general(left, right, (((1,), (1,)), ((), ())), preferred_element_type=F32)
+
+
+def nn(left, right):
+    return lax.dot_general(left, right, (((1,), (0,)), ((), ())), preferred_element_type=F32)
+
+
+def tn(left, right):
+    return lax.dot_general(left, right, (((0,), (0,)), ((), ())), preferred_element_type=F32)
+
+
+def side_by_side(v):
+    half = v.shape[0] // 2
+    return jnp.concatenate([v[:half], v[half:]], axis=1)
+
+
+def slots_of(target_ref, row, count):
+    base = row * count
+    slot = base + lax.broadcasted_iota(jnp.int32, (count, target_ref.shape[1]), 0)
+    return jnp.where(slot == target_ref[...], 1.0, 0.0).astype(BF16)
+
+
+def placed(target_ref, v, row, cap):
+    return side_by_side(nn(slots_of(target_ref, row, 2 * cap), v).astype(BF16))
+
+
+def combined(target_ref, block, row, cap):
+    width = block.shape[1] // 2
+    stacked = jnp.concatenate([block[:, :width], block[:, width:]], axis=0)
+    return tn(slots_of(target_ref, row, 2 * cap), stacked)
+
+
 def start_kernel(
     rows,
     pieces,
     x_ref,
     g_ref,
+    t_ref,
     w_ref,
     s_ref,
     xo_ref,
     go_ref,
     wo_ref,
     so_ref,
+    xp_ref,
+    gp_ref,
     c_send,
     c_recv,
     r_send,
@@ -97,7 +133,9 @@
     order = far_first(rows)
     peers = [{"row": (row + k) % rows} for k in order]
     greet(peers + [{"col": sib}, {"col": across}])
-    step = x_ref.shape[0] // pieces
+    xp_ref[...] = side_by_side(x_ref[...])
+    step = xp_ref.shape[0] // pieces
+    cap = gp_ref.shape[1]
     to_up, to_down = level < levels - 1, level > 0
 
     def weight(at, way, src=None):
@@ -129,7 +167,7 @@
         part = pl.ds(i * step, step)
         for way, peer in ((0, across), (1, sib)):
             copy = push(
-                x_ref.at[part],
+                xp_ref.at[part],
                 xo_ref.at[me, part],
                 c_send.at[way, i],
                 c_recv.at[way, i],
@@ -139,15 +177,22 @@
             sent.append(copy)
     row_copies = []
     for k, peer in enumerate(peers):
+        copy = push(s_ref, so_ref.at[row], r_send.at[0, k], r_recv.at[0, k], peer)
+        copy.start()
+        row_copies.append(copy)
+
+    def send_rows(k):
         target = (row + order[k]) % rows
-        for j, (src, dst) in enumerate(((s_ref, so_ref), (g_ref.at[target], go_ref))):
-            copy = push(src, dst.at[row], r_send.at[j, k], r_recv.at[j, k], peer)
-            copy.start()
-            row_copies.append(copy)
-    xo_ref[me] = x_ref[...]
+        gp_ref[k] = placed(t_ref, g_ref[...], target, cap)
+        copy = push(gp_ref.at[k], go_ref.at[row], r_send.at[1, k], r_recv.at[1, k], peers[k])
+        copy.start()
+        row_copies.append(copy)
+
+    send_rows(0)
+    xo_ref[me] = xp_ref[...]
     wo_ref[row] = w_ref[...]
     so_ref[row] = s_ref[...]
-    go_ref[row] = g_ref[row]
+    todo = list(range(1, rows - 1))
 
     def pass_on(k):
         at = level - k
@@ -190,6 +235,12 @@
             )
             copy.start()
             late.append(copy)
+        for _ in range(2):
+            if todo:
+                send_rows(todo.pop(0))
+    while todo:
+        send_rows(todo.pop(0))
+    go_ref[row] = placed(t_ref, g_ref[...], row, cap)
     for i in range(pieces):
         sent[2 * i].wait_send()
         sent[2 * i + 1].wait()
@@ -210,19 +261,23 @@
         copy.wait()
 
 
-def start_gather(x, g, w, s, rows):
+def start_gather(x, g, target, w, s, rows, cap):
     pieces = 4
+    tokens, width = x.shape
+    packed = (tokens // 2, 2 * width)
     return pl.pallas_call(
         functools.partial(start_kernel, rows, pieces),
         out_shape=(
-            jax.ShapeDtypeStruct((COLS,) + x.shape, x.dtype),
-            jax.ShapeDtypeStruct(g.shape, g.dtype),
+            jax.ShapeDtypeStruct((COLS,) + packed, x.dtype),
+            jax.ShapeDtypeStruct((rows, cap, 2 * width), g.dtype),
             jax.ShapeDtypeStruct((rows,) + w.shape, w.dtype),
             jax.ShapeDtypeStruct((rows,) + s.shape, s.dtype),
         ),
-        in_specs=[VSPEC] * 4,
+        in_specs=[VSPEC] * 5,
         out_specs=(VSPEC,) * 4,
         scratch_shapes=[
+            pltpu.VMEM(packed, x.dtype),
+            pltpu.VMEM((rows - 1, cap, 2 * width), g.dtype),
             DMA((3, pieces)),
             DMA((3, pieces)),
             DMA((2, rows - 1)),
@@ -231,19 +286,75 @@
             DMA((3, rows // 2)),
         ],
         compiler_params=params(0),
-    )(x, g, w, s)
-
-
-def col_gather_kernel(pieces, x_ref, xo_ref, c_send, c_recv):
+    )(x, g, target, w, s)
+
+
+def project_kernel(
+    x_ref, w_ref, gain_ref, shift_ref, bias_ref, q_ref, kv_ref, h_ref, n_ref, r_ref
+):
+    me = lax.axis_index("col")
+    half, width = x_ref.shape[1], x_ref.shape[2] // 2
+    w = w_ref[...].reshape(D, 4 * width)[:, : 3 * width]
+    step = min(half, 256)
+    for i in range(2 * half // step):
+        side, start = i * step // half, i * step % half
+        rows, feats = slice(start, start + step), slice(side * width, (side + 1) * width)
+        x = jnp.concatenate([x_ref[b, rows, feats] for b in range(COLS)], axis=1).astype(F32)
+        mean = jnp.mean(x, axis=-1, keepdims=True)
+        centred = x - mean
+        rstd = lax.rsqrt(jnp.mean(centred * centred, axis=-1, keepdims=True) + epsilon)
+        h = (centred * rstd * gain_ref[...] + shift_ref[...]).astype(BF16)
+        out = slice(i * step, (i + 1) * step)
+        h_ref[out] = h
+        n_ref[out] = (x_ref[me, rows, feats].astype(F32) - mean) * rstd
+        r_ref[out] = rstd
+        qkv = (nn(h, w) + bias_ref[...]).astype(BF16)
+        q_ref[out] = qkv[:, :width] * jnp.asarray(HD**-0.5, BF16)
+        kv_ref[out] = qkv[:, width:]
+
+
+def project(x, w, gain, shift, bias):
+    tokens, width = 2 * x.shape[1], x.shape[2] // 2
+    return pl.pallas_call(
+        project_kernel,
+        out_shape=(
+            jax.ShapeDtypeStruct((tokens, width), BF16),
+            jax.ShapeDtypeStruct((tokens, 2 * width), BF16),
+            jax.ShapeDtypeStruct((tokens, D), BF16),
+            jax.ShapeDtypeStruct((tokens, width), F32),
+            jax.ShapeDtypeStruct((tokens, 1), F32),
+        ),
+        in_specs=[VSPEC] * 5,
+        out_specs=(VSPEC,) * 5,
+        compiler_params=params(),
+    )(x, w, gain, shift, bias)
+
+
+def mid_kernel(
+    pieces,
+    x_ref,
+    w_ref,
+    att_ref,
+    low_ref,
+    do_ref,
+    delta_ref,
+    gw_ref,
+    xp_ref,
+    xo_ref,
+    wide_ref,
+    c_send,
+    c_recv,
+):
     me, sib, across, _ = col_places()
     greet([{"col": sib}, {"col": across}])
-    step = x_ref.shape[0] // pieces
+    xp_ref[...] = side_by_side(x_ref[...].astype(BF16))
+    step = xp_ref.shape[0] // pieces
     sent, late = [], []
     for i in range(pieces):
         part = pl.ds(i * step, step)
         for way, peer in ((0, across), (1, sib)):
             copy = push(
-                x_ref.at[part],
+                xp_ref.at[part],
                 xo_ref.at[me, part],
                 c_send.at[way, i],
                 c_recv.at[way, i],
@@ -251,7 +362,9 @@
             )
             copy.start()
             sent.append(copy)
-    xo_ref[me] = x_ref[...]
+    xo_ref[me] = xp_ref[...]
+    tokens, width = x_ref.shape
+    w = w_ref[...].reshape(D, 4 * width)[:, 3 * width :]
     for i in range(pieces):
         part = pl.ds(i * step, step)
         sent[2 * i].wait_recv()
@@ -268,18 +381,45 @@
         sent[2 * i].wait_send()
         sent[2 * i + 1].wait()
         late[i].wait()
-
-
-def col_gather(x, collective):
+        rows = slice(i * step, (i + 1) * step)
+        for half in range(2):
+            feats = slice(half * width, (half + 1) * width)
+            start = half * (tokens // 2) + i * step
+            out = slice(start, start + step)
+            wide = jnp.concatenate([xo_ref[b, rows, feats] for b in range(COLS)], axis=1)
+            wide_ref[out] = wide
+            do = nn(wide, w).astype(BF16)
+            do_ref[out] = do
+            both = (do.astype(F32) * att_ref[out]).T
+            for h in range(width // HD):
+                delta_ref[h : h + 1, out] = jnp.sum(
+                    both[h * HD : (h + 1) * HD], axis=0, keepdims=True
+                )
+    gw_ref[...] = tn(wide_ref[...], low_ref[...]).astype(BF16)
+
+
+def mid_gradient(x, w, attended, low, collective):
     pieces = 4
+    tokens, width = x.shape
+    packed = (tokens // 2, 2 * width)
     return pl.pallas_call(
-        functools.partial(col_gather_kernel, pieces),
-        out_shape=jax.ShapeDtypeStruct((COLS,) + x.shape, x.dtype),
-        in_specs=[VSPEC],
-        out_specs=VSPEC,
-        scratch_shapes=[DMA((3, pieces)), DMA((3, pieces))],
+        functools.partial(mid_kernel, pieces),
+        out_shape=(
+            jax.ShapeDtypeStruct((tokens, width), BF16),
+            jax.ShapeDtypeStruct((8, tokens), F32),
+            jax.ShapeDtypeStruct((D, width), BF16),
+        ),
+        in_specs=[VSPEC] * 4,
+        out_specs=(VSPEC,) * 3,
+        scratch_shapes=[
+            pltpu.VMEM(packed, BF16),
+            pltpu.VMEM((COLS,) + packed, BF16),
+            pltpu.VMEM((tokens, D), BF16),
+            DMA((3, pieces)),
+            DMA((3, pieces)),
+        ],
         compiler_params=params(collective),
-    )(x)
+    )(x, w, attended, low)
 
 
 def small_kernel(x_ref, xo_ref, c_send, c_recv):
@@ -325,18 +465,6 @@
 
     count = COLS + (level > 0).astype(jnp.int32) + (level < levels - 1).astype(jnp.int32)
     pl.semaphore_wait(barrier, count)
-
-
-def nt(left, right):
-    return lax.dot_general(left, right, (((1,), (1,)), ((), ())), preferred_element_type=F32)
-
-
-def nn(left, right):
-    return lax.dot_general(left, right, (((1,), (0,)), ((), ())), preferred_element_type=F32)
-
-
-def tn(left, right):
-    return lax.dot_general(left, right, (((0,), (0,)), ((), ())), preferred_element_type=F32)
 
 
 def seen(key_start, query_start, shape, prefix):
@@ -813,15 +941,12 @@
         home.append(copy)
     if rows:
         eo_ref[row] = e_ref[row]
-    step = a_ref.shape[0] // pieces
+    half = a_ref.shape[0] // 2
+    step = half // pieces
 
     def term(i, who):
-        return lax.dot_general(
-            a_ref[pl.ds(i * step, step)],
-            b_ref[who],
-            (((1,), (1,)), ((), ())),
-            preferred_element_type=F32,
-        )
+        parts = [nt(a_ref[pl.ds(n * half + i * step, step)], b_ref[who]) for n in range(2)]
+        return jnp.concatenate(parts, axis=1)
 
     def near(i, j):
         part = pl.ds(i * step, step)
@@ -851,7 +976,10 @@
         near(i, 1).wait_recv()
         mine = mine + rx_ref[1, part].astype(F32)
         over(i).wait_recv()
-        out_ref[part] = mine + far_ref[part].astype(F32)
+        mine = mine + far_ref[part].astype(F32)
+        width = mine.shape[1] // 2
+        out_ref[part] = mine[:, :width]
+        out_ref[pl.ds(half + i * step, step)] = mine[:, width:]
     for i in range(pieces):
         near(i, 0).wait_send()
         near(i, 1).wait_send()
@@ -863,8 +991,8 @@
 def product_scatter(a, b, collective, back=None):
     pieces = 4
     tokens, width = a.shape[0], b.shape[1]
-    block = pltpu.VMEM((tokens, width), BF16)
-    pair = pltpu.VMEM((2, tokens, width), BF16)
+    block = pltpu.VMEM((tokens // 2, 2 * width), BF16)
+    pair = pltpu.VMEM((2, tokens // 2, 2 * width), BF16)
     out = jax.ShapeDtypeStruct((tokens, width), F32)
     scratch = [pair, pair, block, block, DMA((3, pieces)), DMA((3, pieces))]
     rows = 0
@@ -882,19 +1010,22 @@
     )(*((a, b, back) if rows else (a, b)))
 
 
-def dispatch_kernel(rows, in_ref, out_ref, r_send, r_recv, c_send, c_recv):
+def dispatch_kernel(rows, x_ref, t_ref, out_ref, in_ref, r_send, r_recv, c_send, c_recv):
     me, sib, across, _ = col_places()
     row = lax.axis_index("row")
     order = far_first(rows)
     peers = [(row + k) % rows for k in order]
     greet([{"row": p} for p in peers] + [{"col": sib}, {"col": across}])
     copies = []
+    cap = in_ref.shape[1]
     for k, peer in enumerate(peers):
+        in_ref[peer] = placed(t_ref, x_ref[...], peer, cap)
         copy = push(
             in_ref.at[peer], out_ref.at[me, row], r_send.at[k], r_recv.at[k], {"row": peer}
         )
         copy.start()
         copies.append(copy)
+    in_ref[row] = placed(t_ref, x_ref[...], row, cap)
 
     def col(src, dst, k, way):
         return push(
@@ -933,19 +1064,38 @@
         copy.wait()
 
 
-def dispatch(x, rows, collective):
+def dispatch(x, target, rows, cap, collective):
+    block = (rows, cap, 2 * x.shape[1])
     return pl.pallas_call(
         functools.partial(dispatch_kernel, rows),
-        out_shape=jax.ShapeDtypeStruct((COLS,) + x.shape, x.dtype),
-        in_specs=[VSPEC],
+        out_shape=jax.ShapeDtypeStruct((COLS,) + block, x.dtype),
+        in_specs=[VSPEC] * 2,
         out_specs=VSPEC,
-        scratch_shapes=[DMA((rows - 1,)), DMA((rows - 1,)), DMA((3, rows)), DMA((3, rows))],
+        scratch_shapes=[
+            pltpu.VMEM(block, x.dtype),
+            DMA((rows - 1,)),
+            DMA((rows - 1,)),
+            DMA((3, rows)),
+            DMA((3, rows)),
+        ],
         compiler_params=params(collective),
-    )(x)
+    )(x, target)
 
 
 def giveback_kernel(
-    rows, in_ref, out_ref, rx_ref, far_ref, tot_ref, fin_ref, send, recv, r_send, r_recv
+    rows,
+    in_ref,
+    t_ref,
+    sum_ref,
+    out_ref,
+    rx_ref,
+    far_ref,
+    tot_ref,
+    fin_ref,
+    send,
+    recv,
+    r_send,
+    r_recv,
 ):
     me, sib, across, diag = col_places()
     row = lax.axis_index("row")
@@ -988,23 +1138,30 @@
         if k >= 1:
             finish(k - 1)
     finish(rows - 1)
+    cap = out_ref.shape[1]
+    sum_ref[...] = combined(t_ref, out_ref[row], row, cap)
+    for k, gap in enumerate(far_first(rows)):
+        source = (row + rows - gap) % rows
+        home(k).wait_recv()
+        sum_ref[...] += combined(t_ref, out_ref[source], source, cap)
     for k in range(rows):
         near(k, 0).wait_send()
         near(k, 1).wait_send()
         over(k).wait_send()
         if k < rows - 1:
-            home(k).wait()
-
-
-def giveback(parts, rows, collective):
+            home(k).wait_send()
+
+
+def giveback(parts, target, rows, collective):
     block = parts.shape[2:]
     one = pltpu.VMEM((rows,) + block, BF16)
     return pl.pallas_call(
         functools.partial(giveback_kernel, rows),
-        out_shape=jax.ShapeDtypeStruct((rows,) + block, BF16),
-        in_specs=[VSPEC],
+        out_shape=jax.ShapeDtypeStruct((target.shape[1], block[1] // 2), F32),
+        in_specs=[VSPEC] * 2,
         out_specs=VSPEC,
         scratch_shapes=[
+            one,
             pltpu.VMEM((2, rows) + block, BF16),
             one,
             one,
@@ -1015,10 +1172,12 @@
             DMA((rows - 1,)),
         ],
         compiler_params=params(collective),
-    )(parts)
-
-
-def end_kernel(rows, w_ref, s_ref, wo_ref, so_ref, wr_ref, sr_ref, send, recv):
+    )(parts, target)
+
+
+def end_kernel(
+    rows, w_ref, s_ref, e_ref, t_ref, mid_ref, wo_ref, so_ref, lo_ref, wr_ref, sr_ref, send, recv
+):
     row = lax.axis_index("row")
     peers = [(row + k) % rows for k in range(1, rows)]
     greet([{"row": p} for p in peers])
@@ -1030,6 +1189,10 @@
             copies.append(copy)
     wo_ref[...] = w_ref[row].astype(F32)
     so_ref[...] = s_ref[row]
+    total = mid_ref[...]
+    for r in range(rows):
+        total = total + combined(t_ref, e_ref[r], r, e_ref.shape[1])
+    lo_ref[...] = total.astype(BF16)
     for k in range(rows - 1):
         copies[2 * k].wait_recv()
         copies[2 * k + 1].wait_recv()
@@ -1039,15 +1202,16 @@
         copy.wait_send()
 
 
-def end_scatter(w, s, rows, collective):
+def end_scatter(w, s, outs, target, mid, rows, collective):
     return pl.pallas_call(
         functools.partial(end_kernel, rows),
         out_shape=(
             jax.ShapeDtypeStruct(w.shape[1:], F32),
             jax.ShapeDtypeStruct(s.shape[1:], F32),
+            jax.ShapeDtypeStruct(mid.shape, BF16),
         ),
-        in_specs=[VSPEC] * 2,
-        out_specs=(VSPEC,) * 2,
+        in_specs=[VSPEC] * 5,
+        out_specs=(VSPEC,) * 3,
         scratch_shapes=[
             pltpu.VMEM((rows - 1,) + w.shape[1:], w.dtype),
             pltpu.VMEM((rows - 1,) + s.shape[1:], s.dtype),
@@ -1055,7 +1219,7 @@
             DMA((2, rows - 1)),
         ],
         compiler_params=params(collective),
-    )(w, s)
+    )(w, s, outs, target, mid)
 
 
 def expert_kernel(
@@ -1071,10 +1235,17 @@
     gdown_ref,
     gbd_ref,
 ):
-    cols, rows, _, cap, width = x_ref.shape
+    cols, rows, cap, both = x_ref.shape
+    width = both // 2
     slots = rows * cap
-    x = jnp.concatenate([x_ref[b, :, 0].reshape(slots, width) for b in range(cols)], axis=1)
-    g = jnp.concatenate([g_ref[b, :, 0].reshape(slots, width) for b in range(cols)], axis=1)
+    first = pl.program_id(0) == 0
+
+    def mine(ref):
+        blocks = [ref[b].reshape(slots, both) for b in range(cols)]
+        blocks = [jnp.where(first, v[:, :width], v[:, width:]) for v in blocks]
+        return jnp.concatenate(blocks, axis=1)
+
+    x, g = mine(x_ref), mine(g_ref)
     gbd_ref[...] = jnp.sum(g.astype(F32), axis=0).reshape(gbd_ref.shape)
     hidden_units = up_ref.shape[2]
     chunk = 256
@@ -1094,16 +1265,20 @@
         gdown_ref[0, cut, :] = tn(hidden, g)
         gup_ref[0, :, cut] = tn(x, grad)
         gbu_ref[0, :, cut] = jnp.sum(grad.astype(F32), axis=0, keepdims=True)
-    for b in range(cols):
-        cut = slice(b * width, (b + 1) * width)
-        part_ref[b, :, 0] = part[:, cut].astype(BF16).reshape(rows, cap, width)
-        gx_ref[b, :, 0] = gx[:, cut].astype(BF16).reshape(rows, cap, width)
+    for e in range(EXP_DEV):
+
+        @pl.when(pl.program_id(0) == e)
+        def _(e=e):
+            lanes = slice(e * width, (e + 1) * width)
+            for b in range(cols):
+                cut = slice(b * width, (b + 1) * width)
+                part_ref[b, :, :, lanes] = part[:, cut].astype(BF16).reshape(rows, cap, width)
+                gx_ref[b, :, :, lanes] = gx[:, cut].astype(BF16).reshape(rows, cap, width)
 
 
 def experts(x, g, w_up, bias_up, w_down):
-    cols, rows, count, cap, width = x.shape
-    slots = pl.BlockSpec((cols, rows, 1, cap, width), lambda e: (0, 0, e, 0, 0))
-    _, features, hidden = w_up.shape
+    slots = pl.BlockSpec(x.shape, lambda e: (0, 0, 0, 0))
+    count, features, hidden = w_up.shape
     return pl.pallas_call(
         expert_kernel,
         grid=(count,),
@@ -1192,21 +1367,15 @@
     before = jnp.dot(earlier.astype(BF16), hits.astype(BF16), preferred_element_type=F32)
     slot_of = jnp.sum(jnp.where(hits, before, 0.0), axis=1).astype(jnp.int32)
     target = expert_of * capacity + slot_of
-    chosen = (
-        jnp.arange(expert_total * capacity, dtype=jnp.int32)[:, None] == target[None, :]
-    ).astype(BF16)
-
-    def place_rows(v):
-        v = jnp.dot(chosen, v, preferred_element_type=F32).astype(BF16)
-        return v.reshape(rows, EXP_DEV, capacity, width)
+    target = target[None, :]
 
     weights = jnp.concatenate([w_query, w_key, w_value, w_output], axis=1)
     x_all, g_own, w_all, s_all = start_gather(
-        layer_in, place_rows(cotangent), weights, small, rows
-    )
-    w_all = w_all.reshape(D, 4 * width)
-    w_qkv = w_all[:, : 3 * width]
-    w_out = w_all[:, 3 * width :].reshape(COLS, width, width)
+        layer_in, cotangent, target, weights, small, rows, capacity
+    )
+    w_flat = w_all.reshape(D, 4 * width)
+    w_qkv = w_flat[:, : 3 * width]
+    w_out = w_flat[:, 3 * width :].reshape(COLS, width, width)
     gain_one, shift_one, gain_two, shift_two, out_bias = (
         s_all[:, i, :share].reshape(D) for i in range(5)
     )
@@ -1222,19 +1391,15 @@
         for i in (5, 6)
     )
 
-    resid = x_all.transpose(1, 0, 2).reshape(tokens, D).astype(F32)
-    mean_one = jnp.mean(resid, axis=-1, keepdims=True)
-    centred = resid - mean_one
-    rstd_one = lax.rsqrt(jnp.mean(centred * centred, axis=-1, keepdims=True) + epsilon)
-    h_one = (centred * rstd_one * gain_one + shift_one).astype(BF16)
     qkv_bias = jnp.concatenate([query_bias, jnp.zeros_like(query_bias), value_bias])
-    qkv = (jnp.dot(h_one, w_qkv, preferred_element_type=F32) + qkv_bias).astype(BF16)
-    queries = qkv[:, :width] * jnp.asarray(HD**-0.5, BF16)
+    queries, keys_values, h_one, normed_one, rstd_one = project(
+        x_all, w_all, gain_one[None], shift_one[None], qkv_bias[None]
+    )
     seq_hit = row // group == jnp.arange(prefix_len.shape[0], dtype=jnp.int32)
     prefix = jnp.sum(jnp.where(seq_hit, prefix_len, 0))
     info = prefix.astype(jnp.int32).reshape(1)
     kv_all, attended, attended_low, lse, g_all = attention_forward(
-        info, queries, qkv[:, width:], g_own, group, low, 1
+        info, queries, keys_values, g_own, group, low, 1
     )
     branch = product_scatter(attended_low, w_out, 2)
     x_own = layer_in.astype(F32)
@@ -1251,11 +1416,11 @@
     gain_two_own = own(gain_two)
     h_two = (normed_two * gain_two_own + own(shift_two)).astype(BF16)
 
-    received = dispatch(place_rows(h_two), rows, 4)
+    received = dispatch(h_two, target, rows, capacity, 4)
     parts, grad_parts, grad_w_up, grad_bias_up, grad_w_down, grad_bias_down = experts(
         received, g_all, w_up, bias_up, w_down
     )
-    grad_h_two = tn(chosen, giveback(grad_parts, rows, 5).reshape(-1, width))
+    grad_h_two = giveback(grad_parts, target, rows, 5)
 
     scaled = grad_h_two * gain_two_own
     sums = jnp.stack([jnp.sum(scaled, axis=-1), jnp.sum(scaled * normed_two, axis=-1)])
@@ -1264,19 +1429,9 @@
     grad_mid = cotangent.astype(F32) + rstd_two * (
         scaled - sums[0][:, None] - normed_two * sums[1][:, None]
     )
-    grad_all = col_gather(grad_mid.astype(BF16), 7)
-    grad_wide = grad_all.transpose(1, 0, 2).reshape(tokens, D)
-    grad_w_out = lax.dot_general(
-        grad_wide, attended_low, (((0,), (0,)), ((), ())), preferred_element_type=F32
-    )
-    grad_attended = jnp.dot(
-        grad_wide, w_out.reshape(D, width), preferred_element_type=F32
-    ).astype(BF16)
-    delta = jnp.sum(
-        (grad_attended.astype(F32) * attended).reshape(tokens, heads, HD), axis=-1
-    ).T
-    delta = jnp.pad(delta, ((0, 8 - heads), (0, 0)))
+    grad_attended, delta, grad_w_out = mid_gradient(grad_mid, w_all, attended, attended_low, 7)
     down_own = lax.dynamic_slice_in_dim(bias_down, col * width, width, 1).astype(F32)
+    down_own = down_own.reshape(1, EXP_DEV * width)
     grad_q, grad_kv, outs = attention_backward(
         info,
         queries,
@@ -1285,7 +1440,7 @@
         lse,
         delta,
         parts,
-        down_own[:, None, :],
+        down_own,
         group,
         low,
         8,
@@ -1296,8 +1451,6 @@
     )
     grad_bias = jnp.sum(grad_qkv, axis=0, dtype=F32)
     grad_h_one, outs = product_scatter(grad_qkv, w_qkv.reshape(COLS, width, 3 * width), 9, outs)
-    layer_out = (mid + tn(chosen, outs.reshape(-1, width))).astype(BF16)
-    normed_one = (x_own - mean_one) * rstd_one
     scaled = grad_h_one * own(gain_one)
     sums = jnp.stack([jnp.sum(scaled, axis=-1), jnp.sum(scaled * normed_one, axis=-1)])
     vectors = jnp.stack(
@@ -1330,9 +1483,10 @@
         ],
         axis=1,
     )
-    weight_terms = jnp.concatenate([grad_w_qkv, grad_w_out], axis=1).astype(BF16)
-    weight_sums, small_sums = end_scatter(
-        weight_terms.reshape(rows, share, 4 * width), small_terms, rows, 11
+    weight_terms = jnp.concatenate([grad_w_qkv.astype(BF16), grad_w_out], axis=1)
+    weight_terms = weight_terms.reshape(rows, share, 4 * width)
+    weight_sums, small_sums, layer_out = end_scatter(
+        weight_terms, small_terms, outs, target, mid, rows, 11
     )
 
     def bias_back(v):

time: 555 us -> 495 us (0.89)
  matrix products: 22.3 us -> 3.52 us
  Pallas kernels: 445 us -> 428 us
  local copies, waits for them, and re-layouts: 45 us -> 33.3 us
  other arithmetic: 32.3 us -> 22.2 us
    dot_general x7 -> x0, matrix products: 18.7 us -> none  [the longest x2 7.51 us: tn(): lax.dot_general(left, right, (((0,), (0,)), ((), ())), preferred_element_...]
    pallas_call x2, Pallas kernels: 50.8 us -> 40.6 us  [product_scatter(): pl.pallas_call(functools.partial(product_kernel, pieces, rows), out_shape...]
    pallas_call x1, Pallas kernels: 41.9 us -> 33.8 us  [start_gather(): pl.pallas_call(functools.partial(start_kernel, rows, pieces), out_shape=(...]
    pallas_call x1, Pallas kernels: 23.2 us -> 30.1 us  [experts(): pl.pallas_call(expert_kernel, grid=(count,), out_shape=(jax.ShapeDtypeStr...]
    convert_element_type x3 -> x0, local copies, waits for them, and re-layouts: 6.43 us -> none  [the longest x1 3.84 us: per_device(): resid = x_all.transpose(1, 0, 2).reshape(tokens, D).astype(F32)]
    pallas_call x1, Pallas kernels: 39.8 us -> 33.4 us  [giveback(): pl.pallas_call(functools.partial(giveback_kernel, rows), out_shape=jax.Sh...]
    pallas_call x1 -> x2, Pallas kernels: 18.1 us -> 22.8 us  [the longest x1 16.4 us: mid_gradient(): pl.pallas_call(functools.partial(mid_kernel, pieces), out_shape=(jax.Shap...]
where the time goes in v4:
time: 495 us; the launch traced here: 489 us
  Pallas kernels  428 us (86%)
  local copies, waits for them, and re-layouts  33.3 us (7%)
  other arithmetic  22.2 us (4%)
    pallas_call x1, Pallas kernels, attention_backward(): pl.pallas_call(functools.partial(backward_kernel, group, low, pieces, tok...  83.9 us
    pallas_call x1, Pallas kernels, dispatch(): pl.pallas_call(functools.partial(dispatch_kernel, rows), out_shape=jax.Sh...  80.1 us
    pallas_call x1, Pallas kernels, attention_forward(): pl.pallas_call(functools.partial(forward_kernel, group, low, pieces, toke...  55.4 us
    pallas_call x2, Pallas kernels, product_scatter(): pl.pallas_call(functools.partial(product_kernel, pieces, rows), out_shape...  40.6 us
    pallas_call x1, Pallas kernels, start_gather(): pl.pallas_call(functools.partial(start_kernel, rows, pieces), out_shape=(...  33.8 us
    pallas_call x1, Pallas kernels, giveback(): pl.pallas_call(functools.partial(giveback_kernel, rows), out_shape=jax.Sh...  33.4 us
    pallas_call x1, Pallas kernels, end_scatter(): pl.pallas_call(functools.partial(end_kernel, rows), out_shape=(jax.ShapeD...  32.7 us
    pallas_call x1, Pallas kernels, experts(): pl.pallas_call(expert_kernel, grid=(count,), out_shape=(jax.ShapeDtypeStr...  30.1 us

profile of v4, /device:TPU:10, one launch (start us, length us, event | category | flops | bytes accessed | tf_op | source)
XLA Modules:
  0.0 488.8 jit_solution(13606382483752471518)
XLA Ops:
  1.4 0.8 convert_element_type.66
  2.1 0.8 convert_element_type.68
  2.9 0.7 bitcast_convert_fusion.2
  3.6 0.7 bitcast_convert_fusion.4
  4.3 0.7 bitcast_convert_fusion.6
  4.9 0.6 stack.102.s_ref
  5.5 0.7 fusion.11
  6.2 6.2 %gather_fusion = s32[1024]{0:T(1024)S(1)} fusion(s32[50304]{0:T(1024)S(1)} %copy-done, s32[1024]{0:T(1024)S(1)} %fusion.11), kind=kCustom, calls=%fused_computation | custom fusion | bytes 12288 | tf_op jit(solution)/shard_map/gather | solution.py:1362
  12.5 0.5 fusion.2
  13.0 0.6 convert_add_fusion
  13.6 1.0 copy.46.x_ref
  14.6 1.0 copy.47.g_ref
  15.6 0.8 pad_maximum_fusion.2.w_ref
  16.4 33.8 %shard_map.323 = (bf16[4,512,384]{2,1,0:T(8,128)(2,1)}, bf16[8,128,384]{2,1,0:T(8,128)(2,1)}, bf16[8,96,768]{2,1,0:T(8,128)(2,1)}, f32[8,8,128]{2,1,0:T(8,128)}) custom-call(bf16[1024,192]{1,0:T(8,128)(2,1)} %copy.46.x_ref, bf16[1024,192]{1,0:T(8,128)(2,1)} %copy.47.g_ref, s32[1,1024]{1,0:T(1,128)} %bitcast.104, bf16[96,768]{1,0:T(8,128)(2,1)} %pad_maximum_fusion.2.w_ref, ...), custom_call_target="tpu_custom_call" | custom-call | tf_op jit(solution)/shard_map/pallas_call | solution.py:268
  50.2 0.9 slice_reduce_fusion.5
  51.5 0.6 broadcast_in_dim.17.bias_ref
  52.1 1.0 slice_reduce_fusion.2
  53.1 0.7 broadcast_in_dim_reshape_squeeze.6.gain_ref
  53.7 0.7 broadcast_in_dim_reshape_squeeze.7.shift_ref
  54.4 6.4 %shard_map.324 = (bf16[1024,192]{1,0:T(8,128)(2,1)}, bf16[1024,384]{1,0:T(8,128)(2,1)}, bf16[1024,768]{1,0:T(8,128)(2,1)}, f32[1024,192]{1,0:T(8,128)}, f32[1024,1]{1,0:T(8,128)}) custom-call(bf16[4,512,384]{2,1,0:T(8,128)(2,1)} %get-tuple-element.48.x_ref, bf16[8,96,768]{2,1,0:T(8,128)(2,1)} %get-tuple-element.49.w_ref, ...), custom_call_target="tpu_custom_call" | custom-call | tf_op jit(solution)/shard_map/pallas_call | solution.py:318
  60.8 55.4 %shard_map.325 = (bf16[8,1024,384]{2,1,0:T(8,128)(2,1)}, f32[1024,192]{1,0:T(8,128)}, bf16[1024,192]{1,0:T(8,128)(2,1)}, f32[8,1024]{1,0:T(8,128)}, bf16[4,8,128,384]{3,2,1,0:T(8,128)(2,1)}) custom-call(s32[1]{0:T(128)S(6)} %select_n.26.info_ref, bf16[1024,192]{1,0:T(8,128)(2,1)} %get-tuple-element.52.q_ref, bf16[1024,384]{1,0:T(8,128)(2,1)} %get-tuple-element.53.kv_ref, ...), custom_call_target="tpu_custom_call" | custom-call | tf_op jit(solution)/shard_map/pallas_call | solution.py:669
  116.2 1.9 slice.153
  118.1 15.4 %shard_map.326 = f32[1024,192]{1,0:T(8,128)} custom-call(bf16[1024,192]{1,0:T(8,128)(2,1)} %get-tuple-element.56.refs_0_.low_ref, bf16[4,192,192]{2,1,0:T(8,128)(2,1)} %bitcast.101), custom_call_target="tpu_custom_call" | custom-call | tf_op jit(solution)/shard_map/pallas_call | solution.py:1003
  133.6 1.5 fusion.13
  135.1 0.4 multiply_reduce_fusion.4
  135.5 0.6 reshape.203.x_ref
  136.1 5.0 %shard_map.327 = f32[4,16,128]{2,1,0:T(8,128)} custom-call(f32[16,128]{1,0:T(8,128)} %reshape.203.x_ref), custom_call_target="tpu_custom_call" | custom-call | tf_op jit(solution)/shard_map/pallas_call | solution.py:440
  141.1 0.8 reshape.204
  142.3 1.1 add_convert_fusion.x_ref
  143.4 80.1 %shard_map.328.x_ref = bf16[4,8,128,384]{3,2,1,0:T(8,128)(2,1)} custom-call(bf16[1024,192]{1,0:T(8,128)(2,1)} %add_convert_fusion.x_ref, s32[1,1024]{1,0:T(1,128)} %bitcast.105), custom_call_target="tpu_custom_call" | custom-call | tf_op jit(solution)/shard_map/pallas_call | solution.py:1069
  223.5 0.6 copy.53.bias_ref
  224.1 30.1 %shard_map.329 = (bf16[4,8,128,384]{3,2,1,0:T(8,128)(2,1)}, bf16[4,8,128,384]{3,2,1,0:T(8,128)(2,1)}, f32[2,768,768]{2,1,0:T(8,128)}, f32[2,1,768]{2,1,0:T(1,128...) custom-call(bf16[4,8,128,384]{3,2,1,0:T(8,128)(2,1)} %shard_map.328.x_ref, ...), custom_call_target="tpu_custom_call" | custom-call | tf_op jit(solution)/shard_map/pallas_call | solution.py:1282
  254.2 33.4 %shard_map.330 = f32[1024,192]{1,0:T(8,128)} custom-call(bf16[4,8,128,384]{3,2,1,0:T(8,128)(2,1)} %get-tuple-element.58.in_ref, s32[1,1024]{1,0:T(1,128)} %bitcast.106), custom_call_target="tpu_custom_call" | custom-call | tf_op jit(solution)/shard_map/pallas_call | solution.py:1158
  287.6 2.0 multiply_reduce_fusion
  289.7 0.6 reshape.206.x_ref
  290.3 5.0 %shard_map.331 = f32[4,16,128]{2,1,0:T(8,128)} custom-call(f32[16,128]{1,0:T(8,128)} %reshape.206.x_ref), custom_call_target="tpu_custom_call" | custom-call | tf_op jit(solution)/shard_map/pallas_call | solution.py:440
  295.3 0.8 reduce_sum.164
  296.1 1.6 fusion.12
  297.8 16.4 %shard_map.332 = (bf16[1024,192]{1,0:T(8,128)(2,1)}, f32[8,1024]{1,0:T(8,128)}, bf16[768,192]{1,0:T(8,128)(2,1)}) custom-call(f32[1024,192]{1,0:T(8,128)} %get-tuple-element.131.x_ref, bf16[8,96,768]{2,1,0:T(8,128)(2,1)} %get-tuple-element.49.w_ref, f32[1024,192]{1,0:T(8,128)} %get-tuple-element.59.att_ref, bf16[1024,192]{1,0:T(8,128)(2,1)} %get-tuple-element.56.refs_0_.low_ref), custom_call_target="tpu_custom_call" | custom-call | tf_op jit(solution)/shard_map/pallas_call | solution.py:405
  314.1 0.8 dynamic-slice_convert_fusion
  314.9 0.6 reshape.229.bias_ref
  315.5 83.9 %shard_map.333 = (bf16[1024,192]{1,0:T(8,128)(2,1)}, bf16[1024,384]{1,0:T(8,128)(2,1)}, bf16[8,128,384]{2,1,0:T(8,128)(2,1)}) custom-call(s32[1]{0:T(128)S(6)} %select_n.26.info_ref, bf16[1024,192]{1,0:T(8,128)(2,1)} %get-tuple-element.52.q_ref, bf16[8,1024,384]{2,1,0:T(8,128)(2,1)} %get-tuple-element.55.kv_ref, bf16[1024,192]{1,0:T(8,128)(2,1)} %get-tuple-element.60.do_ref, ...), custom_call_target="tpu_custom_call" | custom-call | tf_op jit(solution)/shard_map/pallas_call | solution.py:901
  399.4 3.0 pad_maximum_fusion.refs_0_
  402.4 1.1 slice.158
  403.5 25.2 %shard_map.334 = (f32[1024,192]{1,0:T(8,128)}, bf16[8,128,384]{2,1,0:T(8,128)(2,1)}) custom-call(bf16[1024,576]{1,0:T(8,128)(2,1)} %pad_maximum_fusion.refs_0_, bf16[4,192,576]{2,1,0:T(8,128)(2,1)} %bitcast.100, bf16[8,128,384]{2,1,0:T(8,128)(2,1)} %get-tuple-element.67.refs_2_), custom_call_target="tpu_custom_call" | custom-call | tf_op jit(solution)/shard_map/pallas_call | solution.py:1003
  428.8 1.7 multiply_reduce_fusion.2
  430.6 0.6 pad_maximum_fusion.3.x_ref
  431.2 5.1 %shard_map.335 = f32[4,32,128]{2,1,0:T(8,128)} custom-call(f32[32,128]{1,0:T(8,128)} %pad_maximum_fusion.3.x_ref), custom_call_target="tpu_custom_call" | custom-call | tf_op jit(solution)/shard_map/pallas_call | solution.py:440
  436.4 0.8 slice_reduce_fusion
  437.4 2.1 multiply_add_fusion
  439.5 1.2 copy.63
  440.9 0.6 convert_reduce_fusion
  441.9 0.7 fusion.3.s_ref
  442.6 3.0 convolution_convert_fusion
  445.9 1.4 copy.55
  447.3 32.7 %shard_map.336 = (f32[96,768]{1,0:T(8,128)}, f32[8,128]{1,0:T(8,128)}, bf16[1024,192]{1,0:T(8,128)(2,1)}) custom-call(bf16[8,96,768]{2,1,0:T(8,128)(2,1)} %bitcast.99, f32[8,8,128]{2,1,0:T(8,128)} %fusion.3.s_ref, bf16[8,128,384]{2,1,0:T(8,128)(2,1)} %get-tuple-element.70.e_ref, s32[1,1024]{1,0:T(1,128)} %bitcast.107, f32[1024,192]{1,0:T(8,128)} %copy-done.1), custom_call_target="tpu_custom_call" | custom-call | tf_op jit(solution)/shard_map/pallas_call | solution.py:1206
  480.1 1.9 fusion.14
  481.9 2.0 copy.62
  483.9 0.8 slice_reduce_fusion.7
  484.7 0.7 reshape.219
  485.3 0.7 reshape.220
  486.0 1.4 slice_bitcast_fusion.4
  487.4 0.6 copy.81
  488.0 0.6 copy.82
  (91 shorter events, 2.3 us)
Async XLA Ops:
  0.7 5.6 %copy-start = (s32[50304]{0:T(1024)S(1)}, s32[50304]{0:T(1024)}, u32[]{:S(2)}) copy-start(s32[50304]{0:T(1024)} %param.23) | copy-start | bytes 603652
  6.2 7.3 %copy-start.11 = (bf16[1024,192]{0,1:T(8,128)(2,1)S(1)}, bf16[1024,192]{0,1:T(8,128)(2,1)}, u32[]{:S(2)}) copy-start(bf16[1024,192]{0,1:T(8,128)(2,1)} %param.20) | copy-start | bytes 1179652
  6.2 8.3 %copy-start.12 = (bf16[1024,192]{0,1:T(8,128)(2,1)S(1)}, bf16[1024,192]{0,1:T(8,128)(2,1)}, u32[]{:S(2)}) copy-start(bf16[1024,192]{0,1:T(8,128)(2,1)} %param.21) | copy-start | bytes 1179652
  12.4 3.2 copy-start.14
  12.4 3.2 copy-start.15
  12.4 3.2 copy-start.16
  12.4 3.2 copy-start.17
  60.8 72.8 %copy-start.6 = (bf16[1024,192]{1,0:T(8,128)(2,1)S(1)}, bf16[1024,192]{1,0:T(8,128)(2,1)}, u32[]{:S(2)}) copy-start(bf16[1024,192]{1,0:T(8,128)(2,1)} %copy.46.x_ref) | copy-start | bytes 1179652
  135.1 161.0 %copy-start.1 = (f32[1024,192]{1,0:T(8,128)}, f32[1024,192]{1,0:T(8,128)S(1)}, u32[]{:S(2)}) copy-start(f32[1024,192]{1,0:T(8,128)S(1)} %get-tuple-element.133.mid_ref) | copy-start | bytes 2359300
  142.3 81.2 %copy-start.20 = (bf16[2,768]{1,0:T(2,128)(2,1)S(1)}, bf16[2,768]{1,0:T(2,128)(2,1)}, u32[]{:S(2)}) copy-start(bf16[2,768]{1,0:T(2,128)(2,1)} %param.37) | copy-start | bytes 9220
  254.2 41.9 %copy-start.5 = (bf16[1024,192]{1,0:T(8,128)(2,1)S(1)}, bf16[1024,192]{1,0:T(8,128)(2,1)}, u32[]{:S(2)}) copy-start(bf16[1024,192]{1,0:T(8,128)(2,1)} %copy.47.g_ref) | copy-start | bytes 1179652
  287.6 8.5 %copy-start.3 = (f32[1024,192]{1,0:T(8,128)S(1)}, f32[1024,192]{1,0:T(8,128)}, u32[]{:S(2)}) copy-start(f32[1024,192]{1,0:T(8,128)} %shard_map.330) | copy-start | bytes 2359300
  399.4 3.0 copy-start.2
  402.4 26.4 %copy-start.7 = (f32[1024,192]{1,0:T(8,128)S(1)}, f32[1024,192]{1,0:T(8,128)}, u32[]{:S(2)}) copy-start(f32[1024,192]{1,0:T(8,128)} %get-tuple-element.69) | copy-start | bytes 2359300
  403.5 33.7 %copy-start.10 = (f32[1024,1]{1,0:T(8,128)S(1)}, f32[1024,1]{1,0:T(8,128)}, u32[]{:S(2)}) copy-start(f32[1024,1]{1,0:T(8,128)} %get-tuple-element.72) | copy-start | bytes 12292
  403.5 33.9 %copy-start.4 = (f32[1024,192]{1,0:T(8,128)S(1)}, f32[1024,192]{1,0:T(8,128)}, u32[]{:S(2)}) copy-start(f32[1024,192]{1,0:T(8,128)} %get-tuple-element.131.x_ref) | copy-start | bytes 2359300
  437.4 3.4 copy-start.9
  439.5 1.3 copy-start.8
  442.6 3.0 copy-start.13
  447.3 40.1 %copy-start.19 = (f32[2,1,768]{2,1,0:T(1,128)S(1)}, f32[2,1,768]{2,1,0:T(1,128)}, u32[]{:S(2)}) copy-start(f32[2,1,768]{2,1,0:T(1,128)} %get-tuple-element.78) | copy-start | bytes 18436
  447.3 40.7 %copy-start.18 = (f32[2,1,768]{2,1,0:T(1,128)S(1)}, f32[2,1,768]{2,1,0:T(1,128)}, u32[]{:S(2)}) copy-start(f32[2,1,768]{2,1,0:T(1,128)} %get-tuple-element.76) | copy-start | bytes 18436

commit v5 on v4

--- a/solution.py
+++ b/solution.py
@@ -422,29 +422,55 @@
     )(x, w, attended, low)
 
 
-def small_kernel(x_ref, xo_ref, c_send, c_recv):
+def col_peers():
     me = lax.axis_index("col")
-    peers = [{"col": (me + k) % COLS} for k in range(1, COLS)]
-    greet(peers)
+    return [{"col": (me + k) % COLS} for k in range(1, COLS)]
+
+
+def to_rows(columns):
+    lane = lax.broadcasted_iota(jnp.int32, (columns[0].shape[0], 128), 1)
+    v = jnp.zeros(lane.shape, F32)
+    for i, column in enumerate(columns):
+        v = jnp.where(lane == i, column, v)
+    return v.T[:8]
+
+
+def to_columns(lines):
+    place = lax.broadcasted_iota(jnp.int32, (8, lines[0].shape[1]), 0)
+    v = jnp.zeros(place.shape, F32)
+    for i, one in enumerate(lines):
+        v = jnp.where(place == i, one, v)
+    v = v.T
+    return [v[:, i : i + 1] for i in range(len(lines))]
+
+
+def share(snd_ref, all_ref, send, recv):
+    me = lax.axis_index("col")
     copies = []
-    for k, peer in enumerate(peers):
-        copy = push(x_ref, xo_ref.at[me], c_send.at[k], c_recv.at[k], peer)
+    for k, peer in enumerate(col_peers()):
+        copy = push(snd_ref, all_ref.at[me], send.at[k], recv.at[k], peer)
         copy.start()
         copies.append(copy)
-    xo_ref[me] = x_ref[...]
+    all_ref[me] = snd_ref[...]
     for copy in copies:
         copy.wait()
 
 
-def small_gather(x, collective):
-    return pl.pallas_call(
-        small_kernel,
-        out_shape=jax.ShapeDtypeStruct((COLS,) + x.shape, x.dtype),
-        in_specs=[VSPEC],
-        out_specs=VSPEC,
-        scratch_shapes=[DMA((COLS - 1,)), DMA((COLS - 1,))],
-        compiler_params=params(collective),
-    )(x)
+def norm_back(grad, normed, gain, rstd, snd_ref, all_ref, send, recv):
+    tokens = grad.shape[0]
+    scaled = grad * gain
+    sums = [
+        jnp.sum(scaled, axis=-1, keepdims=True),
+        jnp.sum(scaled * normed, axis=-1, keepdims=True),
+    ]
+    snd_ref[:, :tokens] = to_rows(sums)
+    share(snd_ref, all_ref, send, recv)
+    total = all_ref[0, :, :tokens]
+    for b in range(1, COLS):
+        total = total + all_ref[b, :, :tokens]
+    total = total / D
+    first, second = to_columns([total[0:1], total[1:2]])
+    return rstd * (scaled - first - normed * second)
 
 
 def line_greet(levels, row, level, partner):
@@ -700,7 +726,6 @@
     delta_ref,
     e_ref,
     bias_ref,
-    dq_ref,
     out_ref,
     eo_ref,
     part_ref,
@@ -868,11 +893,11 @@
         return carry
 
     lax.fori_loop(0, e_ref.shape[1], finish, 0)
-    dq_ref[...] = (dqt_ref[...] * HD**-0.5).T.astype(BF16)
+    out_ref[:, :width] = (dqt_ref[...] * HD**-0.5).T.astype(BF16)
 
     for i in range(pieces):
         total(level, i, not_top, (level > 0) & (level < low))
-        out_ref[pl.ds(i * step, step)] = acc_ref[...].astype(BF16)
+        out_ref[pl.ds(i * step, step), width:] = acc_ref[...].astype(BF16)
 
     for at in range(levels):
         for i in range(pieces):
@@ -901,12 +926,11 @@
     return pl.pallas_call(
         functools.partial(backward_kernel, group, low, pieces, tokens // 2),
         out_shape=(
-            jax.ShapeDtypeStruct((tokens, width), BF16),
-            jax.ShapeDtypeStruct((tokens, both), BF16),
+            jax.ShapeDtypeStruct((tokens, width + both), BF16),
             jax.ShapeDtypeStruct(e.shape[1:], BF16),
         ),
         in_specs=[SSPEC] + [VSPEC] * 7,
-        out_specs=(VSPEC,) * 3,
+        out_specs=(VSPEC,) * 2,
         scratch_shapes=[
             pltpu.VMEM(kv_all.shape, BF16),
             block,
@@ -923,91 +947,245 @@
     )(info, q, kv_all, do, lse, delta, e, bias)
 
 
-def product_kernel(pieces, rows, *refs):
-    if rows:
-        a_ref, b_ref, e_ref, out_ref, eo_ref = refs[:5]
-        snd_ref, rx_ref, far_ref, tot_ref, send, recv, e_send, e_recv = refs[5:]
-    else:
-        a_ref, b_ref, out_ref, snd_ref, rx_ref, far_ref, tot_ref, send, recv = refs
+def product(pieces, a_ref, w_ref, feats, out_ref, snd_ref, rx_ref, far_ref, tot_ref, sems, fill):
+    send, recv = sems
     me, sib, across, diag = col_places()
+    half = a_ref.shape[0] // 2
+    step = half // pieces
+    per = w_ref.shape[0] // COLS
+    width = out_ref.shape[1]
+
+    def weight(who):
+        return w_ref[pl.ds(who * per, per)].reshape(width, 4 * width)[:, feats]
+
+    def term(i, w):
+        parts = [nt(a_ref[pl.ds(n * half + i * step, step)], w) for n in range(2)]
+        return jnp.concatenate(parts, axis=1)
+
+    def near(i, j):
+        part = pl.ds(i * step, step)
+        return push(
+            snd_ref.at[j, part], rx_ref.at[j, part], send.at[j, i], recv.at[j, i], {"col": sib}
+        )
+
+    def over(i):
+        part = pl.ds(i * step, step)
+        return push(tot_ref.at[part], far_ref.at[part], send.at[2, i], recv.at[2, i], {"col": across})
+
+    w = weight(diag)
+    for i in range(pieces):
+        snd_ref[0, pl.ds(i * step, step)] = term(i, w).astype(BF16)
+        near(i, 0).start()
+    w = weight(across)
+    for i in range(pieces):
+        part = pl.ds(i * step, step)
+        mine = term(i, w)
+        near(i, 0).wait_recv()
+        tot_ref[part] = (mine + rx_ref[0, part].astype(F32)).astype(BF16)
+        over(i).start()
+    w = weight(sib)
+    for i in range(pieces):
+        snd_ref[1, pl.ds(i * step, step)] = term(i, w).astype(BF16)
+        near(i, 1).start()
+    fill()
+    w = weight(me)
+    for i in range(pieces):
+        part = pl.ds(i * step, step)
+        mine = term(i, w)
+        near(i, 1).wait_recv()
+        mine = mine + rx_ref[1, part].astype(F32)
+        over(i).wait_recv()
+        mine = mine + far_ref[part].astype(F32)
+        out_ref[part] = mine[:, :width]
+        out_ref[pl.ds(half + i * step, step)] = mine[:, width:]
+    for i in range(pieces):
+        near(i, 0).wait_send()
+        near(i, 1).wait_send()
+        over(i).wait_send()
+
+
+def product_scratch(pieces, tokens, width):
+    block = pltpu.VMEM((tokens // 2, 2 * width), BF16)
+    pair = pltpu.VMEM((2, tokens // 2, 2 * width), BF16)
+    return [pair, pair, block, block, DMA((3, pieces)), DMA((3, pieces))]
+
+
+def branch_kernel(
+    pieces,
+    a_ref,
+    w_ref,
+    x_ref,
+    bias_ref,
+    gain_ref,
+    shift_ref,
+    mid_ref,
+    normed_ref,
+    rstd_ref,
+    h_ref,
+    snd_ref,
+    rx_ref,
+    far_ref,
+    tot_ref,
+    send,
+    recv,
+    st_ref,
+    all_ref,
+    st_send,
+    st_recv,
+):
+    greet(col_peers())
+    tokens, width = x_ref.shape
+    product(
+        pieces,
+        a_ref,
+        w_ref,
+        slice(3 * width, 4 * width),
+        mid_ref,
+        snd_ref,
+        rx_ref,
+        far_ref,
+        tot_ref,
+        (send, recv),
+        lambda: None,
+    )
+    mid = x_ref[...].astype(F32) + mid_ref[...] + bias_ref[...]
+    mid_ref[...] = mid
+    part_mean = jnp.mean(mid, axis=-1, keepdims=True)
+    part_spread = jnp.sum((mid - part_mean) ** 2, axis=-1, keepdims=True)
+    st_ref[...] = to_rows([part_mean, part_spread])
+    share(st_ref, all_ref, st_send, st_recv)
+    mean = sum(all_ref[b, 0:1] for b in range(COLS)) / COLS
+    spread = sum(
+        all_ref[b, 1:2] + width * (all_ref[b, 0:1] - mean) ** 2 for b in range(COLS)
+    )
+    mean, rstd = to_columns([mean, lax.rsqrt(spread / D + epsilon)])
+    normed = (mid - mean) * rstd
+    normed_ref[...] = normed
+    rstd_ref[...] = rstd
+    h_ref[...] = (normed * gain_ref[...] + shift_ref[...]).astype(BF16)
+
+
+def branch(a, w, x, bias, gain, shift, collective):
+    pieces = 4
+    tokens, width = a.shape
+    rows = jax.ShapeDtypeStruct((tokens, width), F32)
+    return pl.pallas_call(
+        functools.partial(branch_kernel, pieces),
+        out_shape=(
+            rows,
+            rows,
+            jax.ShapeDtypeStruct((tokens, 1), F32),
+            jax.ShapeDtypeStruct((tokens, width), BF16),
+        ),
+        in_specs=[VSPEC] * 6,
+        out_specs=(VSPEC,) * 4,
+        scratch_shapes=product_scratch(pieces, tokens, width)
+        + [
+            pltpu.VMEM((8, tokens), F32),
+            pltpu.VMEM((COLS, 8, tokens), F32),
+            DMA((COLS - 1,)),
+            DMA((COLS - 1,)),
+        ],
+        compiler_params=params(collective),
+    )(a, w, x, bias, gain, shift)
+
+
+def input_kernel(
+    pieces,
+    a_ref,
+    w_ref,
+    e_ref,
+    h_ref,
+    gwo_ref,
+    mid_ref,
+    normed_ref,
+    rstd_ref,
+    gain_ref,
+    vec_ref,
+    gin_ref,
+    eo_ref,
+    wt_ref,
+    all_ref,
+    grad_ref,
+    snd_ref,
+    rx_ref,
+    far_ref,
+    tot_ref,
+    send,
+    recv,
+    st_ref,
+    st_send,
+    st_recv,
+    e_send,
+    e_recv,
+):
+    rows = e_ref.shape[0]
     row = lax.axis_index("row")
     order = far_first(rows)
-    greet([{"row": (row + k) % rows} for k in order] + [{"col": sib}, {"col": across}])
+    greet([{"row": (row + k) % rows} for k in order] + col_peers())
     home = []
     for n, k in enumerate(order):
         peer = (row + k) % rows
         copy = push(e_ref.at[peer], eo_ref.at[row], e_send.at[n], e_recv.at[n], {"row": peer})
         copy.start()
         home.append(copy)
-    if rows:
-        eo_ref[row] = e_ref[row]
-    half = a_ref.shape[0] // 2
-    step = half // pieces
-
-    def term(i, who):
-        parts = [nt(a_ref[pl.ds(n * half + i * step, step)], b_ref[who]) for n in range(2)]
-        return jnp.concatenate(parts, axis=1)
-
-    def near(i, j):
-        part = pl.ds(i * step, step)
-        return push(
-            snd_ref.at[j, part], rx_ref.at[j, part], send.at[j, i], recv.at[j, i], {"col": sib}
-        )
-
-    def over(i):
-        part = pl.ds(i * step, step)
-        return push(tot_ref.at[part], far_ref.at[part], send.at[2, i], recv.at[2, i], {"col": across})
-
-    for i in range(pieces):
-        snd_ref[0, pl.ds(i * step, step)] = term(i, diag).astype(BF16)
-        near(i, 0).start()
-    for i in range(pieces):
-        part = pl.ds(i * step, step)
-        mine = term(i, across)
-        near(i, 0).wait_recv()
-        tot_ref[part] = (mine + rx_ref[0, part].astype(F32)).astype(BF16)
-        over(i).start()
-    for i in range(pieces):
-        snd_ref[1, pl.ds(i * step, step)] = term(i, sib).astype(BF16)
-        near(i, 1).start()
-    for i in range(pieces):
-        part = pl.ds(i * step, step)
-        mine = term(i, me)
-        near(i, 1).wait_recv()
-        mine = mine + rx_ref[1, part].astype(F32)
-        over(i).wait_recv()
-        mine = mine + far_ref[part].astype(F32)
-        width = mine.shape[1] // 2
-        out_ref[part] = mine[:, :width]
-        out_ref[pl.ds(half + i * step, step)] = mine[:, width:]
-    for i in range(pieces):
-        near(i, 0).wait_send()
-        near(i, 1).wait_send()
-        over(i).wait_send()
+    eo_ref[row] = e_ref[row]
+    tokens, width = grad_ref.shape
+
+    def fill():
+        both = [tn(h_ref[...], a_ref[...]).astype(BF16), gwo_ref[...]]
+        wt_ref[...] = jnp.concatenate(both, axis=1)
+
+    product(
+        pieces,
+        a_ref,
+        w_ref,
+        slice(0, 3 * width),
+        grad_ref,
+        snd_ref,
+        rx_ref,
+        far_ref,
+        tot_ref,
+        (send, recv),
+        fill,
+    )
+    grad, normed = grad_ref[...], normed_ref[...]
+    st_ref[:, tokens:] = jnp.zeros((8, st_ref.shape[1] - tokens), F32)
+    st_ref[0:1, tokens : tokens + width] = jnp.sum(grad * normed, axis=0, keepdims=True)
+    st_ref[1:2, tokens : tokens + width] = jnp.sum(grad, axis=0, keepdims=True)
+    st_ref[2:5, tokens : tokens + width] = vec_ref[0:3]
+    gin_ref[...] = mid_ref[...] + norm_back(
+        grad, normed, gain_ref[...], rstd_ref[...], st_ref, all_ref, st_send, st_recv
+    )
     for copy in home:
         copy.wait()
 
 
-def product_scatter(a, b, collective, back=None):
+def input_gradient(a, w, e, h, gwo, mid, normed, rstd, gain, vec, collective):
     pieces = 4
-    tokens, width = a.shape[0], b.shape[1]
-    block = pltpu.VMEM((tokens // 2, 2 * width), BF16)
-    pair = pltpu.VMEM((2, tokens // 2, 2 * width), BF16)
-    out = jax.ShapeDtypeStruct((tokens, width), F32)
-    scratch = [pair, pair, block, block, DMA((3, pieces)), DMA((3, pieces))]
-    rows = 0
-    if back is not None:
-        rows = back.shape[0]
-        out = (out, jax.ShapeDtypeStruct(back.shape, back.dtype))
-        scratch = scratch + [DMA((rows - 1,))] * 2
+    tokens, width = mid.shape
+    wide = tokens + 256
     return pl.pallas_call(
-        functools.partial(product_kernel, pieces, rows),
-        out_shape=out,
-        in_specs=[VSPEC] * (3 if rows else 2),
-        out_specs=(VSPEC, VSPEC) if rows else VSPEC,
-        scratch_shapes=scratch,
+        functools.partial(input_kernel, pieces),
+        out_shape=(
+            jax.ShapeDtypeStruct((tokens, width), F32),
+            jax.ShapeDtypeStruct(e.shape, BF16),
+            jax.ShapeDtypeStruct((D, 4 * width), BF16),
+            jax.ShapeDtypeStruct((COLS, 8, wide), F32),
+        ),
+        in_specs=[VSPEC] * 10,
+        out_specs=(VSPEC,) * 4,
+        scratch_shapes=[pltpu.VMEM((tokens, width), F32)]
+        + product_scratch(pieces, tokens, width)
+        + [
+            pltpu.VMEM((8, wide), F32),
+            DMA((COLS - 1,)),
+            DMA((COLS - 1,)),
+            DMA((e.shape[0] - 1,)),
+            DMA((e.shape[0] - 1,)),
+        ],
         compiler_params=params(collective),
-    )(*((a, b, back) if rows else (a, b)))
+    )(a, w, e, h, gwo, mid, normed, rstd, gain, vec)
 
 
 def dispatch_kernel(rows, x_ref, t_ref, out_ref, in_ref, r_send, r_recv, c_send, c_recv):
@@ -1086,21 +1264,31 @@
     rows,
     in_ref,
     t_ref,
+    cot_ref,
+    normed_ref,
+    rstd_ref,
+    gain_ref,
+    mid_ref,
+    vec_ref,
     sum_ref,
     out_ref,
     rx_ref,
     far_ref,
     tot_ref,
     fin_ref,
+    st_ref,
+    all_ref,
     send,
     recv,
     r_send,
     r_recv,
+    st_send,
+    st_recv,
 ):
     me, sib, across, diag = col_places()
     row = lax.axis_index("row")
     order = [(row + k) % rows for k in far_first(rows)] + [row]
-    greet([{"row": p} for p in order[:-1]] + [{"col": sib}, {"col": across}])
+    greet([{"row": p} for p in order[:-1]] + col_peers())
 
     def near(k, j):
         who = diag if j == 0 else sib
@@ -1144,6 +1332,15 @@
         source = (row + rows - gap) % rows
         home(k).wait_recv()
         sum_ref[...] += combined(t_ref, out_ref[source], source, cap)
+    grad, normed = sum_ref[...], normed_ref[...]
+    mid = cot_ref[...].astype(F32) + norm_back(
+        grad, normed, gain_ref[...], rstd_ref[...], st_ref, all_ref, st_send, st_recv
+    )
+    mid_ref[...] = mid
+    vec_ref[...] = jnp.zeros(vec_ref.shape, F32)
+    vec_ref[0:1] = jnp.sum(grad * normed, axis=0, keepdims=True)
+    vec_ref[1:2] = jnp.sum(grad, axis=0, keepdims=True)
+    vec_ref[2:3] = jnp.sum(mid, axis=0, keepdims=True)
     for k in range(rows):
         near(k, 0).wait_send()
         near(k, 1).wait_send()
@@ -1152,71 +1349,133 @@
             home(k).wait_send()
 
 
-def giveback(parts, target, rows, collective):
+def giveback(parts, target, cot, normed, rstd, gain, rows, collective):
     block = parts.shape[2:]
     one = pltpu.VMEM((rows,) + block, BF16)
     return pl.pallas_call(
         functools.partial(giveback_kernel, rows),
-        out_shape=jax.ShapeDtypeStruct((target.shape[1], block[1] // 2), F32),
-        in_specs=[VSPEC] * 2,
-        out_specs=VSPEC,
+        out_shape=(
+            jax.ShapeDtypeStruct(cot.shape, F32),
+            jax.ShapeDtypeStruct((8, cot.shape[1]), F32),
+        ),
+        in_specs=[VSPEC] * 6,
+        out_specs=(VSPEC,) * 2,
         scratch_shapes=[
+            pltpu.VMEM(cot.shape, F32),
             one,
             pltpu.VMEM((2, rows) + block, BF16),
             one,
             one,
             one,
+            pltpu.VMEM((8, cot.shape[0]), F32),
+            pltpu.VMEM((COLS, 8, cot.shape[0]), F32),
             DMA((3, rows)),
             DMA((3, rows)),
             DMA((rows - 1,)),
             DMA((rows - 1,)),
+            DMA((COLS - 1,)),
+            DMA((COLS - 1,)),
         ],
         compiler_params=params(collective),
-    )(parts, target)
+    )(parts, target, cot, normed, rstd, gain)
 
 
 def end_kernel(
-    rows, w_ref, s_ref, e_ref, t_ref, mid_ref, wo_ref, so_ref, lo_ref, wr_ref, sr_ref, send, recv
+    rows,
+    w_ref,
+    s_ref,
+    e_ref,
+    t_ref,
+    mid_ref,
+    wo_ref,
+    so_ref,
+    lo_ref,
+    px_ref,
+    pt_ref,
+    wr_ref,
+    sr_ref,
+    p_send,
+    p_recv,
+    l_send,
+    l_recv,
+    send,
+    recv,
 ):
-    row = lax.axis_index("row")
-    peers = [(row + k) % rows for k in range(1, rows)]
+    row, _, level, side, partner = line_places(rows)
+    levels = rows // 2
+    peers = [(row + k) % rows for k in far_first(rows)]
     greet([{"row": p} for p in peers])
+    gaps = far_first(levels)
+    targets = [(level + k) % levels for k in gaps] + [level]
+
+    def cross(n):
+        src = w_ref.at[2 * targets[n] + 1 - side]
+        return push(src, px_ref.at[n], p_send.at[n], p_recv.at[n], {"row": partner})
+
+    def along(n):
+        peer = {"row": 2 * targets[n] + side}
+        return push(pt_ref.at[n], wr_ref.at[n], l_send.at[n], l_recv.at[n], peer)
+
+    def total(n):
+        return w_ref[2 * targets[n] + side].astype(F32) + px_ref[n].astype(F32)
+
+    for n in range(levels):
+        cross(n).start()
     copies = []
     for k, peer in enumerate(peers):
-        for j, (src, dst) in enumerate(((w_ref, wr_ref), (s_ref, sr_ref))):
-            copy = push(src.at[peer], dst.at[k], send.at[j, k], recv.at[j, k], {"row": peer})
-            copy.start()
-            copies.append(copy)
-    wo_ref[...] = w_ref[row].astype(F32)
-    so_ref[...] = s_ref[row]
-    total = mid_ref[...]
+        copy = push(s_ref.at[peer], sr_ref.at[k], send.at[k], recv.at[k], {"row": peer})
+        copy.start()
+        copies.append(copy)
+    for n in range(levels - 1):
+        cross(n).wait_recv()
+        pt_ref[n] = total(n).astype(BF16)
+        along(n).start()
+    result = mid_ref[...]
     for r in range(rows):
-        total = total + combined(t_ref, e_ref[r], r, e_ref.shape[1])
-    lo_ref[...] = total.astype(BF16)
-    for k in range(rows - 1):
-        copies[2 * k].wait_recv()
-        copies[2 * k + 1].wait_recv()
-        wo_ref[...] += wr_ref[k].astype(F32)
-        so_ref[...] += sr_ref[k]
+        result = result + combined(t_ref, e_ref[r], r, e_ref.shape[1])
+    lo_ref[...] = result.astype(BF16)
+    small = s_ref[row]
+    for k, copy in enumerate(copies):
+        copy.wait_recv()
+        small = small + sr_ref[k]
+    so_ref[...] = small
+    cross(levels - 1).wait_recv()
+    mine = total(levels - 1)
+    for n in range(levels - 1):
+        along(n).wait_recv()
+        mine = mine + wr_ref[n].astype(F32)
+    wo_ref[...] = mine
+    for n in range(levels):
+        cross(n).wait_send()
+        if n < levels - 1:
+            along(n).wait_send()
     for copy in copies:
         copy.wait_send()
 
 
 def end_scatter(w, s, outs, target, mid, rows, collective):
+    levels = rows // 2
+    one = w.shape[1:]
     return pl.pallas_call(
         functools.partial(end_kernel, rows),
         out_shape=(
-            jax.ShapeDtypeStruct(w.shape[1:], F32),
+            jax.ShapeDtypeStruct(one, F32),
             jax.ShapeDtypeStruct(s.shape[1:], F32),
             jax.ShapeDtypeStruct(mid.shape, BF16),
         ),
         in_specs=[VSPEC] * 5,
         out_specs=(VSPEC,) * 3,
         scratch_shapes=[
-            pltpu.VMEM((rows - 1,) + w.shape[1:], w.dtype),
+            pltpu.VMEM((levels,) + one, w.dtype),
+            pltpu.VMEM((levels - 1,) + one, w.dtype),
+            pltpu.VMEM((levels - 1,) + one, w.dtype),
             pltpu.VMEM((rows - 1,) + s.shape[1:], s.dtype),
-            DMA((2, rows - 1)),
-            DMA((2, rows - 1)),
+            DMA((levels,)),
+            DMA((levels,)),
+            DMA((levels - 1,)),
+            DMA((levels - 1,)),
+            DMA((rows - 1,)),
+            DMA((rows - 1,)),
         ],
         compiler_params=params(collective),
     )(w, s, outs, target, mid)
@@ -1373,9 +1632,6 @@
     x_all, g_own, w_all, s_all = start_gather(
         layer_in, cotangent, target, weights, small, rows, capacity
     )
-    w_flat = w_all.reshape(D, 4 * width)
-    w_qkv = w_flat[:, : 3 * width]
-    w_out = w_flat[:, 3 * width :].reshape(COLS, width, width)
     gain_one, shift_one, gain_two, shift_two, out_bias = (
         s_all[:, i, :share].reshape(D) for i in range(5)
     )
@@ -1401,38 +1657,28 @@
     kv_all, attended, attended_low, lse, g_all = attention_forward(
         info, queries, keys_values, g_own, group, low, 1
     )
-    branch = product_scatter(attended_low, w_out, 2)
-    x_own = layer_in.astype(F32)
-    mid = x_own + branch + own(out_bias)
-
-    part_mean = jnp.mean(mid, axis=-1)
-    part_spread = jnp.sum((mid - part_mean[:, None]) ** 2, axis=-1)
-    stats = jnp.stack([part_mean, part_spread]).reshape(-1, 128)
-    stats = small_gather(stats, 3).reshape(COLS, 2, tokens)
-    mean_two = jnp.mean(stats[:, 0], axis=0)
-    spread = jnp.sum(stats[:, 1] + width * (stats[:, 0] - mean_two) ** 2, axis=0) / D
-    rstd_two = lax.rsqrt(spread + epsilon)[:, None]
-    normed_two = (mid - mean_two[:, None]) * rstd_two
-    gain_two_own = own(gain_two)
-    h_two = (normed_two * gain_two_own + own(shift_two)).astype(BF16)
+    gain_two_own = own(gain_two)[None]
+    mid, normed_two, rstd_two, h_two = branch(
+        attended_low,
+        w_all,
+        layer_in,
+        own(out_bias)[None],
+        gain_two_own,
+        own(shift_two)[None],
+        2,
+    )
 
     received = dispatch(h_two, target, rows, capacity, 4)
     parts, grad_parts, grad_w_up, grad_bias_up, grad_w_down, grad_bias_down = experts(
         received, g_all, w_up, bias_up, w_down
     )
-    grad_h_two = giveback(grad_parts, target, rows, 5)
-
-    scaled = grad_h_two * gain_two_own
-    sums = jnp.stack([jnp.sum(scaled, axis=-1), jnp.sum(scaled * normed_two, axis=-1)])
-    sums = small_gather(sums.reshape(-1, 128), 6).reshape(COLS, 2, tokens)
-    sums = jnp.sum(sums, axis=0) / D
-    grad_mid = cotangent.astype(F32) + rstd_two * (
-        scaled - sums[0][:, None] - normed_two * sums[1][:, None]
+    grad_mid, vectors = giveback(
+        grad_parts, target, cotangent, normed_two, rstd_two, gain_two_own, rows, 5
     )
     grad_attended, delta, grad_w_out = mid_gradient(grad_mid, w_all, attended, attended_low, 7)
     down_own = lax.dynamic_slice_in_dim(bias_down, col * width, width, 1).astype(F32)
     down_own = down_own.reshape(1, EXP_DEV * width)
-    grad_q, grad_kv, outs = attention_backward(
+    grad_qkv, outs = attention_backward(
         info,
         queries,
         kv_all,
@@ -1445,29 +1691,21 @@
         low,
         8,
     )
-    grad_qkv = jnp.concatenate([grad_q, grad_kv], axis=1)
-    grad_w_qkv = lax.dot_general(
-        h_one, grad_qkv, (((0,), (0,)), ((), ())), preferred_element_type=F32
-    )
     grad_bias = jnp.sum(grad_qkv, axis=0, dtype=F32)
-    grad_h_one, outs = product_scatter(grad_qkv, w_qkv.reshape(COLS, width, 3 * width), 9, outs)
-    scaled = grad_h_one * own(gain_one)
-    sums = jnp.stack([jnp.sum(scaled, axis=-1), jnp.sum(scaled * normed_one, axis=-1)])
-    vectors = jnp.stack(
-        [
-            jnp.sum(grad_h_one * normed_one, axis=0),
-            jnp.sum(grad_h_one, axis=0),
-            jnp.sum(grad_h_two * normed_two, axis=0),
-            jnp.sum(grad_h_two, axis=0),
-            jnp.sum(grad_mid, axis=0),
-        ]
-    )
-    vectors = jnp.pad(vectors, ((0, 3), (0, 256 - width))).reshape(-1, 128)
-    shared = small_gather(jnp.concatenate([sums.reshape(-1, 128), vectors]), 10)
-    used = 2 * tokens // 128
-    sums = jnp.sum(shared[:, :used].reshape(COLS, 2, tokens), axis=0) / D
-    grad_in = grad_mid + rstd_one * (scaled - sums[0][:, None] - normed_one * sums[1][:, None])
-    vectors = shared[:, used:].reshape(COLS, 8, 256)[:, :5, :width]
+    grad_in, outs, weight_terms, shared = input_gradient(
+        grad_qkv,
+        w_all,
+        outs,
+        h_one,
+        grad_w_out,
+        grad_mid,
+        normed_one,
+        rstd_one,
+        own(gain_one)[None],
+        vectors,
+        9,
+    )
+    vectors = shared[:, :5, tokens : tokens + width]
     vectors = vectors.transpose(1, 0, 2).reshape(5, rows, share).transpose(1, 0, 2)
 
     def by_row(v):
@@ -1483,7 +1721,6 @@
         ],
         axis=1,
     )
-    weight_terms = jnp.concatenate([grad_w_qkv.astype(BF16), grad_w_out], axis=1)
     weight_terms = weight_terms.reshape(rows, share, 4 * width)
     weight_sums, small_sums, layer_out = end_scatter(
         weight_terms, small_terms, outs, target, mid, rows, 11

time: 495 us -> 461 us (0.931)
  other arithmetic: 22.2 us -> 5.85 us
  Pallas kernels: 428 us -> 414 us
    pallas_call x1, Pallas kernels: 32.7 us -> 22.5 us  [end_scatter(): pl.pallas_call(functools.partial(end_kernel, rows), out_shape=(jax.ShapeD...]
    reduce_sum x8 -> x0, other arithmetic: 8.79 us -> none  [the longest x1 2.04 us: per_device(): jnp.sum(grad_h_two * normed_two, axis=0)]
    pallas_call x6 -> x3, Pallas kernels: 89.1 us -> 86.3 us  [the longest x1 38.2 us: giveback(): pl.pallas_call(functools.partial(giveback_kernel, rows), out_shape=(jax.S...]
where the time goes in v5:
time: 461 us; the launch traced here: 452 us
  Pallas kernels  414 us (90%)
  local copies, waits for them, and re-layouts  29.5 us (6%)
  other arithmetic  5.85 us (1%)
    pallas_call x1, Pallas kernels, attention_backward(): pl.pallas_call(functools.partial(backward_kernel, group, low, pieces, tok...  84 us
    pallas_call x1, Pallas kernels, dispatch(): pl.pallas_call(functools.partial(dispatch_kernel, rows), out_shape=jax.Sh...  79.5 us
    pallas_call x1, Pallas kernels, attention_forward(): pl.pallas_call(functools.partial(forward_kernel, group, low, pieces, toke...  55.2 us
    pallas_call x1, Pallas kernels, giveback(): pl.pallas_call(functools.partial(giveback_kernel, rows), out_shape=(jax.S...  38.2 us
    pallas_call x1, Pallas kernels, start_gather(): pl.pallas_call(functools.partial(start_kernel, rows, pieces), out_shape=(...  33.8 us
    pallas_call x1, Pallas kernels, experts(): pl.pallas_call(expert_kernel, grid=(count,), out_shape=(jax.ShapeDtypeStr...  30.1 us
    pallas_call x1, Pallas kernels, input_gradient(): pl.pallas_call(functools.partial(input_kernel, pieces), out_shape=(jax.Sh...  27.3 us
    pallas_call x1, Pallas kernels, end_scatter(): pl.pallas_call(functools.partial(end_kernel, rows), out_shape=(jax.ShapeD...  22.5 us

profile of v5, /device:TPU:10, one launch (start us, length us, event | category | flops | bytes accessed | tf_op | source)
XLA Modules:
  0.0 451.9 jit_solution(14354129248954124994)
XLA Ops:
  0.7 0.0 copy-start
  1.5 0.8 convert_element_type.52
  2.3 0.8 convert_element_type.54
  3.1 0.7 bitcast_convert_fusion.6
  3.7 0.1 pad.54.clone
  3.8 0.7 bitcast_convert_fusion.4
  4.5 0.7 bitcast_convert_fusion.2
  5.1 0.6 stack.59.s_ref
  5.8 0.8 dynamic-slice_convert_fusion
  6.5 0.6 reshape.146.bias_ref
  7.2 0.7 fusion.7
  7.9 6.2 %gather_fusion = s32[1024]{0:T(1024)S(1)} fusion(s32[50304]{0:T(1024)S(1)} %copy-done, s32[1024]{0:T(1024)S(1)} %fusion.7), kind=kCustom, calls=%fused_computation | custom fusion | bytes 12288 | tf_op jit(solution)/shard_map/gather | solution.py:1621
  14.0 0.5 fusion.2
  14.5 0.6 convert_add_fusion
  15.1 0.6 copy.48.bias_ref
  15.7 0.8 pad_maximum_fusion.w_ref
  16.5 1.0 copy.43.x_ref
  17.5 1.0 copy.44.g_ref.cot_ref
  18.5 33.8 %shard_map.323 = (bf16[4,512,384]{2,1,0:T(8,128)(2,1)}, bf16[8,128,384]{2,1,0:T(8,128)(2,1)}, bf16[8,96,768]{2,1,0:T(8,128)(2,1)}, f32[8,8,128]{2,1,0:T(8,128)}) custom-call(bf16[1024,192]{1,0:T(8,128)(2,1)} %copy.43.x_ref, bf16[1024,192]{1,0:T(8,128)(2,1)} %copy.44.g_ref.cot_ref, s32[1,1024]{1,0:T(1,128)} %bitcast.64, ...), custom_call_target="tpu_custom_call" | custom-call | tf_op jit(solution)/shard_map/pallas_call | solution.py:268
  52.3 0.9 slice_reduce_fusion.4
  53.1 1.0 slice_reduce_fusion
  54.2 0.1 reshape_squeeze.22
  54.2 0.6 dynamic_slice.17
  54.9 0.7 broadcast_in_dim_reshape_squeeze.6.gain_ref
  55.5 0.7 broadcast_in_dim_reshape_squeeze.7.shift_ref
  56.2 0.1 reshape_squeeze.21
  56.3 0.6 dynamic_slice.16
  56.9 0.1 reshape_squeeze.20
  57.0 0.6 dynamic_slice.15
  57.6 0.1 reshape_squeeze.23
  57.7 0.7 dynamic_slice.19
  58.3 0.1 reshape_squeeze.18
  58.4 0.1 reshape.125
  58.5 0.1 reshape_squeeze.19
  58.6 0.1 reshape.126
  58.7 0.1 pad_maximum_fusion.1
  58.8 0.6 broadcast_in_dim.38.bias_ref
  59.4 6.4 %shard_map.324 = (bf16[1024,192]{1,0:T(8,128)(2,1)}, bf16[1024,384]{1,0:T(8,128)(2,1)}, bf16[1024,768]{1,0:T(8,128)(2,1)}, f32[1024,192]{1,0:T(8,128)}, f32[1024,1]{1,0:T(8,128)}) custom-call(bf16[4,512,384]{2,1,0:T(8,128)(2,1)} %get-tuple-element.55.x_ref, bf16[8,96,768]{2,1,0:T(8,128)(2,1)} %get-tuple-element.56.w_ref, ...), custom_call_target="tpu_custom_call" | custom-call | tf_op jit(solution)/shard_map/pallas_call | solution.py:318
  65.7 55.2 %shard_map.325 = (bf16[8,1024,384]{2,1,0:T(8,128)(2,1)}, f32[1024,192]{1,0:T(8,128)}, bf16[1024,192]{1,0:T(8,128)(2,1)}, f32[8,1024]{1,0:T(8,128)}, bf16[4,8,128,384]{3,2,1,0:T(8,128)(2,1)}) custom-call(s32[1]{0:T(128)S(6)} %select_n.24.info_ref, bf16[1024,192]{1,0:T(8,128)(2,1)} %get-tuple-element.58.q_ref, bf16[1024,384]{1,0:T(8,128)(2,1)} %get-tuple-element.59.kv_ref, ...), custom_call_target="tpu_custom_call" | custom-call | tf_op jit(solution)/shard_map/pallas_call | solution.py:695
  121.0 20.8 %shard_map.326 = (f32[1024,192]{1,0:T(8,128)}, f32[1024,192]{1,0:T(8,128)}, f32[1024,1]{1,0:T(8,128)}, bf16[1024,192]{1,0:T(8,128)(2,1)}) custom-call(bf16[1024,192]{1,0:T(8,128)(2,1)} %get-tuple-element.62.a_ref.low_ref, bf16[8,96,768]{2,1,0:T(8,128)(2,1)} %get-tuple-element.56.w_ref, bf16[1024,192]{1,0:T(8,128)(2,1)} %copy.43.x_ref, f32[1,192]{1,0:T(1,128)} %bitcast.81, ...), custom_call_target="tpu_custom_call" | custom-call | tf_op jit(solution)/shard_map/pallas_call | solution.py:1072
  141.7 79.5 %shard_map.327.x_ref = bf16[4,8,128,384]{3,2,1,0:T(8,128)(2,1)} custom-call(bf16[1024,192]{1,0:T(8,128)(2,1)} %get-tuple-element.63.x_ref, s32[1,1024]{1,0:T(1,128)} %bitcast.65), custom_call_target="tpu_custom_call" | custom-call | tf_op jit(solution)/shard_map/pallas_call | solution.py:1247
  221.2 30.1 %shard_map.328 = (bf16[4,8,128,384]{3,2,1,0:T(8,128)(2,1)}, bf16[4,8,128,384]{3,2,1,0:T(8,128)(2,1)}, f32[2,768,768]{2,1,0:T(8,128)}, f32[2,1,768]{2,1,0:T(1,128...) custom-call(bf16[4,8,128,384]{3,2,1,0:T(8,128)(2,1)} %shard_map.327.x_ref, ...), custom_call_target="tpu_custom_call" | custom-call | tf_op jit(solution)/shard_map/pallas_call | solution.py:1541
  251.3 38.2 %shard_map.329 = (f32[1024,192]{1,0:T(8,128)}, f32[8,192]{1,0:T(8,128)}) custom-call(bf16[4,8,128,384]{3,2,1,0:T(8,128)(2,1)} %get-tuple-element.65.in_ref, s32[1,1024]{1,0:T(1,128)} %bitcast.66, bf16[1024,192]{1,0:T(8,128)(2,1)} %copy.44.g_ref.cot_ref, f32[1024,192]{1,0:T(8,128)} %get-tuple-element.66.normed_ref, f32[1024,1]{1,0:T(8,128)} %get-tuple-element.67.rstd_ref, ...), custom_call_target="tpu_custom_call" | custom-call | tf_op jit(solution)/shard_map/pallas_call | solution.py:1355
  289.5 16.5 %shard_map.330 = (bf16[1024,192]{1,0:T(8,128)(2,1)}, f32[8,1024]{1,0:T(8,128)}, bf16[768,192]{1,0:T(8,128)(2,1)}) custom-call(f32[1024,192]{1,0:T(8,128)} %get-tuple-element.68.x_ref.mid_ref, bf16[8,96,768]{2,1,0:T(8,128)(2,1)} %get-tuple-element.56.w_ref, f32[1024,192]{1,0:T(8,128)} %get-tuple-element.69.att_ref, ...), custom_call_target="tpu_custom_call" | custom-call | tf_op jit(solution)/shard_map/pallas_call | solution.py:405
  306.0 84.0 %shard_map.331 = (bf16[1024,576]{1,0:T(8,128)(2,1)}, bf16[8,128,384]{2,1,0:T(8,128)(2,1)}) custom-call(s32[1]{0:T(128)S(6)} %select_n.24.info_ref, bf16[1024,192]{1,0:T(8,128)(2,1)} %get-tuple-element.58.q_ref, bf16[8,1024,384]{2,1,0:T(8,128)(2,1)} %get-tuple-element.61.kv_ref, bf16[1024,192]{1,0:T(8,128)(2,1)} %get-tuple-element.70.do_ref, ...), custom_call_target="tpu_custom_call" | custom-call | tf_op jit(solution)/shard_map/pallas_call | solution.py:926
  390.0 27.3 %shard_map.332 = (f32[1024,192]{1,0:T(8,128)}, bf16[8,128,384]{2,1,0:T(8,128)(2,1)}, bf16[768,768]{1,0:T(8,128)(2,1)}, f32[4,8,1280]{2,1,0:T(8,128)}) custom-call(bf16[1024,576]{1,0:T(8,128)(2,1)} %get-tuple-element.74.a_ref, bf16[8,96,768]{2,1,0:T(8,128)(2,1)} %get-tuple-element.56.w_ref, bf16[8,128,384]{2,1,0:T(8,128)(2,1)} %get-tuple-element.75.e_ref, ...), custom_call_target="tpu_custom_call" | custom-call | tf_op jit(solution)/shard_map/pallas_call | solution.py:1168
  417.4 0.3 convert_reduce_fusion
  417.7 0.6 copy.65
  418.3 0.6 copy.64
  418.9 0.1 reshape.132
  418.9 0.1 reshape.133
  419.0 0.1 reshape.134
  419.1 0.1 reshape.135
  419.2 0.8 slice_bitcast_fusion
  420.0 0.1 reshape.131
  420.1 0.7 fusion.3.s_ref
  420.8 22.5 %shard_map.333 = (f32[96,768]{1,0:T(8,128)}, f32[8,128]{1,0:T(8,128)}, bf16[1024,192]{1,0:T(8,128)(2,1)}) custom-call(bf16[8,96,768]{2,1,0:T(8,128)(2,1)} %bitcast.62, f32[8,8,128]{2,1,0:T(8,128)} %fusion.3.s_ref, bf16[8,128,384]{2,1,0:T(8,128)(2,1)} %get-tuple-element.83.e_ref, s32[1,1024]{1,0:T(1,128)} %bitcast.67, f32[1024,192]{1,0:T(8,128)} %get-tuple-element.84.mid_ref), custom_call_target="tpu_custom_call" | custom-call | tf_op jit(solution)/shard_map/pallas_call | solution.py:1459
  443.2 2.0 copy.56
  445.2 0.8 slice_reduce_fusion.6
  446.0 1.4 slice_bitcast_fusion.1
  447.3 0.7 reshape.137
  448.0 0.7 reshape.136
  448.7 1.9 fusion.8
  450.5 1.2 copy.57
  (33 shorter events, 0.1 us)
Async XLA Ops:
  0.7 7.2 %copy-start = (s32[50304]{0:T(1024)S(1)}, s32[50304]{0:T(1024)}, u32[]{:S(2)}) copy-start(s32[50304]{0:T(1024)} %param.23) | copy-start | bytes 603652
  0.7 14.4 %copy-start.11 = (bf16[2,768]{1,0:T(2,128)(2,1)S(1)}, bf16[2,768]{1,0:T(2,128)(2,1)}, u32[]{:S(2)}) copy-start(bf16[2,768]{1,0:T(2,128)(2,1)} %param.37) | copy-start | bytes 9220
  0.7 15.0 %copy-start.5 = (bf16[96,192]{1,0:T(8,128)(2,1)S(1)}, bf16[96,192]{1,0:T(8,128)(2,1)}, u32[]{:S(2)}) copy-start(bf16[96,192]{1,0:T(8,128)(2,1)} %param.28) | copy-start | bytes 110596
  0.7 15.0 %copy-start.6 = (bf16[96,192]{1,0:T(8,128)(2,1)S(1)}, bf16[96,192]{1,0:T(8,128)(2,1)}, u32[]{:S(2)}) copy-start(bf16[96,192]{1,0:T(8,128)(2,1)} %param.27) | copy-start | bytes 110596
  0.7 15.0 %copy-start.7 = (bf16[96,192]{1,0:T(8,128)(2,1)S(1)}, bf16[96,192]{1,0:T(8,128)(2,1)}, u32[]{:S(2)}) copy-start(bf16[96,192]{1,0:T(8,128)(2,1)} %param.26) | copy-start | bytes 110596
  0.7 15.0 %copy-start.8 = (bf16[96,192]{1,0:T(8,128)(2,1)S(1)}, bf16[96,192]{1,0:T(8,128)(2,1)}, u32[]{:S(2)}) copy-start(bf16[96,192]{1,0:T(8,128)(2,1)} %param.25) | copy-start | bytes 110596
  0.7 15.8 %copy-start.3 = (bf16[1024,192]{0,1:T(8,128)(2,1)S(1)}, bf16[1024,192]{0,1:T(8,128)(2,1)}, u32[]{:S(2)}) copy-start(bf16[1024,192]{0,1:T(8,128)(2,1)} %param.20) | copy-start | bytes 1179652
  7.8 9.7 %copy-start.4 = (bf16[1024,192]{0,1:T(8,128)(2,1)S(1)}, bf16[1024,192]{0,1:T(8,128)(2,1)}, u32[]{:S(2)}) copy-start(bf16[1024,192]{0,1:T(8,128)(2,1)} %param.21) | copy-start | bytes 1179652
  390.0 27.4 %copy-start.1 = (bf16[1024,576]{1,0:T(8,128)(2,1)S(1)}, bf16[1024,576]{1,0:T(8,128)(2,1)}, u32[]{:S(2)}) copy-start(bf16[1024,576]{1,0:T(8,128)(2,1)} %get-tuple-element.74.a_ref) | copy-start | bytes 3538948
  390.0 27.6 %copy-start.10 = (f32[2,1,768]{2,1,0:T(1,128)S(1)}, f32[2,1,768]{2,1,0:T(1,128)}, u32[]{:S(2)}) copy-start(f32[2,1,768]{2,1,0:T(1,128)} %get-tuple-element.90) | copy-start | bytes 18436
  390.0 28.2 %copy-start.9 = (f32[2,1,768]{2,1,0:T(1,128)S(1)}, f32[2,1,768]{2,1,0:T(1,128)}, u32[]{:S(2)}) copy-start(f32[2,1,768]{2,1,0:T(1,128)} %get-tuple-element.92) | copy-start | bytes 18436
  417.4 33.2 %copy-start.2 = (f32[1024,192]{1,0:T(8,128)S(1)}, f32[1024,192]{1,0:T(8,128)}, u32[]{:S(2)}) copy-start(f32[1024,192]{1,0:T(8,128)} %get-tuple-element.111) | copy-start | bytes 2359300

commit v6 on v5

--- a/solution.py
+++ b/solution.py
@@ -90,6 +90,43 @@
     return jnp.concatenate([v[:half], v[half:]], axis=1)
 
 
+def number(shape, axis):
+    return lax.broadcasted_iota(jnp.int32, shape, axis)
+
+
+def route(ids, table, experts, cap):
+    tokens = ids.shape[1]
+    pick = jnp.where(number((table.shape[0], tokens), 0) == ids >> 7, 1.0, 0.0).astype(BF16)
+    found = tn(table, pick)
+    expert = jnp.where(number((128, tokens), 0) == ids & 127, found, 0.0)
+    expert = jnp.sum(expert, axis=0, keepdims=True)
+    hit = number((experts, tokens), 0).astype(F32) == expert
+    pair = (tokens, tokens)
+    earlier = jnp.where(number(pair, 0) < number(pair, 1), 1.0, 0.0).astype(BF16)
+    before = nn(jnp.where(hit, 1.0, 0.0).astype(BF16), earlier)
+    slot = jnp.sum(jnp.where(hit, before, 0.0), axis=0, keepdims=True)
+    return (expert * cap + slot).astype(jnp.int32)
+
+
+def all_features(s_ref, i):
+    rows = s_ref.shape[0]
+    return jnp.concatenate([s_ref[r, i : i + 1, : D // rows] for r in range(rows)], axis=1)
+
+
+def own_features(s_ref, i):
+    rows = s_ref.shape[0]
+    per = rows // COLS
+    block = s_ref[pl.ds(lax.axis_index("col") * per, per)]
+    return jnp.concatenate([block[r, i : i + 1, : D // rows] for r in range(per)], axis=1)
+
+
+def head_features(s_ref, i, heads):
+    rows = s_ref.shape[0]
+    size = HD // rows
+    cuts = [slice(h * size, (h + 1) * size) for h in range(heads)]
+    return jnp.concatenate([s_ref[r, i : i + 1, c] for c in cuts for r in range(rows)], axis=1)
+
+
 def slots_of(target_ref, row, count):
     base = row * count
     slot = base + lax.broadcasted_iota(jnp.int32, (count, target_ref.shape[1]), 0)
@@ -111,13 +148,15 @@
     pieces,
     x_ref,
     g_ref,
-    t_ref,
+    ids_ref,
+    table_ref,
     w_ref,
     s_ref,
     xo_ref,
     go_ref,
     wo_ref,
     so_ref,
+    t_ref,
     xp_ref,
     gp_ref,
     c_send,
@@ -188,6 +227,7 @@
         copy.start()
         row_copies.append(copy)
 
+    t_ref[...] = route(ids_ref[...], table_ref[...], EXP_DEV * rows, cap)
     send_rows(0)
     xo_ref[me] = xp_ref[...]
     wo_ref[row] = w_ref[...]
@@ -261,7 +301,7 @@
         copy.wait()
 
 
-def start_gather(x, g, target, w, s, rows, cap):
+def start_gather(x, g, ids, table, w, s, rows, cap):
     pieces = 4
     tokens, width = x.shape
     packed = (tokens // 2, 2 * width)
@@ -272,9 +312,10 @@
             jax.ShapeDtypeStruct((rows, cap, 2 * width), g.dtype),
             jax.ShapeDtypeStruct((rows,) + w.shape, w.dtype),
             jax.ShapeDtypeStruct((rows,) + s.shape, s.dtype),
+            jax.ShapeDtypeStruct((1, tokens), jnp.int32),
         ),
-        in_specs=[VSPEC] * 5,
-        out_specs=(VSPEC,) * 4,
+        in_specs=[VSPEC] * 6,
+        out_specs=(VSPEC,) * 5,
         scratch_shapes=[
             pltpu.VMEM(packed, x.dtype),
             pltpu.VMEM((rows - 1, cap, 2 * width), g.dtype),
@@ -286,14 +327,18 @@
             DMA((3, rows // 2)),
         ],
         compiler_params=params(0),
-    )(x, g, target, w, s)
+    )(x, g, ids, table, w, s)
 
 
 def project_kernel(
-    x_ref, w_ref, gain_ref, shift_ref, bias_ref, q_ref, kv_ref, h_ref, n_ref, r_ref
+    x_ref, w_ref, s_ref, q_ref, kv_ref, h_ref, n_ref, r_ref
 ):
     me = lax.axis_index("col")
     half, width = x_ref.shape[1], x_ref.shape[2] // 2
+    gain, shift = all_features(s_ref, 0), all_features(s_ref, 1)
+    query = head_features(s_ref, 5, width // HD)
+    value = head_features(s_ref, 6, width // HD)
+    bias = jnp.concatenate([query, jnp.zeros_like(query), value], axis=1)
     w = w_ref[...].reshape(D, 4 * width)[:, : 3 * width]
     step = min(half, 256)
     for i in range(2 * half // step):
@@ -303,17 +348,17 @@
         mean = jnp.mean(x, axis=-1, keepdims=True)
         centred = x - mean
         rstd = lax.rsqrt(jnp.mean(centred * centred, axis=-1, keepdims=True) + epsilon)
-        h = (centred * rstd * gain_ref[...] + shift_ref[...]).astype(BF16)
+        h = (centred * rstd * gain + shift).astype(BF16)
         out = slice(i * step, (i + 1) * step)
         h_ref[out] = h
         n_ref[out] = (x_ref[me, rows, feats].astype(F32) - mean) * rstd
         r_ref[out] = rstd
-        qkv = (nn(h, w) + bias_ref[...]).astype(BF16)
+        qkv = (nn(h, w) + bias).astype(BF16)
         q_ref[out] = qkv[:, :width] * jnp.asarray(HD**-0.5, BF16)
         kv_ref[out] = qkv[:, width:]
 
 
-def project(x, w, gain, shift, bias):
+def project(x, w, s):
     tokens, width = 2 * x.shape[1], x.shape[2] // 2
     return pl.pallas_call(
         project_kernel,
@@ -324,10 +369,10 @@
             jax.ShapeDtypeStruct((tokens, width), F32),
             jax.ShapeDtypeStruct((tokens, 1), F32),
         ),
-        in_specs=[VSPEC] * 5,
+        in_specs=[VSPEC] * 3,
         out_specs=(VSPEC,) * 5,
         compiler_params=params(),
-    )(x, w, gain, shift, bias)
+    )(x, w, s)
 
 
 def mid_kernel(
@@ -625,28 +670,31 @@
         at = jnp.where(t <= level, level - t, t)
         live = (t <= level) | (t < low)
         line_in = live & (cross == 0)
-
-        @pl.when(line_in & (at < level))
+        coming = t + 1
+        via = jnp.where(coming <= level, level - coming, coming)
+        relays = (cross == 1) & ((coming <= level) | (coming < low))
+
+        @pl.when(relays & (via < level))
         def _():
             for i in range(pieces):
-                make(at, i, 0).wait_recv()
+                make(via, i, 0).wait_recv()
 
                 @pl.when(to_up)
                 def _(i=i):
-                    make(at, i, 0).start()
-
-                make(at, i, 2).start()
-
-        @pl.when(line_in & (at > level))
+                    make(via, i, 0).start()
+
+                make(via, i, 2).start()
+
+        @pl.when(relays & (via > level))
         def _():
             for i in range(pieces):
-                make(at, i, 1).wait_recv()
+                make(via, i, 1).wait_recv()
 
                 @pl.when(level > 0)
                 def _(i=i):
-                    make(at, i, 1).start()
-
-                make(at, i, 2).start()
+                    make(via, i, 1).start()
+
+                make(via, i, 2).start()
 
         comes = live & (cross == 1) & ((at < low) | (at < level) | (side == 1))
         when(comes, lambda i: other(at, i).wait_recv())
@@ -1015,9 +1063,7 @@
     a_ref,
     w_ref,
     x_ref,
-    bias_ref,
-    gain_ref,
-    shift_ref,
+    s_ref,
     mid_ref,
     normed_ref,
     rstd_ref,
@@ -1048,7 +1094,7 @@
         (send, recv),
         lambda: None,
     )
-    mid = x_ref[...].astype(F32) + mid_ref[...] + bias_ref[...]
+    mid = x_ref[...].astype(F32) + mid_ref[...] + own_features(s_ref, 4)
     mid_ref[...] = mid
     part_mean = jnp.mean(mid, axis=-1, keepdims=True)
     part_spread = jnp.sum((mid - part_mean) ** 2, axis=-1, keepdims=True)
@@ -1062,10 +1108,10 @@
     normed = (mid - mean) * rstd
     normed_ref[...] = normed
     rstd_ref[...] = rstd
-    h_ref[...] = (normed * gain_ref[...] + shift_ref[...]).astype(BF16)
-
-
-def branch(a, w, x, bias, gain, shift, collective):
+    h_ref[...] = (normed * own_features(s_ref, 2) + own_features(s_ref, 3)).astype(BF16)
+
+
+def branch(a, w, x, s, collective):
     pieces = 4
     tokens, width = a.shape
     rows = jax.ShapeDtypeStruct((tokens, width), F32)
@@ -1077,7 +1123,7 @@
             jax.ShapeDtypeStruct((tokens, 1), F32),
             jax.ShapeDtypeStruct((tokens, width), BF16),
         ),
-        in_specs=[VSPEC] * 6,
+        in_specs=[VSPEC] * 4,
         out_specs=(VSPEC,) * 4,
         scratch_shapes=product_scratch(pieces, tokens, width)
         + [
@@ -1087,7 +1133,7 @@
             DMA((COLS - 1,)),
         ],
         compiler_params=params(collective),
-    )(a, w, x, bias, gain, shift)
+    )(a, w, x, s)
 
 
 def input_kernel(
@@ -1100,7 +1146,7 @@
     mid_ref,
     normed_ref,
     rstd_ref,
-    gain_ref,
+    s_ref,
     vec_ref,
     gin_ref,
     eo_ref,
@@ -1155,7 +1201,7 @@
     st_ref[1:2, tokens : tokens + width] = jnp.sum(grad, axis=0, keepdims=True)
     st_ref[2:5, tokens : tokens + width] = vec_ref[0:3]
     gin_ref[...] = mid_ref[...] + norm_back(
-        grad, normed, gain_ref[...], rstd_ref[...], st_ref, all_ref, st_send, st_recv
+        grad, normed, own_features(s_ref, 0), rstd_ref[...], st_ref, all_ref, st_send, st_recv
     )
     for copy in home:
         copy.wait()
@@ -1267,7 +1313,7 @@
     cot_ref,
     normed_ref,
     rstd_ref,
-    gain_ref,
+    s_ref,
     mid_ref,
     vec_ref,
     sum_ref,
@@ -1334,7 +1380,7 @@
         sum_ref[...] += combined(t_ref, out_ref[source], source, cap)
     grad, normed = sum_ref[...], normed_ref[...]
     mid = cot_ref[...].astype(F32) + norm_back(
-        grad, normed, gain_ref[...], rstd_ref[...], st_ref, all_ref, st_send, st_recv
+        grad, normed, own_features(s_ref, 2), rstd_ref[...], st_ref, all_ref, st_send, st_recv
     )
     mid_ref[...] = mid
     vec_ref[...] = jnp.zeros(vec_ref.shape, F32)
@@ -1618,62 +1664,29 @@
     )
     expert_total = EXP_DEV * rows
     capacity = max(2, 2 * tokens // expert_total)
-    expert_of = hash_table[token_ids]
-    hits = expert_of[:, None] == jnp.arange(expert_total, dtype=jnp.int32)[None, :]
-    earlier = (
-        jnp.arange(tokens, dtype=jnp.int32)[None, :] < jnp.arange(tokens, dtype=jnp.int32)[:, None]
+    table = jnp.pad(hash_table, (0, -hash_table.shape[0] % (128 * 128)))
+    table = table.reshape(-1, 128).astype(BF16)
+
+    weights = jnp.concatenate([w_query, w_key, w_value, w_output], axis=1)
+    x_all, g_own, w_all, s_all, target = start_gather(
+        layer_in, cotangent, token_ids[None], table, weights, small, rows, capacity
     )
-    before = jnp.dot(earlier.astype(BF16), hits.astype(BF16), preferred_element_type=F32)
-    slot_of = jnp.sum(jnp.where(hits, before, 0.0), axis=1).astype(jnp.int32)
-    target = expert_of * capacity + slot_of
-    target = target[None, :]
-
-    weights = jnp.concatenate([w_query, w_key, w_value, w_output], axis=1)
-    x_all, g_own, w_all, s_all = start_gather(
-        layer_in, cotangent, target, weights, small, rows, capacity
-    )
-    gain_one, shift_one, gain_two, shift_two, out_bias = (
-        s_all[:, i, :share].reshape(D) for i in range(5)
-    )
-
-    def own(v):
-        return lax.dynamic_slice_in_dim(v, col * width, width, 0)
-
-    query_bias, value_bias = (
-        s_all[:, i, : heads * bias_share]
-        .reshape(rows, heads, bias_share)
-        .transpose(1, 0, 2)
-        .reshape(width)
-        for i in (5, 6)
-    )
-
-    qkv_bias = jnp.concatenate([query_bias, jnp.zeros_like(query_bias), value_bias])
-    queries, keys_values, h_one, normed_one, rstd_one = project(
-        x_all, w_all, gain_one[None], shift_one[None], qkv_bias[None]
-    )
+
+    queries, keys_values, h_one, normed_one, rstd_one = project(x_all, w_all, s_all)
     seq_hit = row // group == jnp.arange(prefix_len.shape[0], dtype=jnp.int32)
     prefix = jnp.sum(jnp.where(seq_hit, prefix_len, 0))
     info = prefix.astype(jnp.int32).reshape(1)
     kv_all, attended, attended_low, lse, g_all = attention_forward(
         info, queries, keys_values, g_own, group, low, 1
     )
-    gain_two_own = own(gain_two)[None]
-    mid, normed_two, rstd_two, h_two = branch(
-        attended_low,
-        w_all,
-        layer_in,
-        own(out_bias)[None],
-        gain_two_own,
-        own(shift_two)[None],
-        2,
-    )
+    mid, normed_two, rstd_two, h_two = branch(attended_low, w_all, layer_in, s_all, 2)
 
     received = dispatch(h_two, target, rows, capacity, 4)
     parts, grad_parts, grad_w_up, grad_bias_up, grad_w_down, grad_bias_down = experts(
         received, g_all, w_up, bias_up, w_down
     )
     grad_mid, vectors = giveback(
-        grad_parts, target, cotangent, normed_two, rstd_two, gain_two_own, rows, 5
+        grad_parts, target, cotangent, normed_two, rstd_two, s_all, rows, 5
     )
     grad_attended, delta, grad_w_out = mid_gradient(grad_mid, w_all, attended, attended_low, 7)
     down_own = lax.dynamic_slice_in_dim(bias_down, col * width, width, 1).astype(F32)
@@ -1701,7 +1714,7 @@
         grad_mid,
         normed_one,
         rstd_one,
-        own(gain_one)[None],
+        s_all,
         vectors,
         9,
     )

time: 461 us -> 438 us (0.950)
  Pallas kernels: 414 us -> 403 us
  local copies, waits for them, and re-layouts: 29.5 us -> 19.1 us
    pallas_call x1, Pallas kernels: 79.5 us -> 70.8 us  [dispatch(): pl.pallas_call(functools.partial(dispatch_kernel, rows), out_shape=jax.Sh...]
    gather x1 -> x0, local copies, waits for them, and re-layouts: 6.15 us -> none  [per_device(): expert_of = hash_table[token_ids]]
    pallas_call x1, Pallas kernels: 55.2 us -> 49.5 us  [attention_forward(): pl.pallas_call(functools.partial(forward_kernel, group, low, pieces, toke...]
where the time goes in v6:
time: 438 us; the launch traced here: 430 us
  Pallas kernels  403 us (92%)
  local copies, waits for them, and re-layouts  19.1 us (4%)
  other arithmetic  6.31 us (1%)
    pallas_call x1, Pallas kernels, attention_backward(): pl.pallas_call(functools.partial(backward_kernel, group, low, pieces, tok...  84.6 us
    pallas_call x1, Pallas kernels, dispatch(): pl.pallas_call(functools.partial(dispatch_kernel, rows), out_shape=jax.Sh...  70.8 us
    pallas_call x1, Pallas kernels, attention_forward(): pl.pallas_call(functools.partial(forward_kernel, group, low, pieces, toke...  49.5 us
    pallas_call x1, Pallas kernels, giveback(): pl.pallas_call(functools.partial(giveback_kernel, rows), out_shape=(jax.S...  38.8 us
    pallas_call x1, Pallas kernels, start_gather(): pl.pallas_call(functools.partial(start_kernel, rows, pieces), out_shape=(...  33.9 us
    pallas_call x1, Pallas kernels, experts(): pl.pallas_call(expert_kernel, grid=(count,), out_shape=(jax.ShapeDtypeStr...  30.1 us
    pallas_call x1, Pallas kernels, input_gradient(): pl.pallas_call(functools.partial(input_kernel, pieces), out_shape=(jax.Sh...  27.7 us
    pallas_call x1, Pallas kernels, end_scatter(): pl.pallas_call(functools.partial(end_kernel, rows), out_shape=(jax.ShapeD...  22.8 us

profile of v6, /device:TPU:10, one launch (start us, length us, event | category | flops | bytes accessed | tf_op | source)
XLA Modules:
  0.0 429.7 jit_solution(11229921846435507802)
XLA Ops:
  1.3 0.8 convert_element_type.42
  2.1 0.8 convert_element_type.44
  2.9 0.7 bitcast_convert_fusion.2
  3.5 0.7 bitcast_convert_fusion.4
  4.2 0.7 bitcast_convert_fusion.6
  4.9 0.6 stack.59.s_ref
  5.5 2.0 copy.43.x_ref
  7.5 2.0 copy.44.g_ref.cot_ref
  9.5 0.9 convert.30
  10.4 0.7 pad_bitcast_fusion.table_ref
  11.1 1.6 pad_maximum_fusion.w_ref
  12.7 33.9 %shard_map.323 = (bf16[4,512,384]{2,1,0:T(8,128)(2,1)}, bf16[8,128,384]{2,1,0:T(8,128)(2,1)}, bf16[8,96,768]{2,1,0:T(8,128)(2,1)}, f32[8,8,128]{2,1,0:T(8,128)}, s32[1,1024]{1,0:T(1,128)}) custom-call(bf16[1024,192]{1,0:T(8,128)(2,1)} %copy.43.x_ref, bf16[1024,192]{1,0:T(8,128)(2,1)} %copy.44.g_ref.cot_ref, s32[1,1024]{1,0:T(1,128)} %bitcast.65, ...), custom_call_target="tpu_custom_call" | custom-call | tf_op jit(solution)/shard_map/pallas_call | solution.py:308
  46.6 6.7 %shard_map.324 = (bf16[1024,192]{1,0:T(8,128)(2,1)}, bf16[1024,384]{1,0:T(8,128)(2,1)}, bf16[1024,768]{1,0:T(8,128)(2,1)}, f32[1024,192]{1,0:T(8,128)}, f32[1024,1]{1,0:T(8,128)}) custom-call(bf16[4,512,384]{2,1,0:T(8,128)(2,1)} %get-tuple-element.56.x_ref, bf16[8,96,768]{2,1,0:T(8,128)(2,1)} %get-tuple-element.57.w_ref, f32[8,8,128]{2,1,0:T(8,128)} %get-tuple-element.58.s_ref), custom_call_target="tpu_custom_call" | custom-call | tf_op jit(solution)/shard_map/pallas_call | solution.py:363
  53.3 49.5 %shard_map.325 = (bf16[8,1024,384]{2,1,0:T(8,128)(2,1)}, f32[1024,192]{1,0:T(8,128)}, bf16[1024,192]{1,0:T(8,128)(2,1)}, f32[8,1024]{1,0:T(8,128)}, bf16[4,8,128,384]{3,2,1,0:T(8,128)(2,1)}) custom-call(s32[1]{0:T(128)S(6)} %select_n.13.info_ref, bf16[1024,192]{1,0:T(8,128)(2,1)} %get-tuple-element.59.q_ref, bf16[1024,384]{1,0:T(8,128)(2,1)} %get-tuple-element.60.kv_ref, ...), custom_call_target="tpu_custom_call" | custom-call | tf_op jit(solution)/shard_map/pallas_call | solution.py:743
  102.8 0.0 copy-start.4
  102.8 21.2 %shard_map.326 = (f32[1024,192]{1,0:T(8,128)}, f32[1024,192]{1,0:T(8,128)}, f32[1024,1]{1,0:T(8,128)}, bf16[1024,192]{1,0:T(8,128)(2,1)}) custom-call(bf16[1024,192]{1,0:T(8,128)(2,1)} %get-tuple-element.63.a_ref.low_ref, bf16[8,96,768]{2,1,0:T(8,128)(2,1)} %get-tuple-element.57.w_ref, bf16[1024,192]{1,0:T(8,128)(2,1)} %copy.43.x_ref, ...), custom_call_target="tpu_custom_call" | custom-call | tf_op jit(solution)/shard_map/pallas_call | solution.py:1118
  124.1 70.8 %shard_map.327.x_ref = bf16[4,8,128,384]{3,2,1,0:T(8,128)(2,1)} custom-call(bf16[1024,192]{1,0:T(8,128)(2,1)} %get-tuple-element.64.x_ref, s32[1,1024]{1,0:T(1,128)} %get-tuple-element.65.t_ref), custom_call_target="tpu_custom_call" | custom-call | tf_op jit(solution)/shard_map/pallas_call | solution.py:1293
  194.9 0.0 copy-done.4
  194.9 0.6 copy.46.bias_ref
  195.5 30.1 %shard_map.328 = (bf16[4,8,128,384]{3,2,1,0:T(8,128)(2,1)}, bf16[4,8,128,384]{3,2,1,0:T(8,128)(2,1)}, f32[2,768,768]{2,1,0:T(8,128)}, f32[2,1,768]{2,1,0:T(1,128...) custom-call(bf16[4,8,128,384]{3,2,1,0:T(8,128)(2,1)} %shard_map.327.x_ref, ...), custom_call_target="tpu_custom_call" | custom-call | tf_op jit(solution)/shard_map/pallas_call | solution.py:1587
  225.6 38.8 %shard_map.329 = (f32[1024,192]{1,0:T(8,128)}, f32[8,192]{1,0:T(8,128)}) custom-call(bf16[4,8,128,384]{3,2,1,0:T(8,128)(2,1)} %get-tuple-element.67.in_ref, s32[1,1024]{1,0:T(1,128)} %get-tuple-element.65.t_ref, bf16[1024,192]{1,0:T(8,128)(2,1)} %copy.44.g_ref.cot_ref, f32[1024,192]{1,0:T(8,128)} %get-tuple-element.68.normed_ref, ...), custom_call_target="tpu_custom_call" | custom-call | tf_op jit(solution)/shard_map/pallas_call | solution.py:1401
  264.4 16.5 %shard_map.330 = (bf16[1024,192]{1,0:T(8,128)(2,1)}, f32[8,1024]{1,0:T(8,128)}, bf16[768,192]{1,0:T(8,128)(2,1)}) custom-call(f32[1024,192]{1,0:T(8,128)} %get-tuple-element.70.x_ref.mid_ref, bf16[8,96,768]{2,1,0:T(8,128)(2,1)} %get-tuple-element.57.w_ref, f32[1024,192]{1,0:T(8,128)} %get-tuple-element.71.att_ref, ...), custom_call_target="tpu_custom_call" | custom-call | tf_op jit(solution)/shard_map/pallas_call | solution.py:450
  280.9 0.8 dynamic-slice_convert_fusion
  281.7 0.6 reshape.118.bias_ref
  282.3 84.6 %shard_map.331 = (bf16[1024,576]{1,0:T(8,128)(2,1)}, bf16[8,128,384]{2,1,0:T(8,128)(2,1)}) custom-call(s32[1]{0:T(128)S(6)} %select_n.13.info_ref, bf16[1024,192]{1,0:T(8,128)(2,1)} %get-tuple-element.59.q_ref, bf16[8,1024,384]{2,1,0:T(8,128)(2,1)} %get-tuple-element.62.kv_ref, bf16[1024,192]{1,0:T(8,128)(2,1)} %get-tuple-element.72.do_ref, ...), custom_call_target="tpu_custom_call" | custom-call | tf_op jit(solution)/shard_map/pallas_call | solution.py:974
  366.9 0.0 copy-start
  366.9 27.7 %shard_map.332 = (f32[1024,192]{1,0:T(8,128)}, bf16[8,128,384]{2,1,0:T(8,128)(2,1)}, bf16[768,768]{1,0:T(8,128)(2,1)}, f32[4,8,1280]{2,1,0:T(8,128)}) custom-call(bf16[1024,576]{1,0:T(8,128)(2,1)} %get-tuple-element.76.a_ref, bf16[8,96,768]{2,1,0:T(8,128)(2,1)} %get-tuple-element.57.w_ref, bf16[8,128,384]{2,1,0:T(8,128)(2,1)} %get-tuple-element.77.e_ref, ...), custom_call_target="tpu_custom_call" | custom-call | tf_op jit(solution)/shard_map/pallas_call | solution.py:1214
  394.6 0.8 slice_bitcast_fusion
  395.4 0.1 reshape.103
  395.5 0.0 copy-done
  395.5 0.3 convert_reduce_fusion
  395.8 0.0 copy-start.1
  395.8 0.1 reshape.104
  395.9 0.1 reshape.105
  396.0 0.1 reshape.106
  396.1 0.1 reshape.107
  396.1 0.1 pad.60.clone
  396.2 0.7 fusion.s_ref
  396.9 0.0 copy-start.3
  396.9 0.0 copy-start.2
  396.9 22.8 %shard_map.333 = (f32[96,768]{1,0:T(8,128)}, f32[8,128]{1,0:T(8,128)}, bf16[1024,192]{1,0:T(8,128)(2,1)}) custom-call(bf16[8,96,768]{2,1,0:T(8,128)(2,1)} %bitcast.57, f32[8,8,128]{2,1,0:T(8,128)} %fusion.s_ref, bf16[8,128,384]{2,1,0:T(8,128)(2,1)} %get-tuple-element.85.e_ref, s32[1,1024]{1,0:T(1,128)} %get-tuple-element.65.t_ref, ...), custom_call_target="tpu_custom_call" | custom-call | tf_op jit(solution)/shard_map/pallas_call | solution.py:1505
  419.8 1.9 fusion.3
  421.6 2.0 copy.54
  423.6 0.8 slice_reduce_fusion
  424.4 0.7 reshape.108
  425.0 0.7 reshape.109
  425.7 1.4 slice_bitcast_fusion.1
  427.1 0.0 copy-done.1
  427.1 1.2 copy.55
  428.3 0.0 copy-done.3
  428.3 0.6 copy.62
  428.9 0.0 copy-done.2
  428.9 0.6 copy.63
  (7 shorter events, 0.1 us)
Async XLA Ops:
  102.8 92.1 %copy-start.4 = (bf16[2,768]{1,0:T(2,128)(2,1)S(1)}, bf16[2,768]{1,0:T(2,128)(2,1)}, u32[]{:S(2)}) copy-start(bf16[2,768]{1,0:T(2,128)(2,1)} %param.37) | copy-start | bytes 9220
  366.9 28.6 %copy-start = (bf16[1024,576]{1,0:T(8,128)(2,1)S(1)}, bf16[1024,576]{1,0:T(8,128)(2,1)}, u32[]{:S(2)}) copy-start(bf16[1024,576]{1,0:T(8,128)(2,1)} %get-tuple-element.76.a_ref) | copy-start | bytes 3538948
  395.8 31.3 %copy-start.1 = (f32[1024,192]{1,0:T(8,128)S(1)}, f32[1024,192]{1,0:T(8,128)}, u32[]{:S(2)}) copy-start(f32[1024,192]{1,0:T(8,128)} %get-tuple-element.113) | copy-start | bytes 2359300
  396.9 31.4 %copy-start.3 = (f32[2,1,768]{2,1,0:T(1,128)S(1)}, f32[2,1,768]{2,1,0:T(1,128)}, u32[]{:S(2)}) copy-start(f32[2,1,768]{2,1,0:T(1,128)} %get-tuple-element.94) | copy-start | bytes 18436
  396.9 32.0 %copy-start.2 = (f32[2,1,768]{2,1,0:T(1,128)S(1)}, f32[2,1,768]{2,1,0:T(1,128)}, u32[]{:S(2)}) copy-start(f32[2,1,768]{2,1,0:T(1,128)} %get-tuple-element.92) | copy-start | bytes 18436

commit v7 on v6

--- a/solution.py
+++ b/solution.py
@@ -811,7 +811,7 @@
         terms.append(copy)
     dqt_ref[...] = jnp.zeros(dqt_ref.shape, F32)
 
-    def block(blk, masked):
+    def block(blk, masked, leaves, at):
         def body(j, carry):
             start = pl.multiple_of(j * kb, kb)
             keys = pl.ds(start, kb)
@@ -828,6 +828,12 @@
                 part_ref[blk, keys, feats] = nn(grad, q).astype(BF16)
                 part_ref[blk, keys, vals] = nn(probs.astype(BF16), do).astype(BF16)
                 dqt_ref[feats, :] += nn(k.T, grad)
+
+            @pl.when(leaves)
+            def _():
+                for n in range(kb // step):
+                    cross(at, j * (kb // step) + n).start()
+
             return carry
 
         lax.fori_loop(0, tokens // kb, body, 0)
@@ -916,16 +922,11 @@
 
         @pl.when(needed & (blk < place))
         def _():
-            block(blk, False)
+            block(blk, False, goes, at)
 
         @pl.when(needed & (blk >= place))
         def _():
-            block(blk, True)
-
-        @pl.when(goes)
-        def _():
-            for i in range(pieces):
-                cross(at, i).start()
+            block(blk, True, goes, at)
 
         return carry
 
@@ -1242,6 +1243,13 @@
     greet([{"row": p} for p in peers] + [{"col": sib}, {"col": across}])
     copies = []
     cap = in_ref.shape[1]
+
+    def col(src, dst, k, way):
+        return push(
+            src, dst, c_send.at[way, k], c_recv.at[way, k], {"col": across if way == 0 else sib}
+        )
+
+    done, first = [], []
     for k, peer in enumerate(peers):
         in_ref[peer] = placed(t_ref, x_ref[...], peer, cap)
         copy = push(
@@ -1249,18 +1257,12 @@
         )
         copy.start()
         copies.append(copy)
-    in_ref[row] = placed(t_ref, x_ref[...], row, cap)
-
-    def col(src, dst, k, way):
-        return push(
-            src, dst, c_send.at[way, k], c_recv.at[way, k], {"col": across if way == 0 else sib}
-        )
-
-    done, first = [], []
-    for way in range(2):
-        copy = col(in_ref.at[row], out_ref.at[me, row], 0, way)
-        copy.start()
-        (first if way == 0 else done).append(copy)
+        if k == 1:
+            in_ref[row] = placed(t_ref, x_ref[...], row, cap)
+            for way in range(2):
+                copy = col(in_ref.at[row], out_ref.at[me, row], 0, way)
+                copy.start()
+                (first if way == 0 else done).append(copy)
     out_ref[me, row] = in_ref[row]
     sources = [row] + [(row + rows - k) % rows for k in order]
 
@@ -1530,63 +1532,98 @@
 def expert_kernel(
     x_ref,
     g_ref,
-    up_ref,
+    up_hbm,
     bias_ref,
-    down_ref,
+    down_hbm,
     part_ref,
     gx_ref,
+    gup_hbm,
+    gbu_ref,
+    gdown_hbm,
+    gbd_ref,
+    up_ref,
+    down_ref,
     gup_ref,
-    gbu_ref,
     gdown_ref,
-    gbd_ref,
+    xs_ref,
+    gs_ref,
+    sum_ref,
+    gsum_ref,
+    in_sems,
+    out_sems,
 ):
     cols, rows, cap, both = x_ref.shape
     width = both // 2
     slots = rows * cap
-    first = pl.program_id(0) == 0
-
-    def mine(ref):
-        blocks = [ref[b].reshape(slots, both) for b in range(cols)]
-        blocks = [jnp.where(first, v[:, :width], v[:, width:]) for v in blocks]
-        return jnp.concatenate(blocks, axis=1)
-
-    x, g = mine(x_ref), mine(g_ref)
-    gbd_ref[...] = jnp.sum(g.astype(F32), axis=0).reshape(gbd_ref.shape)
-    hidden_units = up_ref.shape[2]
+    count, _, hidden_units = up_ref.shape
     chunk = 256
-    part = jnp.zeros((slots, cols * width), F32)
-    gx = jnp.zeros((slots, cols * width), F32)
-    for f in range(hidden_units // chunk):
-        cut = slice(f * chunk, (f + 1) * chunk)
-        up, down = up_ref[0, :, cut], down_ref[0, cut, :]
-        pre = nn(x, up) + bias_ref[0, :, cut].astype(F32)
-        cdf = 0.5 * (1.0 + lax.erf(pre * (0.5**0.5)))
-        slope = cdf + pre * (jnp.exp(-0.5 * pre * pre) * 0.3989422804014327)
-        hidden = (pre * cdf).astype(BF16)
-        grad = nt(g, down) * slope
-        grad = grad.astype(BF16)
-        part = part + nn(hidden, down)
-        gx = gx + nt(grad, up)
-        gdown_ref[0, cut, :] = tn(hidden, g)
-        gup_ref[0, :, cut] = tn(x, grad)
-        gbu_ref[0, :, cut] = jnp.sum(grad.astype(F32), axis=0, keepdims=True)
-    for e in range(EXP_DEV):
-
-        @pl.when(pl.program_id(0) == e)
-        def _(e=e):
-            lanes = slice(e * width, (e + 1) * width)
-            for b in range(cols):
-                cut = slice(b * width, (b + 1) * width)
-                part_ref[b, :, :, lanes] = part[:, cut].astype(BF16).reshape(rows, cap, width)
-                gx_ref[b, :, :, lanes] = gx[:, cut].astype(BF16).reshape(rows, cap, width)
+    loads = []
+    for e in range(count):
+        for j, (src, dst) in enumerate(((up_hbm, up_ref), (down_hbm, down_ref))):
+            copy = pltpu.make_async_copy(src.at[e], dst.at[e], in_sems.at[j, e])
+            copy.start()
+            loads.append(copy)
+
+    def gup_out(e, f):
+        cut = pl.ds(pl.multiple_of(f * chunk, chunk), chunk)
+        return pltpu.make_async_copy(
+            gup_ref.at[e, :, cut], gup_hbm.at[e, :, cut], out_sems.at[0, e, f]
+        )
+
+    def gdown_out(e, f):
+        cut = pl.ds(pl.multiple_of(f * chunk, chunk), chunk)
+        return pltpu.make_async_copy(
+            gdown_ref.at[e, cut], gdown_hbm.at[e, cut], out_sems.at[1, e, f]
+        )
+
+    for e in range(count):
+        lanes = slice(e * width, (e + 1) * width)
+        for ref, dst in ((x_ref, xs_ref), (g_ref, gs_ref)):
+            blocks = [ref[b].reshape(slots, both)[:, lanes] for b in range(cols)]
+            dst[...] = jnp.concatenate(blocks, axis=1)
+        gbd_ref[e] = jnp.sum(gs_ref[...].astype(F32), axis=0, keepdims=True)
+        sum_ref[...] = jnp.zeros(sum_ref.shape, F32)
+        gsum_ref[...] = jnp.zeros(gsum_ref.shape, F32)
+        loads[2 * e].wait()
+        loads[2 * e + 1].wait()
+
+        def body(f, carry, e=e):
+            cut = pl.ds(pl.multiple_of(f * chunk, chunk), chunk)
+            x, g = xs_ref[...], gs_ref[...]
+            up, down = up_ref[e, :, cut], down_ref[e, cut, :]
+            pre = nn(x, up) + bias_ref[e, :, cut].astype(F32)
+            cdf = 0.5 * (1.0 + lax.erf(pre * (0.5**0.5)))
+            slope = cdf + pre * (jnp.exp(-0.5 * pre * pre) * 0.3989422804014327)
+            hidden = (pre * cdf).astype(BF16)
+            grad = nt(g, down) * slope
+            grad = grad.astype(BF16)
+            sum_ref[...] += nn(hidden, down)
+            gsum_ref[...] += nt(grad, up)
+            gdown_ref[e, cut, :] = tn(hidden, g)
+            gdown_out(e, f).start()
+            gup_ref[e, :, cut] = tn(x, grad)
+            gup_out(e, f).start()
+            gbu_ref[e, :, cut] = jnp.sum(grad.astype(F32), axis=0, keepdims=True)
+            return carry
+
+        lax.fori_loop(0, hidden_units // chunk, body, 0)
+        for b in range(cols):
+            cut = slice(b * width, (b + 1) * width)
+            part_ref[b, :, :, lanes] = sum_ref[:, cut].astype(BF16).reshape(rows, cap, width)
+            gx_ref[b, :, :, lanes] = gsum_ref[:, cut].astype(BF16).reshape(rows, cap, width)
+    for e in range(count):
+        for f in range(hidden_units // chunk):
+            gdown_out(e, f).wait()
+            gup_out(e, f).wait()
 
 
 def experts(x, g, w_up, bias_up, w_down):
-    slots = pl.BlockSpec(x.shape, lambda e: (0, 0, 0, 0))
+    cols, rows, cap, _ = x.shape
     count, features, hidden = w_up.shape
+    slots = rows * cap
+    anywhere = pl.BlockSpec(memory_space=pl.ANY)
     return pl.pallas_call(
         expert_kernel,
-        grid=(count,),
         out_shape=(
             jax.ShapeDtypeStruct(x.shape, BF16),
             jax.ShapeDtypeStruct(x.shape, BF16),
@@ -1595,21 +1632,20 @@
             jax.ShapeDtypeStruct(w_down.shape, F32),
             jax.ShapeDtypeStruct((count, 1, features), F32),
         ),
-        in_specs=[
-            slots,
-            slots,
-            pl.BlockSpec((1, features, hidden), lambda e: (e, 0, 0)),
-            pl.BlockSpec((1, 1, hidden), lambda e: (e, 0, 0)),
-            pl.BlockSpec((1, hidden, features), lambda e: (e, 0, 0)),
+        in_specs=[VSPEC, VSPEC, anywhere, VSPEC, anywhere],
+        out_specs=(VSPEC, VSPEC, anywhere, VSPEC, anywhere, VSPEC),
+        scratch_shapes=[
+            pltpu.VMEM(w_up.shape, BF16),
+            pltpu.VMEM(w_down.shape, BF16),
+            pltpu.VMEM(w_up.shape, F32),
+            pltpu.VMEM(w_down.shape, F32),
+            pltpu.VMEM((slots, features), BF16),
+            pltpu.VMEM((slots, features), BF16),
+            pltpu.VMEM((slots, features), F32),
+            pltpu.VMEM((slots, features), F32),
+            DMA((2, count)),
+            DMA((2, count, hidden // 256)),
         ],
-        out_specs=(
-            slots,
-            slots,
-            pl.BlockSpec((1, features, hidden), lambda e: (e, 0, 0)),
-            pl.BlockSpec((1, 1, hidden), lambda e: (e, 0, 0)),
-            pl.BlockSpec((1, hidden, features), lambda e: (e, 0, 0)),
-            pl.BlockSpec((1, 1, features), lambda e: (e, 0, 0)),
-        ),
         compiler_params=params(),
     )(x, g, w_up, bias_up.reshape(count, 1, hidden), w_down)
 

time: 438 us -> 434 us (level)
  no operation moved by 1% of the time
where the time goes in v7:
time: 434 us; the launch traced here: 427 us
  Pallas kernels  400 us (92%)
  local copies, waits for them, and re-layouts  19.1 us (4%)
  other arithmetic  6.31 us (1%)
    pallas_call x1, Pallas kernels, attention_backward(): pl.pallas_call(functools.partial(backward_kernel, group, low, pieces, tok...  84.3 us
    pallas_call x1, Pallas kernels, dispatch(): pl.pallas_call(functools.partial(dispatch_kernel, rows), out_shape=jax.Sh...  70.9 us
    pallas_call x1, Pallas kernels, attention_forward(): pl.pallas_call(functools.partial(forward_kernel, group, low, pieces, toke...  49.7 us
    pallas_call x1, Pallas kernels, giveback(): pl.pallas_call(functools.partial(giveback_kernel, rows), out_shape=(jax.S...  38.8 us
    pallas_call x1, Pallas kernels, start_gather(): pl.pallas_call(functools.partial(start_kernel, rows, pieces), out_shape=(...  33.9 us
    pallas_call x1, Pallas kernels, experts(): pl.pallas_call(expert_kernel, out_shape=(jax.ShapeDtypeStruct(x.shape, BF...  27.5 us
    pallas_call x1, Pallas kernels, input_gradient(): pl.pallas_call(functools.partial(input_kernel, pieces), out_shape=(jax.Sh...  26.5 us
    pallas_call x1, Pallas kernels, end_scatter(): pl.pallas_call(functools.partial(end_kernel, rows), out_shape=(jax.ShapeD...  23.5 us

profile of v7, /device:TPU:10, one launch (start us, length us, event | category | flops | bytes accessed | tf_op | source)
XLA Modules:
  0.0 426.8 jit_solution(6177145556747686080)
XLA Ops:
  1.3 0.8 convert_element_type.42
  2.1 0.8 convert_element_type.44
  2.9 0.7 bitcast_convert_fusion.2
  3.5 0.7 bitcast_convert_fusion.4
  4.2 0.7 bitcast_convert_fusion.6
  4.9 0.6 stack.59.s_ref
  5.5 2.0 copy.43.x_ref
  7.5 2.0 copy.44.g_ref.cot_ref
  9.5 0.9 convert.30
  10.4 0.7 pad_bitcast_fusion.table_ref
  11.1 1.6 pad_maximum_fusion.w_ref
  12.7 33.9 %shard_map.323 = (bf16[4,512,384]{2,1,0:T(8,128)(2,1)}, bf16[8,128,384]{2,1,0:T(8,128)(2,1)}, bf16[8,96,768]{2,1,0:T(8,128)(2,1)}, f32[8,8,128]{2,1,0:T(8,128)}, s32[1,1024]{1,0:T(1,128)}) custom-call(bf16[1024,192]{1,0:T(8,128)(2,1)} %copy.43.x_ref, bf16[1024,192]{1,0:T(8,128)(2,1)} %copy.44.g_ref.cot_ref, s32[1,1024]{1,0:T(1,128)} %bitcast.65, ...), custom_call_target="tpu_custom_call" | custom-call | tf_op jit(solution)/shard_map/pallas_call | solution.py:308
  46.6 6.7 %shard_map.324 = (bf16[1024,192]{1,0:T(8,128)(2,1)}, bf16[1024,384]{1,0:T(8,128)(2,1)}, bf16[1024,768]{1,0:T(8,128)(2,1)}, f32[1024,192]{1,0:T(8,128)}, f32[1024,1]{1,0:T(8,128)}) custom-call(bf16[4,512,384]{2,1,0:T(8,128)(2,1)} %get-tuple-element.56.x_ref, bf16[8,96,768]{2,1,0:T(8,128)(2,1)} %get-tuple-element.57.w_ref, f32[8,8,128]{2,1,0:T(8,128)} %get-tuple-element.58.s_ref), custom_call_target="tpu_custom_call" | custom-call | tf_op jit(solution)/shard_map/pallas_call | solution.py:363
  53.3 49.7 %shard_map.325 = (bf16[8,1024,384]{2,1,0:T(8,128)(2,1)}, f32[1024,192]{1,0:T(8,128)}, bf16[1024,192]{1,0:T(8,128)(2,1)}, f32[8,1024]{1,0:T(8,128)}, bf16[4,8,128,384]{3,2,1,0:T(8,128)(2,1)}) custom-call(s32[1]{0:T(128)S(6)} %select_n.13.info_ref, bf16[1024,192]{1,0:T(8,128)(2,1)} %get-tuple-element.59.q_ref, bf16[1024,384]{1,0:T(8,128)(2,1)} %get-tuple-element.60.kv_ref, ...), custom_call_target="tpu_custom_call" | custom-call | tf_op jit(solution)/shard_map/pallas_call | solution.py:743
  103.1 0.0 copy-start.4
  103.1 21.2 %shard_map.326 = (f32[1024,192]{1,0:T(8,128)}, f32[1024,192]{1,0:T(8,128)}, f32[1024,1]{1,0:T(8,128)}, bf16[1024,192]{1,0:T(8,128)(2,1)}) custom-call(bf16[1024,192]{1,0:T(8,128)(2,1)} %get-tuple-element.63.a_ref.low_ref, bf16[8,96,768]{2,1,0:T(8,128)(2,1)} %get-tuple-element.57.w_ref, bf16[1024,192]{1,0:T(8,128)(2,1)} %copy.43.x_ref, ...), custom_call_target="tpu_custom_call" | custom-call | tf_op jit(solution)/shard_map/pallas_call | solution.py:1119
  124.3 70.9 %shard_map.327.x_ref = bf16[4,8,128,384]{3,2,1,0:T(8,128)(2,1)} custom-call(bf16[1024,192]{1,0:T(8,128)(2,1)} %get-tuple-element.64.x_ref, s32[1,1024]{1,0:T(1,128)} %get-tuple-element.65.t_ref), custom_call_target="tpu_custom_call" | custom-call | tf_op jit(solution)/shard_map/pallas_call | solution.py:1295
  195.2 0.0 copy-done.4
  195.2 0.6 copy.46.bias_ref
  195.8 27.5 %shard_map.328 = (bf16[4,8,128,384]{3,2,1,0:T(8,128)(2,1)}, bf16[4,8,128,384]{3,2,1,0:T(8,128)(2,1)}, f32[2,768,768]{2,1,0:T(8,128)}, f32[2,1,768]{2,1,0:T(1,128...) custom-call(bf16[4,8,128,384]{3,2,1,0:T(8,128)(2,1)} %shard_map.327.x_ref, ...), custom_call_target="tpu_custom_call" | custom-call | tf_op jit(solution)/shard_map/pallas_call | solution.py:1625
  223.3 38.8 %shard_map.329 = (f32[1024,192]{1,0:T(8,128)}, f32[8,192]{1,0:T(8,128)}) custom-call(bf16[4,8,128,384]{3,2,1,0:T(8,128)(2,1)} %get-tuple-element.67.in_ref, s32[1,1024]{1,0:T(1,128)} %get-tuple-element.65.t_ref, bf16[1024,192]{1,0:T(8,128)(2,1)} %copy.44.g_ref.cot_ref, f32[1024,192]{1,0:T(8,128)} %get-tuple-element.68.normed_ref, ...), custom_call_target="tpu_custom_call" | custom-call | tf_op jit(solution)/shard_map/pallas_call | solution.py:1403
  262.1 16.5 %shard_map.330 = (bf16[1024,192]{1,0:T(8,128)(2,1)}, f32[8,1024]{1,0:T(8,128)}, bf16[768,192]{1,0:T(8,128)(2,1)}) custom-call(f32[1024,192]{1,0:T(8,128)} %get-tuple-element.70.x_ref.mid_ref, bf16[8,96,768]{2,1,0:T(8,128)(2,1)} %get-tuple-element.57.w_ref, f32[1024,192]{1,0:T(8,128)} %get-tuple-element.71.att_ref, ...), custom_call_target="tpu_custom_call" | custom-call | tf_op jit(solution)/shard_map/pallas_call | solution.py:450
  278.6 0.8 dynamic-slice_convert_fusion
  279.4 0.6 reshape.118.bias_ref
  280.0 84.3 %shard_map.331 = (bf16[1024,576]{1,0:T(8,128)(2,1)}, bf16[8,128,384]{2,1,0:T(8,128)(2,1)}) custom-call(s32[1]{0:T(128)S(6)} %select_n.13.info_ref, bf16[1024,192]{1,0:T(8,128)(2,1)} %get-tuple-element.59.q_ref, bf16[8,1024,384]{2,1,0:T(8,128)(2,1)} %get-tuple-element.62.kv_ref, bf16[1024,192]{1,0:T(8,128)(2,1)} %get-tuple-element.72.do_ref, ...), custom_call_target="tpu_custom_call" | custom-call | tf_op jit(solution)/shard_map/pallas_call | solution.py:975
  364.4 0.0 copy-start
  364.4 26.5 %shard_map.332 = (f32[1024,192]{1,0:T(8,128)}, bf16[8,128,384]{2,1,0:T(8,128)(2,1)}, bf16[768,768]{1,0:T(8,128)(2,1)}, f32[4,8,1280]{2,1,0:T(8,128)}) custom-call(bf16[1024,576]{1,0:T(8,128)(2,1)} %get-tuple-element.76.a_ref, bf16[8,96,768]{2,1,0:T(8,128)(2,1)} %get-tuple-element.57.w_ref, bf16[8,128,384]{2,1,0:T(8,128)(2,1)} %get-tuple-element.77.e_ref, ...), custom_call_target="tpu_custom_call" | custom-call | tf_op jit(solution)/shard_map/pallas_call | solution.py:1215
  390.9 0.8 slice_bitcast_fusion
  391.7 0.1 reshape.103
  391.8 0.0 copy-done
  391.8 0.3 convert_reduce_fusion
  392.0 0.0 copy-start.1
  392.0 0.1 reshape.104
  392.1 0.1 reshape.105
  392.2 0.1 reshape.106
  392.3 0.1 reshape.107
  392.4 0.1 pad.60.clone
  392.5 0.7 fusion.s_ref
  393.2 0.0 copy-start.3
  393.2 0.0 copy-start.2
  393.2 23.5 %shard_map.333 = (f32[96,768]{1,0:T(8,128)}, f32[8,128]{1,0:T(8,128)}, bf16[1024,192]{1,0:T(8,128)(2,1)}) custom-call(bf16[8,96,768]{2,1,0:T(8,128)(2,1)} %bitcast.57, f32[8,8,128]{2,1,0:T(8,128)} %fusion.s_ref, bf16[8,128,384]{2,1,0:T(8,128)(2,1)} %get-tuple-element.85.e_ref, s32[1,1024]{1,0:T(1,128)} %get-tuple-element.65.t_ref, ...), custom_call_target="tpu_custom_call" | custom-call | tf_op jit(solution)/shard_map/pallas_call | solution.py:1507
  416.7 1.9 fusion.3
  418.5 2.0 copy.54
  420.5 0.8 slice_reduce_fusion
  421.3 0.7 reshape.108
  421.9 0.7 reshape.109
  422.6 1.4 slice_bitcast_fusion.1
  424.0 0.0 copy-done.1
  424.0 1.2 copy.55
  425.2 0.0 copy-done.3
  425.2 0.6 copy.62
  425.8 0.0 copy-done.2
  425.8 0.6 copy.63
  (7 shorter events, 0.1 us)
Async XLA Ops:
  103.1 92.1 %copy-start.4 = (bf16[2,768]{1,0:T(2,128)(2,1)S(1)}, bf16[2,768]{1,0:T(2,128)(2,1)}, u32[]{:S(2)}) copy-start(bf16[2,768]{1,0:T(2,128)(2,1)} %param.37) | copy-start | bytes 9220
  364.4 27.4 %copy-start = (bf16[1024,576]{1,0:T(8,128)(2,1)S(1)}, bf16[1024,576]{1,0:T(8,128)(2,1)}, u32[]{:S(2)}) copy-start(bf16[1024,576]{1,0:T(8,128)(2,1)} %get-tuple-element.76.a_ref) | copy-start | bytes 3538948
  392.0 31.9 %copy-start.1 = (f32[1024,192]{1,0:T(8,128)S(1)}, f32[1024,192]{1,0:T(8,128)}, u32[]{:S(2)}) copy-start(f32[1024,192]{1,0:T(8,128)} %get-tuple-element.113) | copy-start | bytes 2359300
  393.2 32.0 %copy-start.3 = (f32[2,1,768]{2,1,0:T(1,128)S(1)}, f32[2,1,768]{2,1,0:T(1,128)}, u32[]{:S(2)}) copy-start(f32[2,1,768]{2,1,0:T(1,128)} %get-tuple-element.94) | copy-start | bytes 18436
  393.2 32.6 %copy-start.2 = (f32[2,1,768]{2,1,0:T(1,128)S(1)}, f32[2,1,768]{2,1,0:T(1,128)}, u32[]{:S(2)}) copy-start(f32[2,1,768]{2,1,0:T(1,128)} %get-tuple-element.92) | copy-start | bytes 18436

commit v8 on v7

--- a/solution.py
+++ b/solution.py
@@ -67,6 +67,15 @@
     place = row % group
     level, side = place // 2, place % 2
     return row, place, level, side, row + 1 - 2 * side
+
+
+def paired(row, mask):
+    other, bit = row, 1
+    while bit <= mask:
+        if mask & bit:
+            other = other + bit * (1 - 2 * ((row // bit) % 2))
+        bit *= 2
+    return other
 
 
 def far_first(rows):
@@ -146,8 +155,8 @@
 def start_kernel(
     rows,
     pieces,
-    x_ref,
-    g_ref,
+    x_hbm,
+    g_hbm,
     ids_ref,
     table_ref,
     w_ref,
@@ -157,6 +166,9 @@
     wo_ref,
     so_ref,
     t_ref,
+    x_ref,
+    g_ref,
+    f_sems,
     xp_ref,
     gp_ref,
     c_send,
@@ -171,7 +183,15 @@
     levels = rows // 2
     order = far_first(rows)
     peers = [{"row": (row + k) % rows} for k in order]
+    fetch = [
+        pltpu.make_async_copy(x_hbm, x_ref, f_sems.at[0]),
+        pltpu.make_async_copy(g_hbm, g_ref, f_sems.at[1]),
+    ]
+    fetch[0].start()
+    fetch[1].start()
     greet(peers + [{"col": sib}, {"col": across}])
+    fetch[0].wait()
+    fetch[1].wait()
     xp_ref[...] = side_by_side(x_ref[...])
     step = xp_ref.shape[0] // pieces
     cap = gp_ref.shape[1]
@@ -314,9 +334,12 @@
             jax.ShapeDtypeStruct((rows,) + s.shape, s.dtype),
             jax.ShapeDtypeStruct((1, tokens), jnp.int32),
         ),
-        in_specs=[VSPEC] * 6,
+        in_specs=[pl.BlockSpec(memory_space=pl.ANY)] * 2 + [VSPEC] * 4,
         out_specs=(VSPEC,) * 5,
         scratch_shapes=[
+            pltpu.VMEM(x.shape, x.dtype),
+            pltpu.VMEM(g.shape, g.dtype),
+            DMA((2,)),
             pltpu.VMEM(packed, x.dtype),
             pltpu.VMEM((rows - 1, cap, 2 * width), g.dtype),
             DMA((3, pieces)),
@@ -1081,7 +1104,7 @@
     st_recv,
 ):
     greet(col_peers())
-    tokens, width = x_ref.shape
+    width = x_ref.shape[2] // 2
     product(
         pieces,
         a_ref,
@@ -1095,7 +1118,9 @@
         (send, recv),
         lambda: None,
     )
-    mid = x_ref[...].astype(F32) + mid_ref[...] + own_features(s_ref, 4)
+    own = x_ref[lax.axis_index("col")]
+    own = jnp.concatenate([own[:, :width], own[:, width:]], axis=0)
+    mid = own.astype(F32) + mid_ref[...] + own_features(s_ref, 4)
     mid_ref[...] = mid
     part_mean = jnp.mean(mid, axis=-1, keepdims=True)
     part_spread = jnp.sum((mid - part_mean) ** 2, axis=-1, keepdims=True)
@@ -1238,8 +1263,7 @@
 def dispatch_kernel(rows, x_ref, t_ref, out_ref, in_ref, r_send, r_recv, c_send, c_recv):
     me, sib, across, _ = col_places()
     row = lax.axis_index("row")
-    order = far_first(rows)
-    peers = [(row + k) % rows for k in order]
+    peers = [paired(row, k) for k in range(1, rows)]
     greet([{"row": p} for p in peers] + [{"col": sib}, {"col": across}])
     copies = []
     cap = in_ref.shape[1]
@@ -1250,21 +1274,23 @@
         )
 
     done, first = [], []
-    for k, peer in enumerate(peers):
+    for n, k in enumerate(range(rows - 1, 0, -1)):
+        peer = peers[k - 1]
         in_ref[peer] = placed(t_ref, x_ref[...], peer, cap)
         copy = push(
-            in_ref.at[peer], out_ref.at[me, row], r_send.at[k], r_recv.at[k], {"row": peer}
+            in_ref.at[peer], out_ref.at[me, row], r_send.at[k - 1], r_recv.at[k - 1], {"row": peer}
         )
         copy.start()
         copies.append(copy)
-        if k == 1:
+        if n == 1:
             in_ref[row] = placed(t_ref, x_ref[...], row, cap)
             for way in range(2):
                 copy = col(in_ref.at[row], out_ref.at[me, row], 0, way)
                 copy.start()
                 (first if way == 0 else done).append(copy)
+    copies.reverse()
     out_ref[me, row] = in_ref[row]
-    sources = [row] + [(row + rows - k) % rows for k in order]
+    sources = [row] + peers
 
     def forward(k):
         first[k].wait_recv()
@@ -1715,7 +1741,7 @@
     kv_all, attended, attended_low, lse, g_all = attention_forward(
         info, queries, keys_values, g_own, group, low, 1
     )
-    mid, normed_two, rstd_two, h_two = branch(attended_low, w_all, layer_in, s_all, 2)
+    mid, normed_two, rstd_two, h_two = branch(attended_low, w_all, x_all, s_all, 2)
 
     received = dispatch(h_two, target, rows, capacity, 4)
     parts, grad_parts, grad_w_up, grad_bias_up, grad_w_down, grad_bias_down = experts(

time: 434 us -> 434 us (level)
  no operation moved by 1% of the time
where the time goes in v8:
time: 434 us; the launch traced here: 426 us
  Pallas kernels  399 us (92%)
  local copies, waits for them, and re-layouts  19.1 us (4%)
  other arithmetic  6.31 us (1%)
    pallas_call x1, Pallas kernels, attention_backward(): pl.pallas_call(functools.partial(backward_kernel, group, low, pieces, tok...  83.4 us
    pallas_call x1, Pallas kernels, dispatch(): pl.pallas_call(functools.partial(dispatch_kernel, rows), out_shape=jax.Sh...  73.1 us
    pallas_call x1, Pallas kernels, attention_forward(): pl.pallas_call(functools.partial(forward_kernel, group, low, pieces, toke...  49.7 us
    pallas_call x1, Pallas kernels, giveback(): pl.pallas_call(functools.partial(giveback_kernel, rows), out_shape=(jax.S...  36 us
    pallas_call x1, Pallas kernels, start_gather(): pl.pallas_call(functools.partial(start_kernel, rows, pieces), out_shape=(...  33.6 us
    pallas_call x1, Pallas kernels, experts(): pl.pallas_call(expert_kernel, out_shape=(jax.ShapeDtypeStruct(x.shape, BF...  27.5 us
    pallas_call x1, Pallas kernels, input_gradient(): pl.pallas_call(functools.partial(input_kernel, pieces), out_shape=(jax.Sh...  27.1 us
    pallas_call x1, Pallas kernels, end_scatter(): pl.pallas_call(functools.partial(end_kernel, rows), out_shape=(jax.ShapeD...  23.5 us

profile of v8, /device:TPU:10, one launch (start us, length us, event | category | flops | bytes accessed | tf_op | source)
XLA Modules:
  0.0 426.1 jit_solution(14284762818495845390)
XLA Ops:
  1.3 0.8 convert_element_type.42
  2.1 0.8 convert_element_type.44
  2.9 0.7 bitcast_convert_fusion.2
  3.5 0.7 bitcast_convert_fusion.4
  4.2 0.7 bitcast_convert_fusion.6
  4.9 0.6 stack.59.s_ref
  5.5 2.0 copy.43.g_hbm.cot_ref
  7.5 2.0 copy.42.x_hbm
  9.5 0.9 convert.30
  10.4 0.7 pad_bitcast_fusion.table_ref
  11.1 1.6 pad_maximum_fusion.w_ref
  12.7 33.6 %shard_map.323 = (bf16[4,512,384]{2,1,0:T(8,128)(2,1)}, bf16[8,128,384]{2,1,0:T(8,128)(2,1)}, bf16[8,96,768]{2,1,0:T(8,128)(2,1)}, f32[8,8,128]{2,1,0:T(8,128)}, s32[1,1024]{1,0:T(1,128)}) custom-call(bf16[1024,192]{1,0:T(8,128)(2,1)} %copy.42.x_hbm, bf16[1024,192]{1,0:T(8,128)(2,1)} %copy.43.g_hbm.cot_ref, s32[1,1024]{1,0:T(1,128)} %bitcast.65, ...), custom_call_target="tpu_custom_call" | custom-call | tf_op jit(solution)/shard_map/pallas_call | solution.py:328
  46.3 6.7 %shard_map.324 = (bf16[1024,192]{1,0:T(8,128)(2,1)}, bf16[1024,384]{1,0:T(8,128)(2,1)}, bf16[1024,768]{1,0:T(8,128)(2,1)}, f32[1024,192]{1,0:T(8,128)}, f32[1024,1]{1,0:T(8,128)}) custom-call(bf16[4,512,384]{2,1,0:T(8,128)(2,1)} %get-tuple-element.56.x_ref, bf16[8,96,768]{2,1,0:T(8,128)(2,1)} %get-tuple-element.57.w_ref, f32[8,8,128]{2,1,0:T(8,128)} %get-tuple-element.58.s_ref), custom_call_target="tpu_custom_call" | custom-call | tf_op jit(solution)/shard_map/pallas_call | solution.py:386
  53.1 49.7 %shard_map.325 = (bf16[8,1024,384]{2,1,0:T(8,128)(2,1)}, f32[1024,192]{1,0:T(8,128)}, bf16[1024,192]{1,0:T(8,128)(2,1)}, f32[8,1024]{1,0:T(8,128)}, bf16[4,8,128,384]{3,2,1,0:T(8,128)(2,1)}) custom-call(s32[1]{0:T(128)S(6)} %select_n.13.info_ref, bf16[1024,192]{1,0:T(8,128)(2,1)} %get-tuple-element.59.q_ref, bf16[1024,384]{1,0:T(8,128)(2,1)} %get-tuple-element.60.kv_ref, ...), custom_call_target="tpu_custom_call" | custom-call | tf_op jit(solution)/shard_map/pallas_call | solution.py:766
  102.7 21.7 %shard_map.326 = (f32[1024,192]{1,0:T(8,128)}, f32[1024,192]{1,0:T(8,128)}, f32[1024,1]{1,0:T(8,128)}, bf16[1024,192]{1,0:T(8,128)(2,1)}) custom-call(bf16[1024,192]{1,0:T(8,128)(2,1)} %get-tuple-element.63.a_ref.low_ref, bf16[8,96,768]{2,1,0:T(8,128)(2,1)} %get-tuple-element.57.w_ref, bf16[4,512,384]{2,1,0:T(8,128)(2,1)} %get-tuple-element.56.x_ref, ...), custom_call_target="tpu_custom_call" | custom-call | tf_op jit(solution)/shard_map/pallas_call | solution.py:1144
  124.5 0.0 copy-start.4
  124.5 73.1 %shard_map.327.x_ref = bf16[4,8,128,384]{3,2,1,0:T(8,128)(2,1)} custom-call(bf16[1024,192]{1,0:T(8,128)(2,1)} %get-tuple-element.64.x_ref, s32[1,1024]{1,0:T(1,128)} %get-tuple-element.65.t_ref), custom_call_target="tpu_custom_call" | custom-call | tf_op jit(solution)/shard_map/pallas_call | solution.py:1321
  197.7 0.0 copy-done.4
  197.7 0.6 copy.44.bias_ref
  198.3 27.5 %shard_map.328 = (bf16[4,8,128,384]{3,2,1,0:T(8,128)(2,1)}, bf16[4,8,128,384]{3,2,1,0:T(8,128)(2,1)}, f32[2,768,768]{2,1,0:T(8,128)}, f32[2,1,768]{2,1,0:T(1,128...) custom-call(bf16[4,8,128,384]{3,2,1,0:T(8,128)(2,1)} %shard_map.327.x_ref, ...), custom_call_target="tpu_custom_call" | custom-call | tf_op jit(solution)/shard_map/pallas_call | solution.py:1651
  225.8 36.0 %shard_map.329 = (f32[1024,192]{1,0:T(8,128)}, f32[8,192]{1,0:T(8,128)}) custom-call(bf16[4,8,128,384]{3,2,1,0:T(8,128)(2,1)} %get-tuple-element.67.in_ref, s32[1,1024]{1,0:T(1,128)} %get-tuple-element.65.t_ref, bf16[1024,192]{1,0:T(8,128)(2,1)} %copy.43.g_hbm.cot_ref, f32[1024,192]{1,0:T(8,128)} %get-tuple-element.68.normed_ref, ...), custom_call_target="tpu_custom_call" | custom-call | tf_op jit(solution)/shard_map/pallas_call | solution.py:1429
  261.8 16.5 %shard_map.330 = (bf16[1024,192]{1,0:T(8,128)(2,1)}, f32[8,1024]{1,0:T(8,128)}, bf16[768,192]{1,0:T(8,128)(2,1)}) custom-call(f32[1024,192]{1,0:T(8,128)} %get-tuple-element.70.x_ref.mid_ref, bf16[8,96,768]{2,1,0:T(8,128)(2,1)} %get-tuple-element.57.w_ref, f32[1024,192]{1,0:T(8,128)} %get-tuple-element.71.att_ref, ...), custom_call_target="tpu_custom_call" | custom-call | tf_op jit(solution)/shard_map/pallas_call | solution.py:473
  278.3 0.8 dynamic-slice_convert_fusion
  279.0 0.6 reshape.118.bias_ref
  279.7 83.4 %shard_map.331 = (bf16[1024,576]{1,0:T(8,128)(2,1)}, bf16[8,128,384]{2,1,0:T(8,128)(2,1)}) custom-call(s32[1]{0:T(128)S(6)} %select_n.13.info_ref, bf16[1024,192]{1,0:T(8,128)(2,1)} %get-tuple-element.59.q_ref, bf16[8,1024,384]{2,1,0:T(8,128)(2,1)} %get-tuple-element.62.kv_ref, bf16[1024,192]{1,0:T(8,128)(2,1)} %get-tuple-element.72.do_ref, ...), custom_call_target="tpu_custom_call" | custom-call | tf_op jit(solution)/shard_map/pallas_call | solution.py:998
  363.0 0.0 copy-start
  363.1 27.1 %shard_map.332 = (f32[1024,192]{1,0:T(8,128)}, bf16[8,128,384]{2,1,0:T(8,128)(2,1)}, bf16[768,768]{1,0:T(8,128)(2,1)}, f32[4,8,1280]{2,1,0:T(8,128)}) custom-call(bf16[1024,576]{1,0:T(8,128)(2,1)} %get-tuple-element.76.a_ref, bf16[8,96,768]{2,1,0:T(8,128)(2,1)} %get-tuple-element.57.w_ref, bf16[8,128,384]{2,1,0:T(8,128)(2,1)} %get-tuple-element.77.e_ref, ...), custom_call_target="tpu_custom_call" | custom-call | tf_op jit(solution)/shard_map/pallas_call | solution.py:1240
  390.2 0.8 slice_bitcast_fusion
  391.0 0.1 reshape.103
  391.1 0.0 copy-done
  391.1 0.3 convert_reduce_fusion
  391.3 0.0 copy-start.1
  391.3 0.1 reshape.104
  391.4 0.1 reshape.105
  391.5 0.1 reshape.106
  391.6 0.1 reshape.107
  391.7 0.1 pad.60.clone
  391.8 0.7 fusion.s_ref
  392.5 0.0 copy-start.3
  392.5 0.0 copy-start.2
  392.5 23.5 %shard_map.333 = (f32[96,768]{1,0:T(8,128)}, f32[8,128]{1,0:T(8,128)}, bf16[1024,192]{1,0:T(8,128)(2,1)}) custom-call(bf16[8,96,768]{2,1,0:T(8,128)(2,1)} %bitcast.57, f32[8,8,128]{2,1,0:T(8,128)} %fusion.s_ref, bf16[8,128,384]{2,1,0:T(8,128)(2,1)} %get-tuple-element.85.e_ref, s32[1,1024]{1,0:T(1,128)} %get-tuple-element.65.t_ref, ...), custom_call_target="tpu_custom_call" | custom-call | tf_op jit(solution)/shard_map/pallas_call | solution.py:1533
  416.0 1.9 fusion.3
  417.8 2.0 copy.52
  419.8 0.8 slice_reduce_fusion
  420.6 0.7 reshape.108
  421.2 0.7 reshape.109
  421.9 1.4 slice_bitcast_fusion.1
  423.3 0.0 copy-done.1
  423.3 1.2 copy.53
  424.5 0.0 copy-done.3
  424.5 0.6 copy.60
  425.1 0.0 copy-done.2
  425.1 0.6 copy.61
  (7 shorter events, 0.1 us)
Async XLA Ops:
  124.5 73.2 %copy-start.4 = (bf16[2,768]{1,0:T(2,128)(2,1)S(1)}, bf16[2,768]{1,0:T(2,128)(2,1)}, u32[]{:S(2)}) copy-start(bf16[2,768]{1,0:T(2,128)(2,1)} %param.37) | copy-start | bytes 9220
  363.0 28.0 %copy-start = (bf16[1024,576]{1,0:T(8,128)(2,1)S(1)}, bf16[1024,576]{1,0:T(8,128)(2,1)}, u32[]{:S(2)}) copy-start(bf16[1024,576]{1,0:T(8,128)(2,1)} %get-tuple-element.76.a_ref) | copy-start | bytes 3538948
  391.3 32.0 %copy-start.1 = (f32[1024,192]{1,0:T(8,128)S(1)}, f32[1024,192]{1,0:T(8,128)}, u32[]{:S(2)}) copy-start(f32[1024,192]{1,0:T(8,128)} %get-tuple-element.113) | copy-start | bytes 2359300
  392.5 32.0 %copy-start.3 = (f32[2,1,768]{2,1,0:T(1,128)S(1)}, f32[2,1,768]{2,1,0:T(1,128)}, u32[]{:S(2)}) copy-start(f32[2,1,768]{2,1,0:T(1,128)} %get-tuple-element.94) | copy-start | bytes 18436
  392.5 32.6 %copy-start.2 = (f32[2,1,768]{2,1,0:T(1,128)S(1)}, f32[2,1,768]{2,1,0:T(1,128)}, u32[]{:S(2)}) copy-start(f32[2,1,768]{2,1,0:T(1,128)} %get-tuple-element.92) | copy-start | bytes 18436

commit v9 on v7

--- a/solution.py
+++ b/solution.py
@@ -568,6 +568,8 @@
     x_recv,
     g_send,
     g_recv,
+    e_send,
+    e_recv,
 ):
     levels = group // 2
     row, place, level, side, partner = line_places(group)
@@ -595,6 +597,16 @@
         dst = out_ref.at[2 * at + 1 - side, part]
         return push(dst, dst, x_send.at[at, i], x_recv.at[at, i], {"row": partner})
 
+    detour = pieces // 2
+    top = level == levels - 1
+    by_line = top & (side == 1)
+    not_across = top & (side == 0)
+    lends = (level == levels - 2) & (side == 1)
+
+    def lent(i):
+        dst = out_ref.at[0, pl.ds(i * step, step)]
+        return push(dst, dst, e_send.at[i], e_recv.at[i], {"row": row + 2})
+
     def when(cond, run):
         @pl.when(cond)
         def _():
@@ -683,7 +695,14 @@
                 def _(i=i):
                     make(via, i, 0).start()
 
-                make(via, i, 2).start()
+                if i < detour:
+
+                    @pl.when(jnp.logical_not((via == 0) & not_across))
+                    def _(i=i):
+                        make(via, i, 2).start()
+
+                else:
+                    make(via, i, 2).start()
 
         @pl.when(relays & (via > level))
         def _():
@@ -697,7 +716,26 @@
                 make(via, i, 2).start()
 
         comes = live & (cross == 1) & ((at < low) | (at < level) | (side == 1))
-        when(comes, lambda i: other(at, i).wait_recv())
+
+        @pl.when(comes)
+        def _():
+            for i in range(pieces):
+                if i >= detour:
+                    other(at, i).wait_recv()
+                    continue
+
+                @pl.when((at == 0) & by_line)
+                def _(i=i):
+                    lent(i).wait_recv()
+
+                @pl.when(jnp.logical_not((at == 0) & by_line))
+                def _(i=i):
+                    other(at, i).wait_recv()
+
+                @pl.when((at == 0) & lends)
+                def _(i=i):
+                    lent(i).start()
+
         blk = 2 * at + jnp.where(cross == 0, side, 1 - side)
         needed = line_in | comes
 
@@ -726,11 +764,25 @@
     for k in range(1, levels):
         at = level - k
         when((at >= 0) & to_up, lambda i, at=at: make(at, i, 0).wait_send())
-        when(at >= 0, lambda i, at=at: make(at, i, 2).wait_send())
+        for i in range(pieces):
+            sent = at >= 0
+            if i < detour:
+                sent = sent & jnp.logical_not((at == 0) & not_across)
+
+            @pl.when(sent)
+            def _(at=at, i=i):
+                make(at, i, 2).wait_send()
+
     for k in range(1, low):
         at = level + k
         when((at < low) & (level > 0), lambda i, at=at: make(at, i, 1).wait_send())
         when(at < low, lambda i, at=at: make(at, i, 2).wait_send())
+    for i in range(detour):
+
+        @pl.when(lends)
+        def _(i=i):
+            lent(i).wait_send()
+
     for copy in wide:
         copy.wait()
 
@@ -756,7 +808,8 @@
             pltpu.VMEM((heads, HD + 16, tokens), F32),
         ]
         + [DMA((levels, pieces))] * 6
-        + [DMA((COLS - 1,))] * 2,
+        + [DMA((COLS - 1,))] * 2
+        + [DMA((pieces // 2,))] * 2,
         compiler_params=params(collective),
     )(info, q, kv, g)
 

time: 434 us -> 427 us (0.984)
  Pallas kernels: 400 us -> 392 us
    pallas_call x1, Pallas kernels: 70.9 us -> 64.2 us  [dispatch(): pl.pallas_call(functools.partial(dispatch_kernel, rows), out_shape=jax.Sh...]
where the time goes in v9:
time: 427 us; the launch traced here: 419 us
  Pallas kernels  392 us (92%)
  local copies, waits for them, and re-layouts  19.1 us (4%)
  other arithmetic  6.31 us (1%)
    pallas_call x1, Pallas kernels, attention_backward(): pl.pallas_call(functools.partial(backward_kernel, group, low, pieces, tok...  84 us
    pallas_call x1, Pallas kernels, dispatch(): pl.pallas_call(functools.partial(dispatch_kernel, rows), out_shape=jax.Sh...  64.2 us
    pallas_call x1, Pallas kernels, attention_forward(): pl.pallas_call(functools.partial(forward_kernel, group, low, pieces, toke...  49.9 us
    pallas_call x1, Pallas kernels, giveback(): pl.pallas_call(functools.partial(giveback_kernel, rows), out_shape=(jax.S...  38.2 us
    pallas_call x1, Pallas kernels, start_gather(): pl.pallas_call(functools.partial(start_kernel, rows, pieces), out_shape=(...  33.9 us
    pallas_call x1, Pallas kernels, experts(): pl.pallas_call(expert_kernel, out_shape=(jax.ShapeDtypeStruct(x.shape, BF...  27.5 us
    pallas_call x1, Pallas kernels, input_gradient(): pl.pallas_call(functools.partial(input_kernel, pieces), out_shape=(jax.Sh...  26.4 us
    pallas_call x1, Pallas kernels, end_scatter(): pl.pallas_call(functools.partial(end_kernel, rows), out_shape=(jax.ShapeD...  23.5 us

profile of v9, /device:TPU:10, one launch (start us, length us, event | category | flops | bytes accessed | tf_op | source)
XLA Modules:
  0.0 419.3 jit_solution(14712750906288969602)
XLA Ops:
  1.3 0.8 convert_element_type.42
  2.1 0.8 convert_element_type.44
  2.9 0.7 bitcast_convert_fusion.2
  3.5 0.7 bitcast_convert_fusion.4
  4.2 0.7 bitcast_convert_fusion.6
  4.9 0.6 stack.59.s_ref
  5.5 2.0 copy.43.x_ref
  7.5 2.0 copy.44.g_ref.cot_ref
  9.5 0.9 convert.30
  10.4 0.7 pad_bitcast_fusion.table_ref
  11.1 1.6 pad_maximum_fusion.w_ref
  12.7 33.9 %shard_map.323 = (bf16[4,512,384]{2,1,0:T(8,128)(2,1)}, bf16[8,128,384]{2,1,0:T(8,128)(2,1)}, bf16[8,96,768]{2,1,0:T(8,128)(2,1)}, f32[8,8,128]{2,1,0:T(8,128)}, s32[1,1024]{1,0:T(1,128)}) custom-call(bf16[1024,192]{1,0:T(8,128)(2,1)} %copy.43.x_ref, bf16[1024,192]{1,0:T(8,128)(2,1)} %copy.44.g_ref.cot_ref, s32[1,1024]{1,0:T(1,128)} %bitcast.65, ...), custom_call_target="tpu_custom_call" | custom-call | tf_op jit(solution)/shard_map/pallas_call | solution.py:308
  46.6 6.7 %shard_map.324 = (bf16[1024,192]{1,0:T(8,128)(2,1)}, bf16[1024,384]{1,0:T(8,128)(2,1)}, bf16[1024,768]{1,0:T(8,128)(2,1)}, f32[1024,192]{1,0:T(8,128)}, f32[1024,1]{1,0:T(8,128)}) custom-call(bf16[4,512,384]{2,1,0:T(8,128)(2,1)} %get-tuple-element.56.x_ref, bf16[8,96,768]{2,1,0:T(8,128)(2,1)} %get-tuple-element.57.w_ref, f32[8,8,128]{2,1,0:T(8,128)} %get-tuple-element.58.s_ref), custom_call_target="tpu_custom_call" | custom-call | tf_op jit(solution)/shard_map/pallas_call | solution.py:363
  53.3 49.9 %shard_map.325 = (bf16[8,1024,384]{2,1,0:T(8,128)(2,1)}, f32[1024,192]{1,0:T(8,128)}, bf16[1024,192]{1,0:T(8,128)(2,1)}, f32[8,1024]{1,0:T(8,128)}, bf16[4,8,128,384]{3,2,1,0:T(8,128)(2,1)}) custom-call(s32[1]{0:T(128)S(6)} %select_n.13.info_ref, bf16[1024,192]{1,0:T(8,128)(2,1)} %get-tuple-element.59.q_ref, bf16[1024,384]{1,0:T(8,128)(2,1)} %get-tuple-element.60.kv_ref, ...), custom_call_target="tpu_custom_call" | custom-call | tf_op jit(solution)/shard_map/pallas_call | solution.py:795
  103.2 0.0 copy-start.4
  103.3 21.2 %shard_map.326 = (f32[1024,192]{1,0:T(8,128)}, f32[1024,192]{1,0:T(8,128)}, f32[1024,1]{1,0:T(8,128)}, bf16[1024,192]{1,0:T(8,128)(2,1)}) custom-call(bf16[1024,192]{1,0:T(8,128)(2,1)} %get-tuple-element.63.a_ref.low_ref, bf16[8,96,768]{2,1,0:T(8,128)(2,1)} %get-tuple-element.57.w_ref, bf16[1024,192]{1,0:T(8,128)(2,1)} %copy.43.x_ref, ...), custom_call_target="tpu_custom_call" | custom-call | tf_op jit(solution)/shard_map/pallas_call | solution.py:1172
  124.5 64.2 %shard_map.327.x_ref = bf16[4,8,128,384]{3,2,1,0:T(8,128)(2,1)} custom-call(bf16[1024,192]{1,0:T(8,128)(2,1)} %get-tuple-element.64.x_ref, s32[1,1024]{1,0:T(1,128)} %get-tuple-element.65.t_ref), custom_call_target="tpu_custom_call" | custom-call | tf_op jit(solution)/shard_map/pallas_call | solution.py:1348
  188.7 0.0 copy-done.4
  188.7 0.6 copy.46.bias_ref
  189.3 27.5 %shard_map.328 = (bf16[4,8,128,384]{3,2,1,0:T(8,128)(2,1)}, bf16[4,8,128,384]{3,2,1,0:T(8,128)(2,1)}, f32[2,768,768]{2,1,0:T(8,128)}, f32[2,1,768]{2,1,0:T(1,128...) custom-call(bf16[4,8,128,384]{3,2,1,0:T(8,128)(2,1)} %shard_map.327.x_ref, ...), custom_call_target="tpu_custom_call" | custom-call | tf_op jit(solution)/shard_map/pallas_call | solution.py:1678
  216.8 38.2 %shard_map.329 = (f32[1024,192]{1,0:T(8,128)}, f32[8,192]{1,0:T(8,128)}) custom-call(bf16[4,8,128,384]{3,2,1,0:T(8,128)(2,1)} %get-tuple-element.67.in_ref, s32[1,1024]{1,0:T(1,128)} %get-tuple-element.65.t_ref, bf16[1024,192]{1,0:T(8,128)(2,1)} %copy.44.g_ref.cot_ref, f32[1024,192]{1,0:T(8,128)} %get-tuple-element.68.normed_ref, ...), custom_call_target="tpu_custom_call" | custom-call | tf_op jit(solution)/shard_map/pallas_call | solution.py:1456
  255.0 16.5 %shard_map.330 = (bf16[1024,192]{1,0:T(8,128)(2,1)}, f32[8,1024]{1,0:T(8,128)}, bf16[768,192]{1,0:T(8,128)(2,1)}) custom-call(f32[1024,192]{1,0:T(8,128)} %get-tuple-element.70.x_ref.mid_ref, bf16[8,96,768]{2,1,0:T(8,128)(2,1)} %get-tuple-element.57.w_ref, f32[1024,192]{1,0:T(8,128)} %get-tuple-element.71.att_ref, ...), custom_call_target="tpu_custom_call" | custom-call | tf_op jit(solution)/shard_map/pallas_call | solution.py:450
  271.5 0.8 dynamic-slice_convert_fusion
  272.3 0.6 reshape.118.bias_ref
  272.9 84.0 %shard_map.331 = (bf16[1024,576]{1,0:T(8,128)(2,1)}, bf16[8,128,384]{2,1,0:T(8,128)(2,1)}) custom-call(s32[1]{0:T(128)S(6)} %select_n.13.info_ref, bf16[1024,192]{1,0:T(8,128)(2,1)} %get-tuple-element.59.q_ref, bf16[8,1024,384]{2,1,0:T(8,128)(2,1)} %get-tuple-element.62.kv_ref, bf16[1024,192]{1,0:T(8,128)(2,1)} %get-tuple-element.72.do_ref, ...), custom_call_target="tpu_custom_call" | custom-call | tf_op jit(solution)/shard_map/pallas_call | solution.py:1028
  356.9 0.0 copy-start
  356.9 26.4 %shard_map.332 = (f32[1024,192]{1,0:T(8,128)}, bf16[8,128,384]{2,1,0:T(8,128)(2,1)}, bf16[768,768]{1,0:T(8,128)(2,1)}, f32[4,8,1280]{2,1,0:T(8,128)}) custom-call(bf16[1024,576]{1,0:T(8,128)(2,1)} %get-tuple-element.76.a_ref, bf16[8,96,768]{2,1,0:T(8,128)(2,1)} %get-tuple-element.57.w_ref, bf16[8,128,384]{2,1,0:T(8,128)(2,1)} %get-tuple-element.77.e_ref, ...), custom_call_target="tpu_custom_call" | custom-call | tf_op jit(solution)/shard_map/pallas_call | solution.py:1268
  383.4 0.8 slice_bitcast_fusion
  384.1 0.1 reshape.103
  384.2 0.0 copy-done
  384.2 0.3 convert_reduce_fusion
  384.5 0.0 copy-start.1
  384.5 0.1 reshape.104
  384.6 0.1 reshape.105
  384.7 0.1 reshape.106
  384.8 0.1 reshape.107
  384.9 0.1 pad.60.clone
  384.9 0.7 fusion.s_ref
  385.6 0.0 copy-start.3
  385.6 0.0 copy-start.2
  385.6 23.5 %shard_map.333 = (f32[96,768]{1,0:T(8,128)}, f32[8,128]{1,0:T(8,128)}, bf16[1024,192]{1,0:T(8,128)(2,1)}) custom-call(bf16[8,96,768]{2,1,0:T(8,128)(2,1)} %bitcast.57, f32[8,8,128]{2,1,0:T(8,128)} %fusion.s_ref, bf16[8,128,384]{2,1,0:T(8,128)(2,1)} %get-tuple-element.85.e_ref, s32[1,1024]{1,0:T(1,128)} %get-tuple-element.65.t_ref, ...), custom_call_target="tpu_custom_call" | custom-call | tf_op jit(solution)/shard_map/pallas_call | solution.py:1560
  409.1 1.9 fusion.3
  411.0 2.0 copy.54
  413.0 0.8 slice_reduce_fusion
  413.7 0.7 reshape.108
  414.4 0.7 reshape.109
  415.1 1.4 slice_bitcast_fusion.1
  416.4 0.0 copy-done.1
  416.4 1.2 copy.55
  417.6 0.0 copy-done.3
  417.6 0.6 copy.62
  418.2 0.0 copy-done.2
  418.2 0.6 copy.63
  (7 shorter events, 0.1 us)
Async XLA Ops:
  103.2 85.5 %copy-start.4 = (bf16[2,768]{1,0:T(2,128)(2,1)S(1)}, bf16[2,768]{1,0:T(2,128)(2,1)}, u32[]{:S(2)}) copy-start(bf16[2,768]{1,0:T(2,128)(2,1)} %param.37) | copy-start | bytes 9220
  356.9 27.3 %copy-start = (bf16[1024,576]{1,0:T(8,128)(2,1)S(1)}, bf16[1024,576]{1,0:T(8,128)(2,1)}, u32[]{:S(2)}) copy-start(bf16[1024,576]{1,0:T(8,128)(2,1)} %get-tuple-element.76.a_ref) | copy-start | bytes 3538948
  384.5 31.9 %copy-start.1 = (f32[1024,192]{1,0:T(8,128)S(1)}, f32[1024,192]{1,0:T(8,128)}, u32[]{:S(2)}) copy-start(f32[1024,192]{1,0:T(8,128)} %get-tuple-element.113) | copy-start | bytes 2359300
  385.6 32.0 %copy-start.3 = (f32[2,1,768]{2,1,0:T(1,128)S(1)}, f32[2,1,768]{2,1,0:T(1,128)}, u32[]{:S(2)}) copy-start(f32[2,1,768]{2,1,0:T(1,128)} %get-tuple-element.94) | copy-start | bytes 18436
  385.6 32.6 %copy-start.2 = (f32[2,1,768]{2,1,0:T(1,128)S(1)}, f32[2,1,768]{2,1,0:T(1,128)}, u32[]{:S(2)}) copy-start(f32[2,1,768]{2,1,0:T(1,128)} %get-tuple-element.92) | copy-start | bytes 18436

commit v10 on v9

--- a/solution.py
+++ b/solution.py
@@ -1026,7 +1026,7 @@
     both = 2 * width
     block = pltpu.VMEM((levels, tokens, both), BF16)
     return pl.pallas_call(
-        functools.partial(backward_kernel, group, low, pieces, tokens // 2),
+        functools.partial(backward_kernel, group, low, pieces, tokens // 4),
         out_shape=(
             jax.ShapeDtypeStruct((tokens, width + both), BF16),
             jax.ShapeDtypeStruct(e.shape[1:], BF16),

time: 427 us -> 430 us (level)
  no operation moved by 1% of the time
where the time goes in v10:
time: 430 us; the launch traced here: 422 us
  Pallas kernels  394 us (92%)
  local copies, waits for them, and re-layouts  19.1 us (4%)
  other arithmetic  6.31 us (1%)
    pallas_call x1, Pallas kernels, attention_backward(): pl.pallas_call(functools.partial(backward_kernel, group, low, pieces, tok...  86.8 us
    pallas_call x1, Pallas kernels, dispatch(): pl.pallas_call(functools.partial(dispatch_kernel, rows), out_shape=jax.Sh...  64.2 us
    pallas_call x1, Pallas kernels, attention_forward(): pl.pallas_call(functools.partial(forward_kernel, group, low, pieces, toke...  49.7 us
    pallas_call x1, Pallas kernels, giveback(): pl.pallas_call(functools.partial(giveback_kernel, rows), out_shape=(jax.S...  38.2 us
    pallas_call x1, Pallas kernels, start_gather(): pl.pallas_call(functools.partial(start_kernel, rows, pieces), out_shape=(...  33.9 us
    pallas_call x1, Pallas kernels, experts(): pl.pallas_call(expert_kernel, out_shape=(jax.ShapeDtypeStruct(x.shape, BF...  27.5 us
    pallas_call x1, Pallas kernels, input_gradient(): pl.pallas_call(functools.partial(input_kernel, pieces), out_shape=(jax.Sh...  26.4 us
    pallas_call x1, Pallas kernels, end_scatter(): pl.pallas_call(functools.partial(end_kernel, rows), out_shape=(jax.ShapeD...  23.5 us

profile of v10, /device:TPU:10, one launch (start us, length us, event | category | flops | bytes accessed | tf_op | source)
XLA Modules:
  0.0 421.5 jit_solution(5677000438802298558)
XLA Ops:
  1.3 0.8 convert_element_type.42
  2.1 0.8 convert_element_type.44
  2.9 0.7 bitcast_convert_fusion.2
  3.5 0.7 bitcast_convert_fusion.4
  4.2 0.7 bitcast_convert_fusion.6
  4.9 0.6 stack.59.s_ref
  5.5 2.0 copy.43.x_ref
  7.5 2.0 copy.44.g_ref.cot_ref
  9.5 0.9 convert.30
  10.4 0.7 pad_bitcast_fusion.table_ref
  11.1 1.6 pad_maximum_fusion.w_ref
  12.7 33.9 %shard_map.323 = (bf16[4,512,384]{2,1,0:T(8,128)(2,1)}, bf16[8,128,384]{2,1,0:T(8,128)(2,1)}, bf16[8,96,768]{2,1,0:T(8,128)(2,1)}, f32[8,8,128]{2,1,0:T(8,128)}, s32[1,1024]{1,0:T(1,128)}) custom-call(bf16[1024,192]{1,0:T(8,128)(2,1)} %copy.43.x_ref, bf16[1024,192]{1,0:T(8,128)(2,1)} %copy.44.g_ref.cot_ref, s32[1,1024]{1,0:T(1,128)} %bitcast.65, ...), custom_call_target="tpu_custom_call" | custom-call | tf_op jit(solution)/shard_map/pallas_call | solution.py:308
  46.6 6.7 %shard_map.324 = (bf16[1024,192]{1,0:T(8,128)(2,1)}, bf16[1024,384]{1,0:T(8,128)(2,1)}, bf16[1024,768]{1,0:T(8,128)(2,1)}, f32[1024,192]{1,0:T(8,128)}, f32[1024,1]{1,0:T(8,128)}) custom-call(bf16[4,512,384]{2,1,0:T(8,128)(2,1)} %get-tuple-element.56.x_ref, bf16[8,96,768]{2,1,0:T(8,128)(2,1)} %get-tuple-element.57.w_ref, f32[8,8,128]{2,1,0:T(8,128)} %get-tuple-element.58.s_ref), custom_call_target="tpu_custom_call" | custom-call | tf_op jit(solution)/shard_map/pallas_call | solution.py:363
  53.3 49.7 %shard_map.325 = (bf16[8,1024,384]{2,1,0:T(8,128)(2,1)}, f32[1024,192]{1,0:T(8,128)}, bf16[1024,192]{1,0:T(8,128)(2,1)}, f32[8,1024]{1,0:T(8,128)}, bf16[4,8,128,384]{3,2,1,0:T(8,128)(2,1)}) custom-call(s32[1]{0:T(128)S(6)} %select_n.13.info_ref, bf16[1024,192]{1,0:T(8,128)(2,1)} %get-tuple-element.59.q_ref, bf16[1024,384]{1,0:T(8,128)(2,1)} %get-tuple-element.60.kv_ref, ...), custom_call_target="tpu_custom_call" | custom-call | tf_op jit(solution)/shard_map/pallas_call | solution.py:795
  103.0 0.0 copy-start.4
  103.0 21.2 %shard_map.326 = (f32[1024,192]{1,0:T(8,128)}, f32[1024,192]{1,0:T(8,128)}, f32[1024,1]{1,0:T(8,128)}, bf16[1024,192]{1,0:T(8,128)(2,1)}) custom-call(bf16[1024,192]{1,0:T(8,128)(2,1)} %get-tuple-element.63.a_ref.low_ref, bf16[8,96,768]{2,1,0:T(8,128)(2,1)} %get-tuple-element.57.w_ref, bf16[1024,192]{1,0:T(8,128)(2,1)} %copy.43.x_ref, ...), custom_call_target="tpu_custom_call" | custom-call | tf_op jit(solution)/shard_map/pallas_call | solution.py:1172
  124.2 64.2 %shard_map.327.x_ref = bf16[4,8,128,384]{3,2,1,0:T(8,128)(2,1)} custom-call(bf16[1024,192]{1,0:T(8,128)(2,1)} %get-tuple-element.64.x_ref, s32[1,1024]{1,0:T(1,128)} %get-tuple-element.65.t_ref), custom_call_target="tpu_custom_call" | custom-call | tf_op jit(solution)/shard_map/pallas_call | solution.py:1348
  188.5 0.0 copy-done.4
  188.5 0.6 copy.46.bias_ref
  189.1 27.5 %shard_map.328 = (bf16[4,8,128,384]{3,2,1,0:T(8,128)(2,1)}, bf16[4,8,128,384]{3,2,1,0:T(8,128)(2,1)}, f32[2,768,768]{2,1,0:T(8,128)}, f32[2,1,768]{2,1,0:T(1,128...) custom-call(bf16[4,8,128,384]{3,2,1,0:T(8,128)(2,1)} %shard_map.327.x_ref, ...), custom_call_target="tpu_custom_call" | custom-call | tf_op jit(solution)/shard_map/pallas_call | solution.py:1678
  216.6 38.2 %shard_map.329 = (f32[1024,192]{1,0:T(8,128)}, f32[8,192]{1,0:T(8,128)}) custom-call(bf16[4,8,128,384]{3,2,1,0:T(8,128)(2,1)} %get-tuple-element.67.in_ref, s32[1,1024]{1,0:T(1,128)} %get-tuple-element.65.t_ref, bf16[1024,192]{1,0:T(8,128)(2,1)} %copy.44.g_ref.cot_ref, f32[1024,192]{1,0:T(8,128)} %get-tuple-element.68.normed_ref, ...), custom_call_target="tpu_custom_call" | custom-call | tf_op jit(solution)/shard_map/pallas_call | solution.py:1456
  254.8 16.5 %shard_map.330 = (bf16[1024,192]{1,0:T(8,128)(2,1)}, f32[8,1024]{1,0:T(8,128)}, bf16[768,192]{1,0:T(8,128)(2,1)}) custom-call(f32[1024,192]{1,0:T(8,128)} %get-tuple-element.70.x_ref.mid_ref, bf16[8,96,768]{2,1,0:T(8,128)(2,1)} %get-tuple-element.57.w_ref, f32[1024,192]{1,0:T(8,128)} %get-tuple-element.71.att_ref, ...), custom_call_target="tpu_custom_call" | custom-call | tf_op jit(solution)/shard_map/pallas_call | solution.py:450
  271.3 0.8 dynamic-slice_convert_fusion
  272.1 0.6 reshape.118.bias_ref
  272.7 86.8 %shard_map.331 = (bf16[1024,576]{1,0:T(8,128)(2,1)}, bf16[8,128,384]{2,1,0:T(8,128)(2,1)}) custom-call(s32[1]{0:T(128)S(6)} %select_n.13.info_ref, bf16[1024,192]{1,0:T(8,128)(2,1)} %get-tuple-element.59.q_ref, bf16[8,1024,384]{2,1,0:T(8,128)(2,1)} %get-tuple-element.62.kv_ref, bf16[1024,192]{1,0:T(8,128)(2,1)} %get-tuple-element.72.do_ref, ...), custom_call_target="tpu_custom_call" | custom-call | tf_op jit(solution)/shard_map/pallas_call | solution.py:1028
  359.5 0.0 copy-start
  359.5 26.4 %shard_map.332 = (f32[1024,192]{1,0:T(8,128)}, bf16[8,128,384]{2,1,0:T(8,128)(2,1)}, bf16[768,768]{1,0:T(8,128)(2,1)}, f32[4,8,1280]{2,1,0:T(8,128)}) custom-call(bf16[1024,576]{1,0:T(8,128)(2,1)} %get-tuple-element.76.a_ref, bf16[8,96,768]{2,1,0:T(8,128)(2,1)} %get-tuple-element.57.w_ref, bf16[8,128,384]{2,1,0:T(8,128)(2,1)} %get-tuple-element.77.e_ref, ...), custom_call_target="tpu_custom_call" | custom-call | tf_op jit(solution)/shard_map/pallas_call | solution.py:1268
  385.9 0.8 slice_bitcast_fusion
  386.7 0.1 reshape.103
  386.8 0.0 copy-done
  386.8 0.3 convert_reduce_fusion
  387.0 0.0 copy-start.1
  387.0 0.1 reshape.104
  387.1 0.1 reshape.105
  387.2 0.1 reshape.106
  387.3 0.1 reshape.107
  387.4 0.1 pad.60.clone
  387.5 0.7 fusion.s_ref
  388.2 0.0 copy-start.3
  388.2 0.0 copy-start.2
  388.2 23.5 %shard_map.333 = (f32[96,768]{1,0:T(8,128)}, f32[8,128]{1,0:T(8,128)}, bf16[1024,192]{1,0:T(8,128)(2,1)}) custom-call(bf16[8,96,768]{2,1,0:T(8,128)(2,1)} %bitcast.57, f32[8,8,128]{2,1,0:T(8,128)} %fusion.s_ref, bf16[8,128,384]{2,1,0:T(8,128)(2,1)} %get-tuple-element.85.e_ref, s32[1,1024]{1,0:T(1,128)} %get-tuple-element.65.t_ref, ...), custom_call_target="tpu_custom_call" | custom-call | tf_op jit(solution)/shard_map/pallas_call | solution.py:1560
  411.6 1.9 fusion.3
  413.5 2.0 copy.54
  415.5 0.8 slice_reduce_fusion
  416.2 0.7 reshape.108
  416.9 0.7 reshape.109
  417.6 1.4 slice_bitcast_fusion.1
  418.9 0.0 copy-done.1
  418.9 1.2 copy.55
  420.1 0.0 copy-done.3
  420.1 0.6 copy.62
  420.7 0.0 copy-done.2
  420.7 0.6 copy.63
  (7 shorter events, 0.1 us)
Async XLA Ops:
  103.0 85.5 %copy-start.4 = (bf16[2,768]{1,0:T(2,128)(2,1)S(1)}, bf16[2,768]{1,0:T(2,128)(2,1)}, u32[]{:S(2)}) copy-start(bf16[2,768]{1,0:T(2,128)(2,1)} %param.37) | copy-start | bytes 9220
  359.5 27.2 %copy-start = (bf16[1024,576]{1,0:T(8,128)(2,1)S(1)}, bf16[1024,576]{1,0:T(8,128)(2,1)}, u32[]{:S(2)}) copy-start(bf16[1024,576]{1,0:T(8,128)(2,1)} %get-tuple-element.76.a_ref) | copy-start | bytes 3538948
  387.0 31.9 %copy-start.1 = (f32[1024,192]{1,0:T(8,128)S(1)}, f32[1024,192]{1,0:T(8,128)}, u32[]{:S(2)}) copy-start(f32[1024,192]{1,0:T(8,128)} %get-tuple-element.113) | copy-start | bytes 2359300
  388.2 32.0 %copy-start.3 = (f32[2,1,768]{2,1,0:T(1,128)S(1)}, f32[2,1,768]{2,1,0:T(1,128)}, u32[]{:S(2)}) copy-start(f32[2,1,768]{2,1,0:T(1,128)} %get-tuple-element.94) | copy-start | bytes 18436
  388.2 32.6 %copy-start.2 = (f32[2,1,768]{2,1,0:T(1,128)S(1)}, f32[2,1,768]{2,1,0:T(1,128)}, u32[]{:S(2)}) copy-start(f32[2,1,768]{2,1,0:T(1,128)} %get-tuple-element.92) | copy-start | bytes 18436
